TPU v7x, 128 devices: a whole 4x4x4 slice. The times are simulated.
128 devices in a mesh: gx: 16 (over z, x), gy: 8 (over y, core).
Axes of the slice: x: 4, y: 4, z: 4, core: 2. Of those that a mesh axis runs over, the one named last changes fastest.
Arguments:
- length_scale: float32 [128, 512, 128], P('gx', 'gy'), may hold values from 0.35 to 1
- innovation: float32 [262144], P(('gx', 'gy')), may hold values from -6 to 6
- observed_precision: float32 [262144], P(('gx', 'gy')), may hold values from 0.25 to 4
- profile_weight: float32 [262144, 128], P(('gx', 'gy')), may hold values from -0.5 to 0.5
- stencil_weight: float32 [4, 262144], P(None, ('gx', 'gy')), may hold values from 0.05 to 0.45
- send_rows: int32 [128, 128, 16], P(('gx', 'gy')), may hold values from 0 to 511, as said below
- stencil_rows: int32 [4, 262144], P(None, ('gx', 'gy')), may hold values from 0 to 2047, as said below
- obs_count: int32 [128], P(('gx', 'gy')), may hold values from 256 to 2048
Outputs:
- control: float32 [128, 512, 128], P('gx', 'gy')
- increment: float32 [128, 512, 128], P('gx', 'gy')
Inputs may be any that keep to these rules, and one draw needn't show every extreme that they name: `send_rows`: every entry is a column of the source's tile. Slots of a pair beyond the pair's used count hold 0 and are named by no stencil entry; each pair uses between 4 and 16 slots, one source uses all slots toward every owner, and one owner receives full slots from every source. `stencil_rows`: each entry names a used slot of the pair from its source to the observation's owner, also for slots that are not live.
All inputs are finite; a program needn't handle non-finite values.
Results may differ from a plain program's by a relative error of at most 0.007.
Values sent between devices are 32-bit elements; how exact they have to be, the bound alone decides.
No kernel may reach another device: no remote copies, remote signals or barrier semaphores. Data moves between devices by JAX's collectives and lax.ppermute only.
A program may use at most 64 MiB of HBM per device.

v0:
```python
import math

import jax
import jax.numpy as jnp
from jax import lax
from jax.sharding import PartitionSpec as P

PASSES = 4
ITERS = 2


coupling = 0.12
highest = lax.Precision.HIGHEST


def with_halo(cells, sides, width):
    for axis, dim in sides:
        count = lax.axis_size(axis)
        ends = count - 1
        head = lax.slice_in_dim(cells, 0, width, axis=dim)
        tail = lax.slice_in_dim(cells, cells.shape[dim] - width, cells.shape[dim], axis=dim)
        cells = jnp.concatenate(
            [
                lax.ppermute(tail, axis, [(i, (i + 1) % count) for i in range(ends)]),
                cells,
                lax.ppermute(head, axis, [((i + 1) % count, i) for i in range(ends)]),
            ],
            axis=dim,
        )
    return cells


def diffuse_once(padded, scales):
    centre = padded[1:-1, 1:-1]
    middle = scales[1:-1, 1:-1]
    fluxes = middle * scales[2:, 1:-1] * (centre - padded[2:, 1:-1])
    fluxes = fluxes + middle * scales[:-2, 1:-1] * (centre - padded[:-2, 1:-1])
    fluxes = fluxes + middle * scales[1:-1, 2:] * (centre - padded[1:-1, 2:])
    fluxes = fluxes + middle * scales[1:-1, :-2] * (centre - padded[1:-1, :-2])
    return centre - coupling * fluxes


def stencil_matrix(rows_block, weights_block, slot_total):
    slot_ids = lax.iota(jnp.int32, slot_total)[None, :]
    matrix = weights_block[0][:, None] * (rows_block[0][:, None] == slot_ids).astype(jnp.float32)
    for corner in range(1, 4):
        matrix = matrix + weights_block[corner][:, None] * (
            rows_block[corner][:, None] == slot_ids
        ).astype(jnp.float32)
    return matrix


def on_device(
    length_scale,
    innovation,
    observed_precision,
    profile_weight,
    stencil_weight,
    send_rows,
    stencil_rows,
    obs_count,
):
    tile_rows, tile_cols, levels = length_scale.shape
    owners = send_rows.shape[1]
    slot_count = send_rows.shape[2]
    slot_total = owners * slot_count
    obs_here = innovation.shape[0]
    block_size = math.gcd(obs_here, 512)
    block_count = obs_here // block_size
    send_flat = send_rows.reshape(-1)
    live = (lax.iota(jnp.int32, obs_here) < obs_count[0]).astype(jnp.float32)
    precision = live * observed_precision
    rows_blocks = stencil_rows.reshape(4, block_count, block_size).transpose(1, 0, 2)
    weight_blocks = stencil_weight.reshape(4, block_count, block_size).transpose(1, 0, 2)
    profile_blocks = profile_weight.reshape(block_count, block_size, levels)
    placement = (lax.iota(jnp.int32, tile_rows * tile_cols)[:, None] == send_flat[None, :]).astype(
        jnp.float32
    )
    scales_rim = with_halo(length_scale, (("gx", 0), ("gy", 1)), 1)

    def smooth(field):
        for sweep_index in range(PASSES):
            padded = with_halo(field, (("gx", 0), ("gy", 1)), 1)
            field = diffuse_once(padded, scales_rim)
        return field

    def adjoint(forcing):
        forcing_blocks = forcing.reshape(block_count, block_size)

        def add_block(total, items):
            rows_block, weights_block, profile_block, forcing_block = items
            matrix = stencil_matrix(rows_block, weights_block, slot_total)
            spread_rows = profile_block * forcing_block[:, None]
            term = lax.dot_general(
                matrix,
                spread_rows,
                (((0,), (0,)), ((), ())),
                precision=highest,
                preferred_element_type=jnp.float32,
            )
            return (total + term, None)

        start = jnp.zeros((slot_total, levels), jnp.float32)
        returned_rows, unused = lax.scan(
            add_block, start, (rows_blocks, weight_blocks, profile_blocks, forcing_blocks)
        )
        arrived = lax.all_to_all(
            returned_rows.reshape(owners, slot_count, levels),
            ("gx", "gy"),
            split_axis=0,
            concat_axis=0,
            tiled=True,
        )
        column_sums = jnp.dot(
            placement,
            arrived.reshape(slot_total, levels),
            precision=highest,
            preferred_element_type=jnp.float32,
        )
        return column_sums.reshape(tile_rows, tile_cols, levels)

    right = smooth(adjoint(precision * innovation))
    control = jnp.zeros_like(right)
    increment = jnp.zeros_like(right)
    residual = right
    direction = right
    norm_now = lax.psum(jnp.sum(residual * residual), ("gx", "gy"))
    for iteration in range(ITERS):
        smoothed = smooth(direction)
        flat = smoothed.reshape(tile_rows * tile_cols, levels)
        outgoing = jnp.take(flat, send_flat, axis=0)
        observe_arrived = lax.all_to_all(
            outgoing.reshape(owners, slot_count, levels),
            ("gx", "gy"),
            split_axis=0,
            concat_axis=0,
            tiled=True,
        )
        received = observe_arrived.reshape(slot_total, levels)

        def one_block(items):
            rows_block, weights_block, profile_block = items
            matrix = stencil_matrix(rows_block, weights_block, slot_total)
            gathered = jnp.dot(
                matrix, received, precision=highest, preferred_element_type=jnp.float32
            )
            return jnp.sum(profile_block * gathered, axis=1)

        image = direction + smooth(
            adjoint(
                precision
                * lax.map(one_block, (rows_blocks, weight_blocks, profile_blocks)).reshape(obs_here)
            )
        )
        curvature = lax.psum(jnp.sum(direction * image), ("gx", "gy"))
        step_length = norm_now / curvature
        control = control + step_length * direction
        increment = increment + step_length * smoothed
        residual = residual - step_length * image
        if iteration + 1 < ITERS:
            norm_next = lax.psum(jnp.sum(residual * residual), ("gx", "gy"))
            direction = residual + norm_next / norm_now * direction
            norm_now = norm_next
    return (control, increment)


def solution(mesh):
    return jax.shard_map(
        on_device,
        mesh=mesh,
        in_specs=(
            P("gx", "gy", None),
            P(("gx", "gy")),
            P(("gx", "gy")),
            P(("gx", "gy"), None),
            P(None, ("gx", "gy")),
            P(("gx", "gy"), None, None),
            P(None, ("gx", "gy")),
            P(("gx", "gy")),
        ),
        out_specs=(P("gx", "gy", None), P("gx", "gy", None)),
        check_vma=False,
    )
```

profile of v0, /device:TPU:1, one launch (start us, length us, event | category | flops | bytes accessed | tf_op | source)
XLA Modules:
  0.0 882.8 jit_solution(3930859504831085956)
XLA Ops:
  2.0 49.6 %while.55 = (s32[]{:T(128)}, f32[2048,128]{1,0:T(8,128)}, s32[4,4,512]{2,1,0:T(4,128)}, f32[4,4,512]{2,1,0:T(4,128)}, f32[4,512,128]{2,1,0:T(8,128)}, /*index=5*...) while((s32[]{:T(128)}, f32[2048,128]{1,0:T(8,128)}, ...), condition=%wide.region_1.2_spmd.clone, body=%wide.region_0.1_spmd.clone.sunk | while | flops 1622736896 | bytes 2415295 | solution.py:104
  3.8 10.4 %fusion.445 = f32[2048,128]{1,0:T(8,128)} fusion(f32[512]{0:T(512)S(1)} %bitcast.228, s32[512]{0:T(512)S(1)} %bitcast.240, f32[512]{0:T(512)S(1)} %bitcast.226, s32[512]{0:T(512)S(1)} %bitcast.238, f32[512]{0:T(512)S(1)} %bitcast.227, s32[512]{0:T(512)S(1)} %bitcast.239, f32[512]{0:T(512)S(1)} %bitcast.225, s32[512]{0:T(512)S(1)} %bitcast.237, ...), kind=kOutput, calls=%fused_computation.78.clone.1 | convolution fusion | flops 1622736896 | bytes 2378241 | tf_op jit(solution)/shard_map/while/body/eval_jaxpr/dot_general | solution.py:94
  15.9 10.7 %fusion.445 = f32[2048,128]{1,0:T(8,128)} fusion(f32[512]{0:T(512)S(1)} %bitcast.228, s32[512]{0:T(512)S(1)} %bitcast.240, f32[512]{0:T(512)S(1)} %bitcast.226, s32[512]{0:T(512)S(1)} %bitcast.238, f32[512]{0:T(512)S(1)} %bitcast.227, s32[512]{0:T(512)S(1)} %bitcast.239, f32[512]{0:T(512)S(1)} %bitcast.225, s32[512]{0:T(512)S(1)} %bitcast.237, ...), kind=kOutput, calls=%fused_computation.78.clone.1 | convolution fusion | flops 1622736896 | bytes 2378241 | tf_op jit(solution)/shard_map/while/body/eval_jaxpr/dot_general | solution.py:94
  28.4 10.7 %fusion.445 = f32[2048,128]{1,0:T(8,128)} fusion(f32[512]{0:T(512)S(1)} %bitcast.228, s32[512]{0:T(512)S(1)} %bitcast.240, f32[512]{0:T(512)S(1)} %bitcast.226, s32[512]{0:T(512)S(1)} %bitcast.238, f32[512]{0:T(512)S(1)} %bitcast.227, s32[512]{0:T(512)S(1)} %bitcast.239, f32[512]{0:T(512)S(1)} %bitcast.225, s32[512]{0:T(512)S(1)} %bitcast.237, ...), kind=kOutput, calls=%fused_computation.78.clone.1 | convolution fusion | flops 1622736896 | bytes 2378241 | tf_op jit(solution)/shard_map/while/body/eval_jaxpr/dot_general | solution.py:94
  40.9 10.7 %fusion.445 = f32[2048,128]{1,0:T(8,128)} fusion(f32[512]{0:T(512)S(1)} %bitcast.228, s32[512]{0:T(512)S(1)} %bitcast.240, f32[512]{0:T(512)S(1)} %bitcast.226, s32[512]{0:T(512)S(1)} %bitcast.238, f32[512]{0:T(512)S(1)} %bitcast.227, s32[512]{0:T(512)S(1)} %bitcast.239, f32[512]{0:T(512)S(1)} %bitcast.225, s32[512]{0:T(512)S(1)} %bitcast.237, ...), kind=kOutput, calls=%fused_computation.78.clone.1 | convolution fusion | flops 1622736896 | bytes 2378241 | tf_op jit(solution)/shard_map/while/body/eval_jaxpr/dot_general | solution.py:94
  51.6 11.5 %all-to-all-start = ((f32[128,16,128]{2,1,0:T(8,128)}), f32[128,16,128]{2,1,0:T(8,128)S(1)}, u32[]{:S(2)}, u32[]{:S(2)}) async-start(f32[128,16,128]{2,1,0:T(8,128)} %bitcast.26), calls=%async_computation | async-start | bytes 2097152 | tf_op jit(solution)/shard_map/all_to_all | solution.py:107
  67.9 5.8 collective-permute-done.2
  76.6 5.5 all-to-all-done
  125.6 5.0 collective-permute-start.15
  140.4 5.0 collective-permute-start.19
  162.5 6.6 collective-permute-start.25
  172.0 5.0 collective-permute-start.27
  179.3 6.7 collective-permute-start.29
  188.9 5.0 collective-permute-start.31
  196.2 6.7 collective-permute-start.33
  205.8 5.0 collective-permute-start.35
  211.8 5.5 gather_fusion
  218.6 18.3 %all-to-all-start.1 = ((f32[128,16,128]{2,1,0:T(8,128)}), f32[128,16,128]{2,1,0:T(8,128)}, u32[]{:S(2)}, u32[]{:S(2)}) async-start(f32[128,16,128]{2,1,0:T(8,128)} %bitcast.34), calls=%async_computation.1 | async-start | bytes 2097152 | tf_op jit(solution)/shard_map/all_to_all | solution.py:132
  238.3 17.2 %all-to-all-done.1 = f32[128,16,128]{2,1,0:T(8,128)} async-done(((f32[128,16,128]{2,1,0:T(8,128)}), f32[128,16,128]{2,1,0:T(8,128)}, u32[]{:S(2)}, u32[]{:S(2)}) %all-to-all-start.1) | async-done | bytes 1048608 | tf_op jit(solution)/shard_map/all_to_all | solution.py:132
  255.5 31.6 %while.53 = (s32[]{:T(128)}, f32[4,512]{1,0:T(4,128)S(1)}, f32[4,512,128]{1,2,0:T(8,128)}, s32[4,4,512]{2,1,0:T(4,128)S(1)}, f32[4,4,512]{2,1,0:T(4,128)S(1)}, /...) while((s32[]{:T(128)}, f32[4,512]{1,0:T(4,128)S(1)}, ...), condition=%wide.region_6.8_spmd, body=%wide.region_4.7_spmd.sunk | while | flops 1622277632 | bytes 1366201 | solution.py:152
  255.6 7.8 fusion.440
  263.4 7.8 fusion.440
  271.3 7.8 fusion.440
  279.2 7.8 fusion.440
  287.1 41.9 %while.56 = (s32[]{:T(128)}, f32[2048,128]{1,0:T(8,128)}, s32[4,4,512]{2,1,0:T(4,128)S(1)}, f32[4,4,512]{2,1,0:T(4,128)S(1)}, f32[4,512,128]{2,1,0:T(8,128)S(1)}...) while((s32[]{:T(128)}, f32[2048,128]{1,0:T(8,128)}, ...), condition=%wide.region_8.10_spmd.clone, body=%wide.region_7.9_spmd.clone.sunk | while | flops 1622736896 | bytes 2414787 | solution.py:104
  287.6 9.4 %fusion.447 = f32[2048,128]{1,0:T(8,128)} fusion(f32[512]{0:T(512)S(1)} %bitcast.232, s32[512]{0:T(512)S(1)} %bitcast.244, f32[512]{0:T(512)S(1)} %bitcast.230, s32[512]{0:T(512)S(1)} %bitcast.242, f32[512]{0:T(512)S(1)} %bitcast.231, s32[512]{0:T(512)S(1)} %bitcast.243, f32[512]{0:T(512)S(1)} %bitcast.229, s32[512]{0:T(512)S(1)} %bitcast.241, ...), kind=kOutput, calls=%fused_computation.114.clone.1 | convolution fusion | flops 1622736896 | bytes 2377733 | tf_op jit(solution)/shard_map/while/body/eval_jaxpr/dot_general | solution.py:94
  297.1 10.6 %fusion.447 = f32[2048,128]{1,0:T(8,128)} fusion(f32[512]{0:T(512)S(1)} %bitcast.232, s32[512]{0:T(512)S(1)} %bitcast.244, f32[512]{0:T(512)S(1)} %bitcast.230, s32[512]{0:T(512)S(1)} %bitcast.242, f32[512]{0:T(512)S(1)} %bitcast.231, s32[512]{0:T(512)S(1)} %bitcast.243, f32[512]{0:T(512)S(1)} %bitcast.229, s32[512]{0:T(512)S(1)} %bitcast.241, ...), kind=kOutput, calls=%fused_computation.114.clone.1 | convolution fusion | flops 1622736896 | bytes 2377733 | tf_op jit(solution)/shard_map/while/body/eval_jaxpr/dot_general | solution.py:94
  307.8 10.6 %fusion.447 = f32[2048,128]{1,0:T(8,128)} fusion(f32[512]{0:T(512)S(1)} %bitcast.232, s32[512]{0:T(512)S(1)} %bitcast.244, f32[512]{0:T(512)S(1)} %bitcast.230, s32[512]{0:T(512)S(1)} %bitcast.242, f32[512]{0:T(512)S(1)} %bitcast.231, s32[512]{0:T(512)S(1)} %bitcast.243, f32[512]{0:T(512)S(1)} %bitcast.229, s32[512]{0:T(512)S(1)} %bitcast.241, ...), kind=kOutput, calls=%fused_computation.114.clone.1 | convolution fusion | flops 1622736896 | bytes 2377733 | tf_op jit(solution)/shard_map/while/body/eval_jaxpr/dot_general | solution.py:94
  318.4 10.6 %fusion.447 = f32[2048,128]{1,0:T(8,128)} fusion(f32[512]{0:T(512)S(1)} %bitcast.232, s32[512]{0:T(512)S(1)} %bitcast.244, f32[512]{0:T(512)S(1)} %bitcast.230, s32[512]{0:T(512)S(1)} %bitcast.242, f32[512]{0:T(512)S(1)} %bitcast.231, s32[512]{0:T(512)S(1)} %bitcast.243, f32[512]{0:T(512)S(1)} %bitcast.229, s32[512]{0:T(512)S(1)} %bitcast.241, ...), kind=kOutput, calls=%fused_computation.114.clone.1 | convolution fusion | flops 1622736896 | bytes 2377733 | tf_op jit(solution)/shard_map/while/body/eval_jaxpr/dot_general | solution.py:94
  329.1 23.9 %all_to_all.25 = f32[128,16,128]{2,1,0:T(8,128)S(1)} all-to-all(f32[128,16,128]{2,1,0:T(8,128)} %bitcast.221), channel_id=1, replica_groups=mesh['gx'=16,'gy'=8] {'gx','gy'}, dimensions={0} | all-to-all | bytes 2097152 | tf_op jit(solution)/shard_map/all_to_all | solution.py:107
  392.2 5.0 collective-permute-start.47
  413.7 72.7 %all-reduce = (f32[]{:T(128)}, f32[]{:T(128)}) all-reduce(f32[]{:T(128)} %get-tuple-element.256, f32[]{:T(128)} %get-tuple-element.255), channel_id=1, replica_groups=mesh['gx'=16,'gy'=8] {'gx','gy'}, use_global_device_ids=true, to_apply=%region_3.4 | all-reduce | flops 2 | bytes 16 | tf_op jit(solution)/shard_map/psum | solution.py:127
  488.3 63.0 %psum.30 = f32[]{:T(128)} all-reduce(f32[]{:T(128)} %multiply_reduce_fusion), channel_id=1, replica_groups=mesh['gx'=16,'gy'=8] {'gx','gy'}, use_global_device_ids=true, to_apply=%region_12.14 | all-reduce | flops 1 | bytes 8 | tf_op jit(solution)/shard_map/psum | solution.py:161
  610.5 5.5 gather_fusion.1
  617.3 16.6 %all-to-all-start.3 = ((f32[128,16,128]{2,1,0:T(8,128)}), f32[128,16,128]{2,1,0:T(8,128)}, u32[]{:S(2)}, u32[]{:S(2)}) async-start(f32[128,16,128]{2,1,0:T(8,128)} %bitcast.42), calls=%async_computation.3 | async-start | bytes 2097152 | tf_op jit(solution)/shard_map/all_to_all | solution.py:132
  634.0 18.5 %all-to-all-done.3 = f32[128,16,128]{2,1,0:T(8,128)} async-done(((f32[128,16,128]{2,1,0:T(8,128)}), f32[128,16,128]{2,1,0:T(8,128)}, u32[]{:S(2)}, u32[]{:S(2)}) %all-to-all-start.3) | async-done | bytes 1048608 | tf_op jit(solution)/shard_map/all_to_all | solution.py:132
  652.5 31.5 %while.54 = (s32[]{:T(128)}, f32[4,512]{1,0:T(4,128)S(1)}, f32[4,512,128]{1,2,0:T(8,128)}, s32[4,4,512]{2,1,0:T(4,128)S(1)}, f32[4,4,512]{2,1,0:T(4,128)S(1)}, /...) while((s32[]{:T(128)}, f32[4,512]{1,0:T(4,128)S(1)}, ...), condition=%wide.region_15.17_spmd, body=%wide.region_13.16_spmd.sunk | while | flops 1622277632 | bytes 1366201 | solution.py:152
  652.6 7.8 fusion.443
  660.4 7.8 fusion.443
  668.3 7.8 fusion.443
  676.2 7.8 fusion.443
  684.1 39.4 %while.57 = (s32[]{:T(128)}, f32[2048,128]{1,0:T(8,128)S(1)}, s32[4,4,512]{2,1,0:T(4,128)S(1)}, f32[4,4,512]{2,1,0:T(4,128)S(1)}, f32[4,512,128]{2,1,0:T(8,128)}...) while((s32[]{:T(128)}, f32[2048,128]{1,0:T(8,128)S(1)}, ...), condition=%wide.region_17.19_spmd.clone, body=%wide.region_16.18_spmd.clone.sunk | while | flops 1622736896 | bytes 2415295 | solution.py:104
  684.4 9.7 %fusion.449 = f32[2048,128]{1,0:T(8,128)S(1)} fusion(f32[512]{0:T(512)S(1)} %bitcast.236, s32[512]{0:T(512)S(1)} %bitcast.248, f32[512]{0:T(512)S(1)} %bitcast.234, s32[512]{0:T(512)S(1)} %bitcast.246, f32[512]{0:T(512)S(1)} %bitcast.235, s32[512]{0:T(512)S(1)} %bitcast.247, f32[512]{0:T(512)S(1)} %bitcast.233, s32[512]{0:T(512)S(1)} %bitcast.245, ...), kind=kOutput, calls=%fused_computation.150.clone.1 | convolution fusion | flops 1622736896 | bytes 2378241 | tf_op jit(solution)/shard_map/while/body/eval_jaxpr/dot_general | solution.py:94
  694.2 9.7 %fusion.449 = f32[2048,128]{1,0:T(8,128)S(1)} fusion(f32[512]{0:T(512)S(1)} %bitcast.236, s32[512]{0:T(512)S(1)} %bitcast.248, f32[512]{0:T(512)S(1)} %bitcast.234, s32[512]{0:T(512)S(1)} %bitcast.246, f32[512]{0:T(512)S(1)} %bitcast.235, s32[512]{0:T(512)S(1)} %bitcast.247, f32[512]{0:T(512)S(1)} %bitcast.233, s32[512]{0:T(512)S(1)} %bitcast.245, ...), kind=kOutput, calls=%fused_computation.150.clone.1 | convolution fusion | flops 1622736896 | bytes 2378241 | tf_op jit(solution)/shard_map/while/body/eval_jaxpr/dot_general | solution.py:94
  704.0 9.7 %fusion.449 = f32[2048,128]{1,0:T(8,128)S(1)} fusion(f32[512]{0:T(512)S(1)} %bitcast.236, s32[512]{0:T(512)S(1)} %bitcast.248, f32[512]{0:T(512)S(1)} %bitcast.234, s32[512]{0:T(512)S(1)} %bitcast.246, f32[512]{0:T(512)S(1)} %bitcast.235, s32[512]{0:T(512)S(1)} %bitcast.247, f32[512]{0:T(512)S(1)} %bitcast.233, s32[512]{0:T(512)S(1)} %bitcast.245, ...), kind=kOutput, calls=%fused_computation.150.clone.1 | convolution fusion | flops 1622736896 | bytes 2378241 | tf_op jit(solution)/shard_map/while/body/eval_jaxpr/dot_general | solution.py:94
  713.8 9.7 %fusion.449 = f32[2048,128]{1,0:T(8,128)S(1)} fusion(f32[512]{0:T(512)S(1)} %bitcast.236, s32[512]{0:T(512)S(1)} %bitcast.248, f32[512]{0:T(512)S(1)} %bitcast.234, s32[512]{0:T(512)S(1)} %bitcast.246, f32[512]{0:T(512)S(1)} %bitcast.235, s32[512]{0:T(512)S(1)} %bitcast.247, f32[512]{0:T(512)S(1)} %bitcast.233, s32[512]{0:T(512)S(1)} %bitcast.245, ...), kind=kOutput, calls=%fused_computation.150.clone.1 | convolution fusion | flops 1622736896 | bytes 2378241 | tf_op jit(solution)/shard_map/while/body/eval_jaxpr/dot_general | solution.py:94
  723.5 23.3 %all_to_all.26 = f32[128,16,128]{2,1,0:T(8,128)S(1)} all-to-all(f32[128,16,128]{2,1,0:T(8,128)S(1)} %bitcast.220), channel_id=1, replica_groups=mesh['gx'=16,'gy'=8] {'gx','gy'}, dimensions={0} | all-to-all | bytes 2097152 | tf_op jit(solution)/shard_map/all_to_all | solution.py:107
  807.4 72.7 %psum.31 = f32[]{:T(128)} all-reduce(f32[]{:T(128)} %fusion.126), channel_id=1, replica_groups=mesh['gx'=16,'gy'=8] {'gx','gy'}, use_global_device_ids=true, to_apply=%region_19.21 | all-reduce | flops 1 | bytes 8 | tf_op jit(solution)/shard_map/psum | solution.py:155
  (321 shorter events, 279.4 us)
Async XLA Ops:
  51.6 30.4 %all-to-all-start = ((f32[128,16,128]{2,1,0:T(8,128)}), f32[128,16,128]{2,1,0:T(8,128)S(1)}, u32[]{:S(2)}, u32[]{:S(2)}) async-start(f32[128,16,128]{2,1,0:T(8,128)} %bitcast.26), calls=%async_computation | async-start | bytes 2097152 | tf_op jit(solution)/shard_map/all_to_all | solution.py:107
  63.1 10.6 %collective-permute-start.2 = (f32[1,64,128]{2,1,0:T(8,128)S(1)}, f32[1,64,128]{2,1,0:T(8,128)S(1)}, u32[]{:S(2)}, u32[]{:S(2)}) collective-permute-start(f32[1,64,128]{2,1,0:T(8,128)S(1)} %get-tuple-element.445), channel_id=1, source_target_pairs={{0,8},{8,16},{16,24},{24,32},{32,40},{40,48},{48,56},{56,64},{64,7... | collective-permute-start | bytes 98312 | tf_op jit(solution)/shard_map/ppermute | solution.py:24
  66.4 10.1 %collective-permute-start = (f32[1,64,128]{2,1,0:T(8,128)S(1)}, f32[1,64,128]{2,1,0:T(8,128)S(1)}, u32[]{:S(2)}, u32[]{:S(2)}) collective-permute-start(f32[1,64,128]{2,1,0:T(8,128)S(1)} %get-tuple-element.446), channel_id=1, source_target_pairs={{8,0},{16,8},{24,16},{32,24},{40,32},{48,40},{56,48},{64,56},{72,6... | collective-permute-start | bytes 98312 | tf_op jit(solution)/shard_map/ppermute | solution.py:26
  84.1 11.5 %collective-permute-start.1 = (f32[1,64,128]{2,1,0:T(8,128)S(1)}, f32[1,64,128]{2,1,0:T(8,128)S(1)}, u32[]{:S(2)}, u32[]{:S(2)}) collective-permute-start(f32[1,64,128]{2,1,0:T(8,128)S(1)} %get-tuple-element.448), channel_id=1, source_target_pairs={{8,0},{16,8},{24,16},{32,24},{40,32},{48,40},{56,48},{64,56},{72,6... | collective-permute-start | bytes 98312 | tf_op jit(solution)/shard_map/ppermute | solution.py:26
  85.4 10.2 %collective-permute-start.3 = (f32[1,64,128]{2,1,0:T(8,128)S(1)}, f32[1,64,128]{2,1,0:T(8,128)S(1)}, u32[]{:S(2)}, u32[]{:S(2)}) collective-permute-start(f32[1,64,128]{2,1,0:T(8,128)S(1)} %get-tuple-element.447), channel_id=1, source_target_pairs={{0,8},{8,16},{16,24},{24,32},{32,40},{40,48},{48,56},{56,64},{64,7... | collective-permute-start | bytes 98312 | tf_op jit(solution)/shard_map/ppermute | solution.py:24
  89.7 11.6 %collective-permute-start.4 = (f32[10,1,128]{2,1,0:T(1,128)S(1)}, f32[10,1,128]{2,1,0:T(1,128)S(1)}, u32[]{:S(2)}, u32[]{:S(2)}) collective-permute-start(f32[10,1,128]{2,1,0:T(1,128)S(1)} %get-tuple-element.404), channel_id=1, source_target_pairs={{1,0},{2,1},{3,2},{4,3},{5,4},{6,5},{7,6},{9,8},{10,9},{11,10},{12... | collective-permute-start | bytes 15368 | tf_op jit(solution)/shard_map/ppermute | solution.py:26
  93.7 7.6 collective-permute-start.6
  108.7 7.1 collective-permute-start.10
  116.8 5.9 collective-permute-start.12
  123.7 7.0 collective-permute-start.14
  125.6 5.8 collective-permute-start.15
  131.6 5.9 collective-permute-start.16
  138.5 7.0 collective-permute-start.18
  140.4 5.8 collective-permute-start.19
  146.4 5.9 collective-permute-start.20
  153.3 7.0 collective-permute-start.22
  161.2 7.9 collective-permute-start.24
  162.5 7.6 collective-permute-start.25
  170.1 7.0 collective-permute-start.26
  178.0 8.0 collective-permute-start.28
  179.3 7.7 collective-permute-start.29
  187.0 7.0 collective-permute-start.30
  194.9 8.0 collective-permute-start.32
  196.2 7.7 collective-permute-start.33
  203.9 7.0 collective-permute-start.34
  218.6 36.9 %all-to-all-start.1 = ((f32[128,16,128]{2,1,0:T(8,128)}), f32[128,16,128]{2,1,0:T(8,128)}, u32[]{:S(2)}, u32[]{:S(2)}) async-start(f32[128,16,128]{2,1,0:T(8,128)} %bitcast.34), calls=%async_computation.1 | async-start | bytes 2097152 | tf_op jit(solution)/shard_map/all_to_all | solution.py:132
  361.4 6.2 collective-permute-start.38
  369.0 6.1 collective-permute-start.40
  375.9 6.6 collective-permute-start.42
  383.4 5.9 collective-permute-start.44
  390.3 7.0 collective-permute-start.46
  398.2 5.9 collective-permute-start.48
  405.1 7.0 collective-permute-start.50
  558.9 6.4 collective-permute-start.54
  566.2 5.9 collective-permute-start.56
  573.1 7.0 collective-permute-start.58
  581.0 5.9 collective-permute-start.60
  587.9 7.0 collective-permute-start.62
  595.8 5.9 collective-permute-start.64
  602.7 7.0 collective-permute-start.66
  617.3 35.2 %all-to-all-start.3 = ((f32[128,16,128]{2,1,0:T(8,128)}), f32[128,16,128]{2,1,0:T(8,128)}, u32[]{:S(2)}, u32[]{:S(2)}) async-start(f32[128,16,128]{2,1,0:T(8,128)} %bitcast.42), calls=%async_computation.3 | async-start | bytes 2097152 | tf_op jit(solution)/shard_map/all_to_all | solution.py:132
  755.3 6.5 collective-permute-start.70
  762.8 5.9 collective-permute-start.72
  769.7 6.6 collective-permute-start.74
  777.2 5.9 collective-permute-start.76
  784.1 7.0 collective-permute-start.78
  792.0 5.9 collective-permute-start.80
  798.9 7.0 collective-permute-start.82
  (45 other events, 319.4 us)
where the time goes:
time: 895 us; the launch traced here: 883 us
  starting transfers between devices  313 us (35%)
  blocking collectives  256 us (29%)
  matrix products  191 us (21%)
  waiting for transfers between devices  83.8 us (9%)
  local copies, waits for them, and re-layouts  20.7 us (2%)
  other arithmetic  9.8 us (1%)
    ppermute x42, starting transfers between devices, with_halo(): lax.ppermute(tail, axis, [(i, (i + 1) % count) for i in range(ends)])  187 us
    dot_general x12, matrix products, add_block(): lax.dot_general(matrix, spread_rows, (((0,), (0,)), ((), ())), precision=...  123 us
    ppermute x42, starting transfers between devices, with_halo(): lax.ppermute(head, axis, [((i + 1) % count, i) for i in range(ends)])  79.8 us
    psum x1, blocking collectives, on_device(): norm_now = lax.psum(jnp.sum(residual * residual), ('gx', 'gy'))  72.7 us
    psum x1, blocking collectives, on_device(): curvature = lax.psum(jnp.sum(direction * image), ('gx', 'gy'))  72.7 us
    psum x1, blocking collectives, on_device(): norm_next = lax.psum(jnp.sum(residual * residual), ('gx', 'gy'))  63 us
    dot_general x8, matrix products, one_block(): jnp.dot(matrix, received, precision=highest, preferred_element_type=jnp.f...  62.1 us
    all_to_all x2, blocking collectives, adjoint(): lax.all_to_all(returned_rows.reshape(owners, slot_count, levels), ('gx',...  47.2 us
  transfers between devices with their start and end apart: 87, of which 44 were waited for; matrix products, arithmetic and copies ran while one was open for 0% of the time, Pallas kernels for 0%

commit v1 on v0

v1 whole, which is shorter than its diff:
```python
import jax
import jax.numpy as jnp
from jax import lax
from jax.experimental import pallas as pl
from jax.experimental.pallas import tpu as pltpu
from jax.sharding import PartitionSpec as P


MIB = 1 << 20
COUPLING = 0.12
PASSES = 4
HALO = 2 * PASSES
CHUNK = 256
bf16 = jnp.bfloat16
f32 = jnp.float32


def mm(lhs, rhs):
    return jnp.dot(lhs, rhs, preferred_element_type=f32)


def halves(values):
    high = values.astype(bf16)
    return high, (values - high.astype(f32)).astype(bf16)


def live_precision(count_ref, precision_ref, step):
    place = step * CHUNK + lax.broadcasted_iota(jnp.int32, (1, CHUNK), 1)
    return jnp.where(place < count_ref[0], precision_ref[...], 0.0)


def spread_pair(profile, forcing):
    column = jnp.broadcast_to(forcing, (profile.shape[1], CHUNK)).T
    return jnp.concatenate(halves(profile * column), axis=1)


def build_kernel(
    count_ref, rows_ref, weights_ref, innovation_ref, precision_ref, profile_ref,
    high_ref, low_ref, out_ref, total_ref,
):
    step = pl.program_id(0)
    forcing = live_precision(count_ref, precision_ref, step) * innovation_ref[...]
    pair = spread_pair(profile_ref[...], forcing)
    rows = [rows_ref[k : k + 1, :] for k in range(4)]
    weights = [weights_ref[k : k + 1, :] for k in range(4)]
    for k in range(1, 4):
        for j in range(k):
            same = rows[k] == rows[j]
            weights[j] = weights[j] + jnp.where(same, weights[k], 0.0)
            weights[k] = jnp.where(same, 0.0, weights[k])

    @pl.when(step == 0)
    def _():
        total_ref[...] = jnp.zeros_like(total_ref)

    def one(index, carry):
        base = pl.multiple_of(index * CHUNK, CHUNK)
        slot = base + lax.broadcasted_iota(jnp.int32, (CHUNK, CHUNK), 0)
        matrix = jnp.zeros((CHUNK, CHUNK), f32)
        for k in (3, 2, 1, 0):
            matrix = jnp.where(rows[k] == slot, weights[k], matrix)
        high, low = halves(matrix)
        high_ref[0, pl.ds(base, CHUNK), :] = high
        low_ref[0, pl.ds(base, CHUNK), :] = low
        total_ref[pl.ds(base, CHUNK), :] += mm(high, pair) + mm(low, pair)
        return carry

    lax.fori_loop(0, total_ref.shape[0] // CHUNK, one, 0)

    @pl.when(step == pl.num_programs(0) - 1)
    def _():
        levels = out_ref.shape[1]
        out_ref[...] = total_ref[:, :levels] + total_ref[:, levels:]


def transpose_pair(received_ref, turned_ref):
    levels = received_ref.shape[1]

    def one(index, carry):
        base = pl.multiple_of(index * levels, levels)
        high, low = halves(received_ref[pl.ds(base, levels), :].T)
        turned_ref[:levels, pl.ds(base, levels)] = high
        turned_ref[levels:, pl.ds(base, levels)] = low
        return carry

    lax.fori_loop(0, received_ref.shape[0] // levels, one, 0)


def observe(turned_ref, high_ref, low_ref, profile):
    levels = profile.shape[1]
    both = mm(turned_ref[...], high_ref[0]) + mm(turned_ref[...], low_ref[0])
    return jnp.sum(profile.T * (both[:levels] + both[levels:]), axis=0, keepdims=True)


def observe_adjoint_kernel(
    count_ref, received_ref, high_ref, low_ref, precision_ref, profile_ref,
    out_ref, turned_ref, total_ref,
):
    step = pl.program_id(0)

    @pl.when(step == 0)
    def _():
        transpose_pair(received_ref, turned_ref)
        total_ref[...] = jnp.zeros_like(total_ref)

    profile = profile_ref[...]
    seen = observe(turned_ref, high_ref, low_ref, profile)
    pair = spread_pair(profile, live_precision(count_ref, precision_ref, step) * seen)

    def one(index, carry):
        base = pl.multiple_of(index * CHUNK, CHUNK)
        total_ref[pl.ds(base, CHUNK), :] += mm(
            high_ref[0, pl.ds(base, CHUNK), :], pair
        ) + mm(low_ref[0, pl.ds(base, CHUNK), :], pair)
        return carry

    lax.fori_loop(0, total_ref.shape[0] // CHUNK, one, 0)

    @pl.when(step == pl.num_programs(0) - 1)
    def _():
        levels = out_ref.shape[1]
        out_ref[...] = total_ref[:, :levels] + total_ref[:, levels:]


def observe_norm_kernel(
    count_ref, received_ref, high_ref, low_ref, precision_ref, profile_ref, first_ref, second_ref,
    out_ref, turned_ref, total_ref,
):
    step = pl.program_id(0)

    @pl.when(step == 0)
    def _():
        transpose_pair(received_ref, turned_ref)
        total_ref[...] = jnp.zeros_like(total_ref)

    seen = observe(turned_ref, high_ref, low_ref, profile_ref[...])
    total_ref[...] += live_precision(count_ref, precision_ref, step) * seen * seen

    @pl.when(step == pl.num_programs(0) - 1)
    def _():
        lane = lax.broadcasted_iota(jnp.int32, out_ref.shape, 1)
        parts = (first_ref[0], second_ref[0], second_ref[1], total_ref[...])
        row = jnp.zeros(out_ref.shape, f32)
        for k in range(4):
            row = jnp.where(lane == k, jnp.sum(parts[k]), row)
        out_ref[...] = row


def place_kernel(send_ref, arrived_ref, out_ref, pair_ref):
    slots, levels = arrived_ref.shape

    def split(index, carry):
        base = pl.multiple_of(index * CHUNK, CHUNK)
        high, low = halves(arrived_ref[pl.ds(base, CHUNK), :])
        pair_ref[pl.ds(base, CHUNK), :levels] = high
        pair_ref[pl.ds(base, CHUNK), levels:] = low
        return carry

    lax.fori_loop(0, slots // CHUNK, split, 0)
    size = 128

    def one(index, carry):
        base = pl.multiple_of(index * size, size)
        column = base + lax.broadcasted_iota(jnp.int32, (size, slots), 0)
        matrix = jnp.where(column == send_ref[...], 1.0, 0.0).astype(bf16)
        both = mm(matrix, pair_ref[...])
        out_ref[pl.ds(base, size), :] = both[:, :levels] + both[:, levels:]
        return carry

    lax.fori_loop(0, out_ref.shape[0] // size, one, 0)


def smooth_kernel(
    send_ref, centre_ref, up_ref, down_ref, left_ref, right_ref,
    scale_ref, scale_up_ref, scale_down_ref, scale_left_ref, scale_right_ref,
    *rest,
):
    *given, half_ref, full_ref, out_ref, sums_ref, field, east, north = rest
    across, along, levels = centre_ref.shape
    wide, tall = across + 2 * HALO, along + 2 * HALO

    def fill(target, middle, above, below, west, easterly):
        target[HALO : HALO + across, HALO : HALO + along] = middle[...]
        target[:HALO, HALO : HALO + along] = above[...]
        target[HALO + across :, HALO : HALO + along] = below[...]
        target[:, :HALO] = west[...]
        target[:, HALO + along :] = easterly[...]

    fill(field, scale_ref, scale_up_ref, scale_down_ref, scale_left_ref, scale_right_ref)

    def conductance(i, carry):
        here = COUPLING * field[i]
        after = field[jnp.minimum(i + 1, wide - 1)]
        east[i] = here * after
        north[i, : tall - 1] = here[: tall - 1] * field[i, 1:]
        north[i, tall - 1 :] = jnp.zeros((1, levels), f32)
        return carry

    lax.fori_loop(0, wide, conductance, 0)
    fill(field, centre_ref, up_ref, down_ref, left_ref, right_ref)

    def sweep(k):
        def row(i, carry):
            here, inward = carry
            after = field[i + 1, 1:-1]
            outward = east[i, 1:-1] * (after - here)
            above = north[i, 1:-1] * (field[i, 2:] - here)
            below = north[i, :-2] * (here - field[i, :-2])
            field[i, 1:-1] = here + ((outward - inward) + (above - below))
            return after, outward

        here = field[k, 1:-1]
        lax.fori_loop(k, wide - k, row, (here, east[k - 1, 1:-1] * (here - field[k - 1, 1:-1])))

    def middle():
        return field[HALO : HALO + across, HALO : HALO + along]

    for k in range(1, PASSES + 1):
        sweep(k)
    half = middle()
    half_ref[...] = half
    if given:
        sums_ref[0] = jnp.sum((given[0][...] * half).reshape(-1, 8, levels), axis=0)
        sums_ref[1] = jnp.sum((half * half).reshape(-1, 8, levels), axis=0)
    else:
        sums_ref[0] = jnp.sum((half * half).reshape(-1, 8, levels), axis=0)
    for k in range(PASSES + 1, HALO + 1):
        sweep(k)
    full = middle()
    full_ref[...] = full
    columns = across * along
    pair = jnp.concatenate(halves(full.reshape(columns, levels)), axis=1)

    def gather(index, carry):
        base = pl.multiple_of(index * levels, levels)
        wanted = jnp.broadcast_to(send_ref[:, pl.ds(base, levels)].astype(f32), (levels, levels)).T
        lane = lax.broadcasted_iota(jnp.int32, (levels, levels), 1).astype(f32)
        matrix = jnp.concatenate(
            [jnp.where(wanted == lane + q, 1.0, 0.0).astype(bf16) for q in range(0, columns, levels)],
            axis=1,
        )
        both = mm(matrix, pair)
        out_ref[pl.ds(base, levels), :] = both[:, :levels] + both[:, levels:]
        return carry

    lax.fori_loop(0, out_ref.shape[0] // levels, gather, 0)


def finish_kernel(sums_ref, b_ref, sb_ref, p_ref, sp_ref, control_ref, increment_ref):
    total = jnp.sum(sums_ref[...], axis=0, keepdims=True)
    lane = lax.broadcasted_iota(jnp.int32, total.shape, 1)
    a, c, e, f = [jnp.sum(jnp.where(lane == k, total, 0.0), axis=1, keepdims=True) for k in range(4)]
    slope = c / a
    first = 1.0 / (1.0 + slope)
    rest = e / a - slope * slope
    ratio = first * first * rest
    curved = rest + (f / a - 2.0 * slope * (e / a) + slope * slope * slope)
    second = ratio / (first * first * curved - ratio * ratio * (1.0 + slope))
    of_b = first + second * (ratio + first * slope)
    of_p = -second * first
    control_ref[...] = of_b * b_ref[...] + of_p * p_ref[...]
    increment_ref[...] = of_b * sb_ref[...] + of_p * sp_ref[...]


def step_from(cells, axis, up):
    count = lax.axis_size(axis)
    pairs = [(i, i + 1) if up else (i + 1, i) for i in range(count - 1)]
    return lax.ppermute(cells, axis, pairs)


def rims(cells):
    along = cells.shape[1]
    up = step_from(cells, "gx", True)
    down = step_from(cells, "gx", False)
    tail = jnp.concatenate([x[:, along - HALO :] for x in (up, cells, down)], axis=0)
    head = jnp.concatenate([x[:, :HALO] for x in (up, cells, down)], axis=0)
    return up, down, step_from(tail, "gy", True), step_from(head, "gy", False)


def exchange(rows):
    return lax.all_to_all(rows, ("gx", "gy"), split_axis=0, concat_axis=0, tiled=True)


def params(mib):
    return pltpu.CompilerParams(vmem_limit_bytes=mib * MIB)


def on_device(
    length_scale, innovation, observed_precision, profile_weight, stencil_weight, send_rows, stencil_rows, obs_count,
):
    across, along, levels = length_scale.shape
    owners, slot_count = send_rows.shape[1:]
    slots = owners * slot_count
    columns = across * along
    obs = innovation.shape[0]
    steps = obs // CHUNK
    send = send_rows.reshape(1, slots)
    innovation = innovation.reshape(1, obs)
    precision = observed_precision.reshape(1, obs)
    scale_rims = rims(length_scale)

    whole = pl.BlockSpec(memory_space=pltpu.VMEM)
    scalar = pl.BlockSpec(memory_space=pltpu.SMEM)
    four = pl.BlockSpec((4, CHUNK), lambda i: (0, i))
    line = pl.BlockSpec((1, CHUNK), lambda i: (0, i))
    profile = pl.BlockSpec((CHUNK, levels), lambda i: (i, 0))
    block = pl.BlockSpec((1, slots, CHUNK), lambda i: (i, 0, 0))
    rows_all = pl.BlockSpec((slots, levels), lambda i: (0, 0))
    half_matrix = jax.ShapeDtypeStruct((steps, slots, CHUNK), bf16)
    slot_rows = jax.ShapeDtypeStruct((slots, levels), f32)
    tile = jax.ShapeDtypeStruct((across, along, levels), f32)

    def trade(rows):
        return exchange(rows.reshape(owners, slot_count, levels)).reshape(slots, levels)

    def to_columns(arrived):
        return pl.pallas_call(
            place_kernel,
            out_shape=jax.ShapeDtypeStruct((columns, levels), f32),
            in_specs=[whole, whole],
            out_specs=whole,
            scratch_shapes=[pltpu.VMEM((slots, 2 * levels), bf16)],
            compiler_params=params(24),
            name="place",
        )(send, arrived).reshape(across, along, levels)

    def smooth_twice(cells, given):
        grown = (across + 2 * HALO, along + 2 * HALO, levels)
        count = 1 + len(given)
        return pl.pallas_call(
            smooth_kernel,
            out_shape=(tile, tile, slot_rows, jax.ShapeDtypeStruct((count, 8, levels), f32)),
            in_specs=[whole] * (11 + len(given)),
            out_specs=(whole,) * 4,
            scratch_shapes=[pltpu.VMEM(grown, f32)] * 3,
            compiler_params=params(24),
            name="smooth",
        )(send, cells, *rims(cells), length_scale, *scale_rims, *given)

    high, low, spread = pl.pallas_call(
        build_kernel,
        grid=(steps,),
        out_shape=(half_matrix, half_matrix, slot_rows),
        in_specs=[scalar, four, four, line, line, profile],
        out_specs=(block, block, rows_all),
        scratch_shapes=[pltpu.VMEM((slots, 2 * levels), f32)],
        compiler_params=params(32),
        name="build",
    )(obs_count, stencil_rows, stencil_weight, innovation, precision, profile_weight)

    b, sb, outgoing, first_sums = smooth_twice(to_columns(trade(spread)), ())

    spread = pl.pallas_call(
        observe_adjoint_kernel,
        grid=(steps,),
        out_shape=slot_rows,
        in_specs=[scalar, rows_all, block, block, line, profile],
        out_specs=rows_all,
        scratch_shapes=[pltpu.VMEM((2 * levels, slots), bf16), pltpu.VMEM((slots, 2 * levels), f32)],
        compiler_params=params(32),
        name="observe_adjoint",
    )(obs_count, trade(outgoing), high, low, precision, profile_weight)

    p, sp, outgoing, second_sums = smooth_twice(to_columns(trade(spread)), (b,))

    sums = pl.pallas_call(
        observe_norm_kernel,
        grid=(steps,),
        out_shape=jax.ShapeDtypeStruct((owners, levels), f32),
        in_specs=[
            scalar, rows_all, block, block, line, profile,
            pl.BlockSpec((1, 8, levels), lambda i: (0, 0, 0)),
            pl.BlockSpec((2, 8, levels), lambda i: (0, 0, 0)),
        ],
        out_specs=pl.BlockSpec((owners, levels), lambda i: (0, 0)),
        scratch_shapes=[pltpu.VMEM((2 * levels, slots), bf16), pltpu.VMEM((1, CHUNK), f32)],
        compiler_params=params(32),
        name="observe_norm",
    )(obs_count, trade(outgoing), high, low, precision, profile_weight, first_sums, second_sums)

    sums = exchange(sums.reshape(owners, 1, levels)).reshape(owners, levels)

    return pl.pallas_call(
        finish_kernel,
        out_shape=(
            jax.ShapeDtypeStruct((columns, levels), f32),
            jax.ShapeDtypeStruct((columns, levels), f32),
        ),
        in_specs=[whole] * 5,
        out_specs=(whole, whole),
        compiler_params=params(16),
        name="finish",
    )(sums, *(x.reshape(columns, levels) for x in (b, sb, p, sp)))


def solution(mesh):
    def run(*args):
        control, increment = on_device(*args)
        shape = args[0].shape
        return control.reshape(shape), increment.reshape(shape)

    return jax.shard_map(
        run,
        mesh=mesh,
        in_specs=(
            P("gx", "gy", None),
            P(("gx", "gy")),
            P(("gx", "gy")),
            P(("gx", "gy"), None),
            P(None, ("gx", "gy")),
            P(("gx", "gy"), None, None),
            P(None, ("gx", "gy")),
            P(("gx", "gy")),
        ),
        out_specs=(P("gx", "gy", None), P("gx", "gy", None)),
        check_vma=False,
    )
```

time: 895 us -> 259 us (0.29); the launches traced: 883 us -> 258 us
  starting transfers between devices: 313 us -> 45.7 us
  matrix products: 191 us -> 0 us
  blocking collectives: 256 us -> 94.8 us
  Pallas kernels: 0 us -> 67.7 us
  waiting for transfers between devices: 83.8 us -> 28.4 us
  other arithmetic: 9.8 us -> 0.06 us
    ppermute x84 -> x12, starting transfers between devices: 267 us -> 34.2 us  [step_from(): return lax.ppermute(cells, axis, pairs)]
    psum x3 -> x0, blocking collectives: 208 us -> none  [the longest x1 72.7 us: on_device(): norm_now = lax.psum(jnp.sum(residual * residual), ('gx', 'gy'))]
    dot_general x23 -> x0, matrix products: 191 us -> none  [the longest x12 123 us: add_block(): lax.dot_general(matrix, spread_rows, (((0,), (0,)), ((), ())), precision=...]
    pallas_call x0 -> x8, Pallas kernels: none -> 67.7 us  [the longest x1 23.5 us: on_device(): pl.pallas_call(observe_adjoint_kernel, grid=(steps,), out_shape=slot_rows...]
    all_to_all x2 -> x4, blocking collectives: 47.2 us -> 94.8 us  [exchange(): lax.all_to_all(rows, ('gx', 'gy'), split_axis=0, concat_axis=0, tiled=True)]
    all_to_all x3 -> x1, waiting for transfers between devices: 41.2 us -> 0.01 us  [exchange(): lax.all_to_all(rows, ('gx', 'gy'), split_axis=0, concat_axis=0, tiled=True)]
    all_to_all x3 -> x1, starting transfers between devices: 46.4 us -> 11.5 us  [exchange(): lax.all_to_all(rows, ('gx', 'gy'), split_axis=0, concat_axis=0, tiled=True)]
    unnamed x17 -> x27, local copies, waits for them, and re-layouts: 0.16 us -> 19.2 us
  transfers between devices with their start and end apart: 87 -> 13, of which waited for: 44 -> 7; matrix products, arithmetic and copies ran while one was open for 0% -> 1% of each run, Pallas kernels for 0% -> 1%
where the time goes in v1:
time: 259 us; the launch traced here: 258 us
  blocking collectives  94.8 us (37%)
  Pallas kernels  67.7 us (26%)
  starting transfers between devices  45.7 us (18%)
  waiting for transfers between devices  28.4 us (11%)
  local copies, waits for them, and re-layouts  20.1 us (8%)
    all_to_all x4, blocking collectives, exchange(): lax.all_to_all(rows, ('gx', 'gy'), split_axis=0, concat_axis=0, tiled=True)  94.8 us
    ppermute x12, starting transfers between devices, step_from(): return lax.ppermute(cells, axis, pairs)  34.2 us
    ppermute x12, waiting for transfers between devices, step_from(): return lax.ppermute(cells, axis, pairs)  28.4 us
    pallas_call x1, Pallas kernels, on_device(): pl.pallas_call(observe_adjoint_kernel, grid=(steps,), out_shape=slot_rows...  23.5 us
    unnamed x27, local copies, waits for them, and re-layouts  19.2 us
    pallas_call x1, Pallas kernels, on_device(): pl.pallas_call(build_kernel, grid=(steps,), out_shape=(half_matrix, half_...  18.8 us
    pallas_call x2, Pallas kernels, smooth_twice(): pl.pallas_call(smooth_kernel, out_shape=(tile, tile, slot_rows, jax.Shape...  13.6 us
    all_to_all x1, starting transfers between devices, exchange(): lax.all_to_all(rows, ('gx', 'gy'), split_axis=0, concat_axis=0, tiled=True)  11.5 us
  transfers between devices with their start and end apart: 13, of which 7 were waited for; matrix products, arithmetic and copies ran while one was open for 1% of the time, Pallas kernels for 1%

profile of v1, /device:TPU:1, one launch (start us, length us, event | category | flops | bytes accessed | tf_op | source)
XLA Modules:
  0.0 258.3 jit_solution(11196608616293665464)
XLA Ops:
  1.3 1.2 copy-done.4
  2.5 0.7 copy-done.8
  3.2 0.8 copy-done.10
  4.0 0.8 copy-done.11
  4.7 0.7 copy-done.12
  5.4 18.8 %build.1 = (bf16[8,2048,256]{2,1,0:T(8,128)(2,1)S(1)}, bf16[8,2048,256]{2,1,0:T(8,128)(2,1)S(1)}, f32[2048,128]{1,0:T(8,128)}) custom-call(s32[1]{0:T(128)S(6)} %copy.14.count_ref, s32[4,2048]{1,0:T(4,128)S(1)} %copy-done.10, f32[4,2048]{1,0:T(4,128)S(1)} %copy-done.11, f32[1,2048]{1,0:T(1,128)S(1)} %bitcast.46, f32[1,2048]{1,0:T(1,128)S(1)} %bitcast.43, ...), custom_call_target="tpu_custom_call" | custom-call | tf_op jit(solution)/shard_map/build/pallas_call | solution.py:340
  24.2 3.3 %copy-done = bf16[8,2048,256]{2,1,0:T(8,128)(2,1)} copy-done((bf16[8,2048,256]{2,1,0:T(8,128)(2,1)}, bf16[8,2048,256]{2,1,0:T(8,128)(2,1)S(1)}, u32[]{:S(2)}) %copy-start) | copy-done | bytes 8388632
  27.5 3.2 %copy-done.2 = bf16[8,2048,256]{2,1,0:T(8,128)(2,1)} copy-done((bf16[8,2048,256]{2,1,0:T(8,128)(2,1)}, bf16[8,2048,256]{2,1,0:T(8,128)(2,1)S(1)}, u32[]{:S(2)}) %copy-start.2) | copy-done | bytes 8388632
  30.7 11.5 %all-to-all-start = ((f32[128,16,128]{2,1,0:T(8,128)}), f32[128,16,128]{2,1,0:T(8,128)S(1)}, u32[]{:S(2)}, u32[]{:S(2)}) async-start(f32[128,16,128]{2,1,0:T(8,128)} %bitcast.2), calls=%async_computation | async-start | bytes 2097152 | tf_op jit(solution)/shard_map/all_to_all | solution.py:281
  42.2 1.3 collective-permute-start.5
  43.5 4.0 %collective-permute-start.4 = (f32[8,64,128]{2,1,0:T(8,128)}, f32[8,64,128]{2,1,0:T(8,128)S(1)}, u32[]{:S(2)}, u32[]{:S(2)}) collective-permute-start(f32[8,64,128]{2,1,0:T(8,128)} %scale_ref.3), channel_id=1, source_target_pairs={{0,8},{8,16},{16,24},{24,32},{32,40},{40,48},{48,56},{56,64},{64,7... | collective-permute-start | bytes 786440 | tf_op jit(solution)/shard_map/ppermute | solution.py:268
  47.5 0.8 fusion.4
  48.4 0.8 copy.12
  49.1 0.1 reshape.67.send_ref
  49.2 11.3 %collective-permute-done.5.scale_down_ref = f32[8,64,128]{2,1,0:T(8,128)S(1)} collective-permute-done((f32[8,64,128]{2,1,0:T(8,128)}, f32[8,64,128]{2,1,0:T(8,128)S(1)}, u32[]{:S(2)}, u32[]{:S(2)}) %collective-permute-start.5) | collective-permute-done | bytes 262176 | tf_op jit(solution)/shard_map/ppermute | solution.py:268
  60.6 3.9 %collective-permute-start.6 = (f32[24,8,128]{2,1,0:T(8,128)S(1)}, f32[24,8,128]{2,1,0:T(8,128)S(1)}, u32[]{:S(2)}, u32[]{:S(2)}) collective-permute-start(f32[24,8,128]{2,1,0:T(8,128)S(1)} %pad_maximum_fusion.2), channel_id=1, source_target_pairs={{0,1},{1,2},{2,3},{3,4},{4,5},{5,6},{6,7},{8,9},{9,10},{10,11},{11... | collective-permute-start | bytes 294920 | tf_op jit(solution)/shard_map/ppermute | solution.py:268
  64.5 1.4 place.2
  65.9 1.3 collective-permute-start.1
  67.3 1.9 collective-permute-start.7
  69.2 4.0 %collective-permute-start = (f32[8,64,128]{2,1,0:T(8,128)S(1)}, f32[8,64,128]{2,1,0:T(8,128)S(1)}, u32[]{:S(2)}, u32[]{:S(2)}) collective-permute-start(f32[8,64,128]{2,1,0:T(8,128)S(1)} %bitcast.28), channel_id=1, source_target_pairs={{0,8},{8,16},{16,24},{24,32},{32,40},{40,48},{48,56},{56,64},{64,7... | collective-permute-start | bytes 786440 | tf_op jit(solution)/shard_map/ppermute | solution.py:268
  73.2 2.0 collective-permute-done.1.down_ref
  75.2 3.1 %collective-permute-done.up_ref = f32[8,64,128]{2,1,0:T(8,128)S(1)} collective-permute-done((f32[8,64,128]{2,1,0:T(8,128)S(1)}, f32[8,64,128]{2,1,0:T(8,128)S(1)}, u32[]{:S(2)}, u32[]{:S(2)}) %collective-permute-start) | collective-permute-done | bytes 262176 | tf_op jit(solution)/shard_map/ppermute | solution.py:268
  78.3 4.4 %collective-permute-start.2 = (f32[24,8,128]{2,1,0:T(8,128)S(1)}, f32[24,8,128]{2,1,0:T(8,128)S(1)}, u32[]{:S(2)}, u32[]{:S(2)}) collective-permute-start(f32[24,8,128]{2,1,0:T(8,128)S(1)} %pad_maximum_fusion), channel_id=1, source_target_pairs={{0,1},{1,2},{2,3},{3,4},{4,5},{5,6},{6,7},{8,9},{9,10},{10,11},{11... | collective-permute-start | bytes 294920 | tf_op jit(solution)/shard_map/ppermute | solution.py:268
  82.7 1.9 collective-permute-start.3
  84.6 0.0 collective-permute-done.7.scale_right_ref
  84.7 0.0 collective-permute-done.2.left_ref
  84.7 4.0 %collective-permute-done.3.right_ref = f32[24,8,128]{2,1,0:T(8,128)S(1)} collective-permute-done((f32[24,8,128]{2,1,0:T(8,128)S(1)}, f32[24,8,128]{2,1,0:T(8,128)S(1)}, u32[]{:S(2)}, u32[]{:S(2)}) %collective-permute-start.3) | collective-permute-done | bytes 98336 | tf_op jit(solution)/shard_map/ppermute | solution.py:268
  88.6 0.9 copy-done.6
  89.6 6.8 %smooth.2 = (f32[8,64,128]{2,1,0:T(8,128)S(1)}, f32[8,64,128]{2,1,0:T(8,128)S(1)}, f32[2048,128]{1,0:T(8,128)S(1)}, f32[1,8,128]{2,1,0:T(8,128)S(1)}) custom-call(s32[1,2048]{1,0:T(1,128)S(1)} %reshape.67.send_ref, f32[8,64,128]{2,1,0:T(8,128)S(1)} %bitcast.30, f32[8,64,128]{2,1,0:T(8,128)S(1)} %collective-permute-done.up_ref, ...), custom_call_target="tpu_custom_call" | custom-call | tf_op jit(solution)/shard_map/smooth/pallas_call | solution.py:330
  96.4 30.4 %all_to_all.25 = f32[128,16,128]{2,1,0:T(8,128)S(1)} all-to-all(f32[128,16,128]{2,1,0:T(8,128)S(1)} %bitcast.37), channel_id=1, replica_groups=mesh['gx'=16,'gy'=8] {'gx','gy'}, dimensions={0} | all-to-all | bytes 2097152 | tf_op jit(solution)/shard_map/all_to_all | solution.py:281
  126.9 3.4 %copy-done.1 = bf16[8,2048,256]{2,1,0:T(8,128)(2,1)S(1)} copy-done((bf16[8,2048,256]{2,1,0:T(8,128)(2,1)S(1)}, bf16[8,2048,256]{2,1,0:T(8,128)(2,1)}, u32[]{:S(2)}) %copy-start.1) | copy-done | bytes 8388632
  130.2 3.4 %copy-done.3 = bf16[8,2048,256]{2,1,0:T(8,128)(2,1)S(1)} copy-done((bf16[8,2048,256]{2,1,0:T(8,128)(2,1)S(1)}, bf16[8,2048,256]{2,1,0:T(8,128)(2,1)}, u32[]{:S(2)}) %copy-start.3) | copy-done | bytes 8388632
  133.6 23.5 %observe_adjoint.1 = f32[2048,128]{1,0:T(8,128)S(1)} custom-call(s32[1]{0:T(128)S(6)} %copy.14.count_ref, f32[2048,128]{1,0:T(8,128)S(1)} %bitcast.25, bf16[8,2048,256]{2,1,0:T(8,128)(2,1)S(1)} %copy-done.1, bf16[8,2048,256]{2,1,0:T(8,128)(2,1)S(1)} %copy-done.3, f32[1,2048]{1,0:T(1,128)S(1)} %bitcast.44, f32[2048,128]{1,0:T(8,128)S(1)} %copy-done.5), custom_call_target="tpu_custom_call" | custom-call | tf_op jit(solution)/shard_map/observe_adjoint/pallas_call | solution.py:353
  157.2 23.3 %all_to_all.26 = f32[128,16,128]{2,1,0:T(8,128)S(1)} all-to-all(f32[128,16,128]{2,1,0:T(8,128)S(1)} %bitcast.26), channel_id=1, replica_groups=mesh['gx'=16,'gy'=8] {'gx','gy'}, dimensions={0} | all-to-all | bytes 2097152 | tf_op jit(solution)/shard_map/all_to_all | solution.py:281
  180.4 1.4 place.3
  181.9 1.3 collective-permute-start.9
  183.2 4.0 %collective-permute-start.8 = (f32[8,64,128]{2,1,0:T(8,128)S(1)}, f32[8,64,128]{2,1,0:T(8,128)S(1)}, u32[]{:S(2)}, u32[]{:S(2)}) collective-permute-start(f32[8,64,128]{2,1,0:T(8,128)S(1)} %bitcast.32), channel_id=1, source_target_pairs={{0,8},{8,16},{16,24},{24,32},{32,40},{40,48},{48,56},{56,64},{64,7... | collective-permute-start | bytes 786440 | tf_op jit(solution)/shard_map/ppermute | solution.py:268
  187.2 3.1 %collective-permute-done.9.down_ref = f32[8,64,128]{2,1,0:T(8,128)S(1)} collective-permute-done((f32[8,64,128]{2,1,0:T(8,128)S(1)}, f32[8,64,128]{2,1,0:T(8,128)S(1)}, u32[]{:S(2)}, u32[]{:S(2)}) %collective-permute-start.9) | collective-permute-done | bytes 262176 | tf_op jit(solution)/shard_map/ppermute | solution.py:268
  190.4 0.9 collective-permute-done.8.up_ref
  191.3 4.3 %collective-permute-start.10 = (f32[24,8,128]{2,1,0:T(8,128)S(1)}, f32[24,8,128]{2,1,0:T(8,128)S(1)}, u32[]{:S(2)}, u32[]{:S(2)}) collective-permute-start(f32[24,8,128]{2,1,0:T(8,128)S(1)} %pad_maximum_fusion.4), channel_id=1, source_target_pairs={{0,1},{1,2},{2,3},{3,4},{4,5},{5,6},{6,7},{8,9},{9,10},{10,11},{11... | collective-permute-start | bytes 294920 | tf_op jit(solution)/shard_map/ppermute | solution.py:268
  195.6 1.9 collective-permute-start.11
  197.5 0.0 collective-permute-done.10.left_ref
  197.6 4.0 %collective-permute-done.11.right_ref = f32[24,8,128]{2,1,0:T(8,128)S(1)} collective-permute-done((f32[24,8,128]{2,1,0:T(8,128)S(1)}, f32[24,8,128]{2,1,0:T(8,128)S(1)}, u32[]{:S(2)}, u32[]{:S(2)}) %collective-permute-start.11) | collective-permute-done | bytes 98336 | tf_op jit(solution)/shard_map/ppermute | solution.py:268
  201.6 6.8 %smooth.3 = (f32[8,64,128]{2,1,0:T(8,128)S(1)}, f32[8,64,128]{2,1,0:T(8,128)S(1)}, f32[2048,128]{1,0:T(8,128)S(1)}, f32[2,8,128]{2,1,0:T(8,128)S(1)}) custom-call(s32[1,2048]{1,0:T(1,128)S(1)} %reshape.67.send_ref, f32[8,64,128]{2,1,0:T(8,128)S(1)} %bitcast.34, f32[8,64,128]{2,1,0:T(8,128)S(1)} %collective-permute-done.8.up_ref, ...), custom_call_target="tpu_custom_call" | custom-call | tf_op jit(solution)/shard_map/smooth/pallas_call | solution.py:330
  208.4 27.1 %all_to_all.27 = f32[128,16,128]{2,1,0:T(8,128)S(1)} all-to-all(f32[128,16,128]{2,1,0:T(8,128)S(1)} %bitcast.36), channel_id=1, replica_groups=mesh['gx'=16,'gy'=8] {'gx','gy'}, dimensions={0} | all-to-all | bytes 2097152 | tf_op jit(solution)/shard_map/all_to_all | solution.py:281
  235.5 7.9 %observe_norm.1 = f32[128,128]{1,0:T(8,128)S(1)} custom-call(s32[1]{0:T(128)S(6)} %copy.14.count_ref, f32[2048,128]{1,0:T(8,128)S(1)} %bitcast.24, bf16[8,2048,256]{2,1,0:T(8,128)(2,1)S(1)} %copy-done.1, bf16[8,2048,256]{2,1,0:T(8,128)(2,1)S(1)} %copy-done.3, f32[1,2048]{1,0:T(1,128)S(1)} %bitcast.45, f32[2048,128]{1,0:T(8,128)S(1)} %copy-done.5, ...), custom_call_target="tpu_custom_call" | custom-call | tf_op jit(solution)/shard_map/observe_norm/pallas_call | solution.py:366
  243.3 14.0 %all_to_all.28 = f32[128,1,128]{2,1,0:T(1,128)S(1)} all-to-all(f32[128,1,128]{2,1,0:T(1,128)S(1)} %bitcast.38), channel_id=1, replica_groups=mesh['gx'=16,'gy'=8] {'gx','gy'}, dimensions={0} | all-to-all | bytes 131072 | tf_op jit(solution)/shard_map/all_to_all | solution.py:281
  257.3 1.0 finish.1
  (33 shorter events, 0.1 us)
Async XLA Ops:
  1.3 1.2 copy-start.4
  2.5 0.7 copy-start.8
  3.2 0.8 copy-start.10
  4.0 0.8 copy-start.11
  4.7 0.7 copy-start.12
  5.4 121.4 %copy-start.5 = (f32[2048,128]{1,0:T(8,128)S(1)}, f32[2048,128]{1,0:T(8,128)}, u32[]{:S(2)}) copy-start(f32[2048,128]{1,0:T(8,128)} %profile_ref.5) | copy-start | bytes 3145732
  5.4 121.4 %copy-start.9 = (f32[2048]{0:T(1024)S(1)}, f32[2048]{0:T(1024)}, u32[]{:S(2)}) copy-start(f32[2048]{0:T(1024)} %param.10) | copy-start | bytes 24580
  24.2 3.3 %copy-start = (bf16[8,2048,256]{2,1,0:T(8,128)(2,1)}, bf16[8,2048,256]{2,1,0:T(8,128)(2,1)S(1)}, u32[]{:S(2)}) copy-start(bf16[8,2048,256]{2,1,0:T(8,128)(2,1)S(1)} %get-tuple-element.17.high_ref) | copy-start | bytes 25165828
  27.5 3.2 %copy-start.2 = (bf16[8,2048,256]{2,1,0:T(8,128)(2,1)}, bf16[8,2048,256]{2,1,0:T(8,128)(2,1)S(1)}, u32[]{:S(2)}) copy-start(bf16[8,2048,256]{2,1,0:T(8,128)(2,1)S(1)} %get-tuple-element.18.low_ref) | copy-start | bytes 25165828
  30.7 33.8 %all-to-all-start = ((f32[128,16,128]{2,1,0:T(8,128)}), f32[128,16,128]{2,1,0:T(8,128)S(1)}, u32[]{:S(2)}, u32[]{:S(2)}) async-start(f32[128,16,128]{2,1,0:T(8,128)} %bitcast.2), calls=%async_computation | async-start | bytes 2097152 | tf_op jit(solution)/shard_map/all_to_all | solution.py:281
  42.2 18.3 %collective-permute-start.5 = (f32[8,64,128]{2,1,0:T(8,128)}, f32[8,64,128]{2,1,0:T(8,128)S(1)}, u32[]{:S(2)}, u32[]{:S(2)}) collective-permute-start(f32[8,64,128]{2,1,0:T(8,128)} %scale_ref.3), channel_id=1, source_target_pairs={{8,0},{16,8},{24,16},{32,24},{40,32},{48,40},{56,48},{64,56},{72,6... | collective-permute-start | bytes 786440 | tf_op jit(solution)/shard_map/ppermute | solution.py:268
  43.5 17.1 %collective-permute-start.4 = (f32[8,64,128]{2,1,0:T(8,128)}, f32[8,64,128]{2,1,0:T(8,128)S(1)}, u32[]{:S(2)}, u32[]{:S(2)}) collective-permute-start(f32[8,64,128]{2,1,0:T(8,128)} %scale_ref.3), channel_id=1, source_target_pairs={{0,8},{8,16},{16,24},{24,32},{32,40},{40,48},{48,56},{56,64},{64,7... | collective-permute-start | bytes 786440 | tf_op jit(solution)/shard_map/ppermute | solution.py:268
  60.6 24.0 %collective-permute-start.6 = (f32[24,8,128]{2,1,0:T(8,128)S(1)}, f32[24,8,128]{2,1,0:T(8,128)S(1)}, u32[]{:S(2)}, u32[]{:S(2)}) collective-permute-start(f32[24,8,128]{2,1,0:T(8,128)S(1)} %pad_maximum_fusion.2), channel_id=1, source_target_pairs={{0,1},{1,2},{2,3},{3,4},{4,5},{5,6},{6,7},{8,9},{9,10},{10,11},{11... | collective-permute-start | bytes 294920 | tf_op jit(solution)/shard_map/ppermute | solution.py:268
  65.9 9.3 %collective-permute-start.1 = (f32[8,64,128]{2,1,0:T(8,128)S(1)}, f32[8,64,128]{2,1,0:T(8,128)S(1)}, u32[]{:S(2)}, u32[]{:S(2)}) collective-permute-start(f32[8,64,128]{2,1,0:T(8,128)S(1)} %bitcast.27), channel_id=1, source_target_pairs={{8,0},{16,8},{24,16},{32,24},{40,32},{48,40},{56,48},{64,56},{72,6... | collective-permute-start | bytes 786440 | tf_op jit(solution)/shard_map/ppermute | solution.py:268
  67.3 17.4 %collective-permute-start.7 = (f32[24,8,128]{2,1,0:T(8,128)S(1)}, f32[24,8,128]{2,1,0:T(8,128)S(1)}, u32[]{:S(2)}, u32[]{:S(2)}) collective-permute-start(f32[24,8,128]{2,1,0:T(8,128)S(1)} %pad_maximum_fusion.3), channel_id=1, source_target_pairs={{1,0},{2,1},{3,2},{4,3},{5,4},{6,5},{7,6},{9,8},{10,9},{11,10},{12... | collective-permute-start | bytes 294920 | tf_op jit(solution)/shard_map/ppermute | solution.py:268
  69.2 9.1 %collective-permute-start = (f32[8,64,128]{2,1,0:T(8,128)S(1)}, f32[8,64,128]{2,1,0:T(8,128)S(1)}, u32[]{:S(2)}, u32[]{:S(2)}) collective-permute-start(f32[8,64,128]{2,1,0:T(8,128)S(1)} %bitcast.28), channel_id=1, source_target_pairs={{0,8},{8,16},{16,24},{24,32},{32,40},{40,48},{48,56},{56,64},{64,7... | collective-permute-start | bytes 786440 | tf_op jit(solution)/shard_map/ppermute | solution.py:268
  78.3 6.4 %collective-permute-start.2 = (f32[24,8,128]{2,1,0:T(8,128)S(1)}, f32[24,8,128]{2,1,0:T(8,128)S(1)}, u32[]{:S(2)}, u32[]{:S(2)}) collective-permute-start(f32[24,8,128]{2,1,0:T(8,128)S(1)} %pad_maximum_fusion), channel_id=1, source_target_pairs={{0,1},{1,2},{2,3},{3,4},{4,5},{5,6},{6,7},{8,9},{9,10},{10,11},{11... | collective-permute-start | bytes 294920 | tf_op jit(solution)/shard_map/ppermute | solution.py:268
  82.7 5.9 %collective-permute-start.3 = (f32[24,8,128]{2,1,0:T(8,128)S(1)}, f32[24,8,128]{2,1,0:T(8,128)S(1)}, u32[]{:S(2)}, u32[]{:S(2)}) collective-permute-start(f32[24,8,128]{2,1,0:T(8,128)S(1)} %pad_maximum_fusion.1), channel_id=1, source_target_pairs={{1,0},{2,1},{3,2},{4,3},{5,4},{6,5},{7,6},{9,8},{10,9},{11,10},{12... | collective-permute-start | bytes 294920 | tf_op jit(solution)/shard_map/ppermute | solution.py:268
  88.6 1.0 copy-start.6
  126.9 3.4 %copy-start.1 = (bf16[8,2048,256]{2,1,0:T(8,128)(2,1)S(1)}, bf16[8,2048,256]{2,1,0:T(8,128)(2,1)}, u32[]{:S(2)}) copy-start(bf16[8,2048,256]{2,1,0:T(8,128)(2,1)} %copy-done) | copy-start | bytes 25165828
  130.2 3.4 %copy-start.3 = (bf16[8,2048,256]{2,1,0:T(8,128)(2,1)S(1)}, bf16[8,2048,256]{2,1,0:T(8,128)(2,1)}, u32[]{:S(2)}) copy-start(bf16[8,2048,256]{2,1,0:T(8,128)(2,1)} %copy-done.2) | copy-start | bytes 25165828
  133.6 67.9 %copy-start.7 = (f32[8,64,128]{2,1,0:T(8,128)S(1)}, f32[8,64,128]{2,1,0:T(8,128)}, u32[]{:S(2)}) copy-start(f32[8,64,128]{2,1,0:T(8,128)} %scale_ref.3) | copy-start | bytes 786436
  181.9 8.4 %collective-permute-start.9 = (f32[8,64,128]{2,1,0:T(8,128)S(1)}, f32[8,64,128]{2,1,0:T(8,128)S(1)}, u32[]{:S(2)}, u32[]{:S(2)}) collective-permute-start(f32[8,64,128]{2,1,0:T(8,128)S(1)} %bitcast.31), channel_id=1, source_target_pairs={{8,0},{16,8},{24,16},{32,24},{40,32},{48,40},{56,48},{64,56},{72,6... | collective-permute-start | bytes 786440 | tf_op jit(solution)/shard_map/ppermute | solution.py:268
  183.2 8.0 %collective-permute-start.8 = (f32[8,64,128]{2,1,0:T(8,128)S(1)}, f32[8,64,128]{2,1,0:T(8,128)S(1)}, u32[]{:S(2)}, u32[]{:S(2)}) collective-permute-start(f32[8,64,128]{2,1,0:T(8,128)S(1)} %bitcast.32), channel_id=1, source_target_pairs={{0,8},{8,16},{16,24},{24,32},{32,40},{40,48},{48,56},{56,64},{64,7... | collective-permute-start | bytes 786440 | tf_op jit(solution)/shard_map/ppermute | solution.py:268
  191.3 6.3 %collective-permute-start.10 = (f32[24,8,128]{2,1,0:T(8,128)S(1)}, f32[24,8,128]{2,1,0:T(8,128)S(1)}, u32[]{:S(2)}, u32[]{:S(2)}) collective-permute-start(f32[24,8,128]{2,1,0:T(8,128)S(1)} %pad_maximum_fusion.4), channel_id=1, source_target_pairs={{0,1},{1,2},{2,3},{3,4},{4,5},{5,6},{6,7},{8,9},{9,10},{10,11},{11... | collective-permute-start | bytes 294920 | tf_op jit(solution)/shard_map/ppermute | solution.py:268
  195.6 5.9 %collective-permute-start.11 = (f32[24,8,128]{2,1,0:T(8,128)S(1)}, f32[24,8,128]{2,1,0:T(8,128)S(1)}, u32[]{:S(2)}, u32[]{:S(2)}) collective-permute-start(f32[24,8,128]{2,1,0:T(8,128)S(1)} %pad_maximum_fusion.5), channel_id=1, source_target_pairs={{1,0},{2,1},{3,2},{4,3},{5,4},{6,5},{7,6},{9,8},{10,9},{11,10},{12... | collective-permute-start | bytes 294920 | tf_op jit(solution)/shard_map/ppermute | solution.py:268

commit v2 on v1

v2 whole, which is shorter than its diff:
```python
import jax
import jax.numpy as jnp
from jax import lax
from jax.experimental import pallas as pl
from jax.experimental.pallas import tpu as pltpu
from jax.sharding import PartitionSpec as P


MIB = 1 << 20
COUPLING = 0.12
PASSES = 4
HALO = 2 * PASSES
CHUNK = 256
bf16 = jnp.bfloat16
f32 = jnp.float32


def mm(lhs, rhs):
    return jnp.dot(lhs, rhs, preferred_element_type=f32)


def halves(values):
    high = values.astype(bf16)
    return high, (values - high.astype(f32)).astype(bf16)


def live_precision(count_ref, precision_ref):
    place = lax.broadcasted_iota(jnp.int32, precision_ref.shape, 1)
    return jnp.where(place < count_ref[0], precision_ref[...], 0.0)


def matrix_kernel(rows_hbm, weights_hbm, out_ref, rows_ref, weights_ref, sems):
    copies = [
        pltpu.make_async_copy(rows_hbm, rows_ref, sems.at[0]),
        pltpu.make_async_copy(weights_hbm, weights_ref, sems.at[1]),
    ]
    for copy in copies:
        copy.start()
    for copy in copies:
        copy.wait()
    slots, obs = out_ref.shape[0], rows_ref.shape[1]
    rows = [rows_ref[k : k + 1, :] for k in range(4)]
    weights = [weights_ref[k : k + 1, :] for k in range(4)]
    for k in range(1, 4):
        for j in range(k):
            same = rows[k] == rows[j]
            weights[j] = weights[j] + jnp.where(same, weights[k], 0.0)
            weights[k] = jnp.where(same, 0.0, weights[k])
    parts = [halves(weight) for weight in weights]
    shape = (CHUNK, CHUNK)
    slot = lax.broadcasted_iota(jnp.int32, shape, 0).astype(f32).astype(bf16)

    def one(index, carry):
        base = pl.multiple_of(index * CHUNK, CHUNK)
        near = [(row - base).astype(f32).astype(bf16) for row in rows]
        for at in range(0, obs, CHUNK):
            high = jnp.zeros(shape, bf16)
            low = jnp.zeros(shape, bf16)
            for k in (3, 2, 1, 0):
                cut = slice(at, at + CHUNK)
                hit = jnp.broadcast_to(near[k][:, cut], shape) == slot
                high = jnp.where(hit, jnp.broadcast_to(parts[k][0][:, cut], shape), high)
                low = jnp.where(hit, jnp.broadcast_to(parts[k][1][:, cut], shape), low)
            out_ref[pl.ds(base, CHUNK), at : at + CHUNK] = high
            out_ref[pl.ds(base, CHUNK), obs + at : obs + at + CHUNK] = low
        return carry

    lax.fori_loop(0, slots // CHUNK, one, 0)


def spread_rows(matrix_ref, pair_ref, out_ref):
    levels = out_ref.shape[1]
    size = 4 * CHUNK

    def one(index, carry):
        base = pl.multiple_of(index * size, size)
        both = mm(matrix_ref[pl.ds(base, size), :], pair_ref[...])
        out_ref[pl.ds(base, size), :] = both[:, :levels] + both[:, levels:]
        return carry

    lax.fori_loop(0, out_ref.shape[0] // size, one, 0)


def fill_pair(profile_ref, forcing, pair_ref):
    obs, levels = profile_ref.shape
    for at in range(0, obs, levels):
        column = jnp.broadcast_to(forcing[:, at : at + levels], (levels, levels)).T
        high, low = halves(profile_ref[at : at + levels, :] * column)
        for base in (at, obs + at):
            pair_ref[base : base + levels, :levels] = high
            pair_ref[base : base + levels, levels:] = low


def spread_kernel(count_ref, innovation_ref, precision_ref, profile_ref, matrix_ref, out_ref, pair_ref):
    forcing = live_precision(count_ref, precision_ref) * innovation_ref[...]
    fill_pair(profile_ref, forcing, pair_ref)
    spread_rows(matrix_ref, pair_ref, out_ref)


def observe(received_ref, matrix_ref, profile_ref, turned_ref, seen_ref):
    slots, levels = received_ref.shape
    obs = profile_ref.shape[0]
    for at in range(0, slots, levels):
        high, low = halves(received_ref[at : at + levels, :].T)
        turned_ref[:levels, at : at + levels] = high
        turned_ref[levels:, at : at + levels] = low
    size = 4 * CHUNK

    def one(index, carry):
        base = pl.multiple_of(index * size, size)
        both = mm(turned_ref[...], matrix_ref[:, pl.ds(base, size)])
        gathered = both[:levels] + both[levels:]
        gathered = gathered + mm(
            turned_ref[:levels], matrix_ref[:, pl.ds(pl.multiple_of(obs + index * size, size), size)]
        )
        seen_ref[:, pl.ds(base, size)] = jnp.sum(
            profile_ref[pl.ds(base, size), :].T * gathered, axis=0, keepdims=True
        )
        return carry

    lax.fori_loop(0, obs // size, one, 0)


def observe_adjoint_kernel(
    count_ref, received_ref, precision_ref, profile_ref, matrix_ref, out_ref, turned_ref, seen_ref, pair_ref,
):
    observe(received_ref, matrix_ref, profile_ref, turned_ref, seen_ref)
    fill_pair(profile_ref, live_precision(count_ref, precision_ref) * seen_ref[...], pair_ref)
    spread_rows(matrix_ref, pair_ref, out_ref)


def observe_norm_kernel(
    count_ref, received_ref, precision_ref, profile_ref, matrix_ref, first_ref, second_ref,
    out_ref, turned_ref, seen_ref,
):
    observe(received_ref, matrix_ref, profile_ref, turned_ref, seen_ref)
    seen = seen_ref[...]
    lane = lax.broadcasted_iota(jnp.int32, out_ref.shape, 1)
    parts = (first_ref[0], second_ref[0], second_ref[1], live_precision(count_ref, precision_ref) * seen * seen)
    row = jnp.zeros(out_ref.shape, f32)
    for k in range(4):
        row = jnp.where(lane == k, jnp.sum(parts[k]), row)
    out_ref[...] = row


def place_kernel(send_ref, arrived_ref, out_ref, pair_ref):
    slots, levels = arrived_ref.shape

    def split(index, carry):
        base = pl.multiple_of(index * CHUNK, CHUNK)
        high, low = halves(arrived_ref[pl.ds(base, CHUNK), :])
        pair_ref[pl.ds(base, CHUNK), :levels] = high
        pair_ref[pl.ds(base, CHUNK), levels:] = low
        return carry

    lax.fori_loop(0, slots // CHUNK, split, 0)
    size = 128

    def one(index, carry):
        base = pl.multiple_of(index * size, size)
        column = base + lax.broadcasted_iota(jnp.int32, (size, slots), 0)
        matrix = jnp.where(column == send_ref[...], 1.0, 0.0).astype(bf16)
        both = mm(matrix, pair_ref[...])
        out_ref[pl.ds(base, size), :] = both[:, :levels] + both[:, levels:]
        return carry

    lax.fori_loop(0, out_ref.shape[0] // size, one, 0)


def strip_kernel(place_ref, cells_ref, one_ref, two_ref, first_ref, second_ref):
    across, along, _ = cells_ref.shape
    odd = place_ref[1]
    head_or_tail = pl.multiple_of((1 - odd) * (along - HALO), HALO)
    tail_or_head = pl.multiple_of(odd * (along - HALO), HALO)
    for target, at in ((first_ref, head_or_tail), (second_ref, tail_or_head)):
        for k, source in enumerate((one_ref, cells_ref, two_ref)):
            target[k * across : (k + 1) * across] = source[:, pl.ds(at, HALO), :]


def fill(place_ref, target, cells_ref, one_ref, two_ref, first_ref, second_ref):
    across, along, _ = cells_ref.shape
    odd_x, odd_y = place_ref[0], place_ref[1]
    above = (1 - odd_x) * (across + HALO)
    below = odd_x * (across + HALO)
    target[HALO : HALO + across, HALO : HALO + along] = cells_ref[...]
    target[pl.ds(above, HALO), HALO : HALO + along] = one_ref[...]
    target[pl.ds(below, HALO), HALO : HALO + along] = two_ref[...]
    for source, at in ((first_ref, 1 - odd_y), (second_ref, odd_y)):
        start = pl.multiple_of(at * (along + HALO), HALO)
        for k, row in enumerate((above, HALO, below)):
            target[pl.ds(row, HALO), pl.ds(start, HALO), :] = source[k * across : (k + 1) * across]


def conduct_kernel(place_ref, cells_ref, one_ref, two_ref, first_ref, second_ref, east_ref, north_ref, field):
    wide, tall, levels = field.shape
    across, along, _ = cells_ref.shape
    fill(place_ref, field, cells_ref, one_ref, two_ref, first_ref, second_ref)
    edges = (place_ref[2] == 0, place_ref[2] == place_ref[4] - 1, place_ref[3] == 0, place_ref[3] == place_ref[5] - 1)

    @pl.when(edges[0])
    def _():
        field[:HALO] = jnp.zeros((HALO, tall, levels), f32)

    @pl.when(edges[1])
    def _():
        field[HALO + across :] = jnp.zeros((HALO, tall, levels), f32)

    @pl.when(edges[2])
    def _():
        field[:, :HALO] = jnp.zeros((wide, HALO, levels), f32)

    @pl.when(edges[3])
    def _():
        field[:, HALO + along :] = jnp.zeros((wide, HALO, levels), f32)

    def one(i, carry):
        here = COUPLING * field[i]
        after = field[jnp.minimum(i + 1, wide - 1)]
        east_ref[i] = here * after
        north_ref[i, : tall - 1] = here[: tall - 1] * field[i, 1:]
        north_ref[i, tall - 1 :] = jnp.zeros((1, levels), f32)
        return carry

    lax.fori_loop(0, wide, one, 0)


def smooth_kernel(place_ref, send_ref, cells_ref, one_ref, two_ref, first_ref, second_ref, east, north, *rest):
    *given, half_ref, full_ref, out_ref, sums_ref, field = rest
    across, along, levels = cells_ref.shape
    wide = across + 2 * HALO
    fill(place_ref, field, cells_ref, one_ref, two_ref, first_ref, second_ref)

    def sweep(k):
        def row(i, carry):
            here, inward = carry
            after = field[i + 1, 1:-1]
            outward = east[i, 1:-1] * (after - here)
            above = north[i, 1:-1] * (field[i, 2:] - here)
            below = north[i, :-2] * (here - field[i, :-2])
            field[i, 1:-1] = here + ((outward - inward) + (above - below))
            return after, outward

        here = field[k, 1:-1]
        lax.fori_loop(k, wide - k, row, (here, east[k - 1, 1:-1] * (here - field[k - 1, 1:-1])))

    def middle():
        return field[HALO : HALO + across, HALO : HALO + along]

    for k in range(1, PASSES + 1):
        sweep(k)
    half = middle()
    half_ref[...] = half
    if given:
        sums_ref[0] = jnp.sum((given[0][...] * half).reshape(-1, 8, levels), axis=0)
        sums_ref[1] = jnp.sum((half * half).reshape(-1, 8, levels), axis=0)
    else:
        sums_ref[0] = jnp.sum((half * half).reshape(-1, 8, levels), axis=0)
    for k in range(PASSES + 1, HALO + 1):
        sweep(k)
    full = middle()
    full_ref[...] = full
    columns = across * along
    pair = jnp.concatenate(halves(full.reshape(columns, levels)), axis=1)

    def gather(index, carry):
        base = pl.multiple_of(index * levels, levels)
        wanted = jnp.broadcast_to(send_ref[:, pl.ds(base, levels)].astype(f32), (levels, levels)).T
        lane = lax.broadcasted_iota(jnp.int32, (levels, levels), 1).astype(f32)
        matrix = jnp.concatenate(
            [jnp.where(wanted == lane + q, 1.0, 0.0).astype(bf16) for q in range(0, columns, levels)],
            axis=1,
        )
        both = mm(matrix, pair)
        out_ref[pl.ds(base, levels), :] = both[:, :levels] + both[:, levels:]
        return carry

    lax.fori_loop(0, out_ref.shape[0] // levels, gather, 0)


def finish_kernel(sums_ref, b_ref, sb_ref, p_ref, sp_ref, control_ref, increment_ref):
    total = jnp.sum(sums_ref[...], axis=0, keepdims=True)
    lane = lax.broadcasted_iota(jnp.int32, total.shape, 1)
    a, c, e, f = [jnp.sum(jnp.where(lane == k, total, 0.0), axis=1, keepdims=True) for k in range(4)]
    slope = c / a
    first = 1.0 / (1.0 + slope)
    rest = e / a - slope * slope
    ratio = first * first * rest
    curved = rest + (f / a - 2.0 * slope * (e / a) + slope * slope * slope)
    second = ratio / (first * first * curved - ratio * ratio * (1.0 + slope))
    of_b = first + second * (ratio + first * slope)
    of_p = -second * first
    control_ref[...] = of_b * b_ref[...] + of_p * p_ref[...]
    increment_ref[...] = of_b * sb_ref[...] + of_p * sp_ref[...]


def swap(cells, axis, odd):
    count = lax.axis_size(axis)
    pairs = [(i, (i + 1) % count) for i in range(odd, count, 2)]
    return lax.ppermute(cells, axis, pairs + [(j, i) for i, j in pairs])


def exchange(rows):
    return lax.all_to_all(rows, ("gx", "gy"), split_axis=0, concat_axis=0, tiled=True)


def params(mib):
    return pltpu.CompilerParams(vmem_limit_bytes=mib * MIB)


def cost(flops, size):
    return pl.CostEstimate(flops=flops, bytes_accessed=size, transcendentals=0)


def on_device(
    length_scale, innovation, observed_precision, profile_weight, stencil_weight, send_rows, stencil_rows, obs_count,
):
    across, along, levels = length_scale.shape
    owners, slot_count = send_rows.shape[1:]
    slots = owners * slot_count
    columns = across * along
    obs = innovation.shape[0]
    send = send_rows.reshape(1, slots)
    innovation = innovation.reshape(1, obs)
    precision = observed_precision.reshape(1, obs)
    at_x, at_y = lax.axis_index("gx"), lax.axis_index("gy")
    sizes = [jnp.int32(lax.axis_size(axis)) for axis in ("gx", "gy")]
    place = jnp.stack([at_x % 2, at_y % 2, at_x, at_y, *sizes]).astype(jnp.int32)

    whole = pl.BlockSpec(memory_space=pltpu.VMEM)
    scalar = pl.BlockSpec(memory_space=pltpu.SMEM)
    afar = pl.BlockSpec(memory_space=pltpu.HBM)
    slot_rows = jax.ShapeDtypeStruct((slots, levels), f32)
    tile = jax.ShapeDtypeStruct((across, along, levels), f32)
    strip = jax.ShapeDtypeStruct((across + 2 * HALO, HALO, levels), f32)
    grown = (across + 2 * HALO, along + 2 * HALO, levels)
    pair_scratch = pltpu.VMEM((2 * obs, 2 * levels), bf16)
    turned_scratch = pltpu.VMEM((2 * levels, slots), bf16)
    seen_scratch = pltpu.VMEM((1, obs), f32)

    def trade(rows):
        return exchange(rows.reshape(owners, slot_count, levels)).reshape(slots, levels)

    def strips(cells, one, two):
        return pl.pallas_call(
            strip_kernel,
            out_shape=(strip, strip),
            in_specs=[scalar] + [whole] * 3,
            out_specs=(whole, whole),
            compiler_params=params(2),
            name="strips",
        )(place, cells, one, two)

    def over_x(cells):
        return swap(cells, "gx", 0), swap(cells, "gx", 1)

    def over_y(first, second):
        return swap(first, "gy", 0), swap(second, "gy", 1)

    scale_x = over_x(length_scale)
    matrix = pl.pallas_call(
        matrix_kernel,
        out_shape=jax.ShapeDtypeStruct((slots, 2 * obs), bf16),
        in_specs=[afar, afar],
        out_specs=whole,
        scratch_shapes=[
            pltpu.VMEM((4, obs), jnp.int32),
            pltpu.VMEM((4, obs), f32),
            pltpu.SemaphoreType.DMA((2,)),
        ],
        compiler_params=params(4),
        cost_estimate=cost(1 << 30, 1 << 24),
        name="matrix",
    )(*(pltpu.with_memory_space_constraint(x, pltpu.HBM) for x in (stencil_rows, stencil_weight)))
    innovation, *scale_x = lax.optimization_barrier((innovation, *scale_x))
    scale_y = over_y(*strips(length_scale, *scale_x))
    spread = pl.pallas_call(
        spread_kernel,
        out_shape=slot_rows,
        in_specs=[scalar] + [whole] * 4,
        out_specs=whole,
        scratch_shapes=[pair_scratch],
        compiler_params=params(14),
        cost_estimate=cost(8 << 30, 1 << 24),
        name="spread",
    )(obs_count, innovation, precision, profile_weight, matrix)
    spread, *scale_y = lax.optimization_barrier((spread, *scale_y))
    conductances = pl.pallas_call(
        conduct_kernel,
        out_shape=(jax.ShapeDtypeStruct(grown, f32),) * 2,
        in_specs=[scalar] + [whole] * 5,
        out_specs=(whole, whole),
        scratch_shapes=[pltpu.VMEM(grown, f32)],
        compiler_params=params(4),
        name="conduct",
    )(place, length_scale, *scale_x, *scale_y)
    spread, send, *conductances = lax.optimization_barrier((spread, send, *conductances))

    def to_columns(arrived):
        return pl.pallas_call(
            place_kernel,
            out_shape=jax.ShapeDtypeStruct((columns, levels), f32),
            in_specs=[whole, whole],
            out_specs=whole,
            scratch_shapes=[pltpu.VMEM((slots, 2 * levels), bf16)],
            compiler_params=params(8),
            name="place",
        )(send, arrived).reshape(across, along, levels)

    def smooth_twice(cells, given):
        aside = over_x(cells)
        count = 1 + len(given)
        return pl.pallas_call(
            smooth_kernel,
            out_shape=(tile, tile, slot_rows, jax.ShapeDtypeStruct((count, 8, levels), f32)),
            in_specs=[scalar] + [whole] * (8 + len(given)),
            out_specs=(whole,) * 4,
            scratch_shapes=[pltpu.VMEM(grown, f32)],
            compiler_params=params(8),
            name="smooth",
        )(place, send, cells, *aside, *over_y(*strips(cells, *aside)), *conductances, *given)

    b, sb, outgoing, first_sums = smooth_twice(to_columns(trade(spread)), ())

    spread = pl.pallas_call(
        observe_adjoint_kernel,
        out_shape=slot_rows,
        in_specs=[scalar] + [whole] * 4,
        out_specs=whole,
        scratch_shapes=[turned_scratch, seen_scratch, pair_scratch],
        compiler_params=params(16),
        name="observe_adjoint",
    )(obs_count, trade(outgoing), precision, profile_weight, matrix)

    p, sp, outgoing, second_sums = smooth_twice(to_columns(trade(spread)), (b,))

    sums = pl.pallas_call(
        observe_norm_kernel,
        out_shape=jax.ShapeDtypeStruct((owners, levels), f32),
        in_specs=[scalar] + [whole] * 6,
        out_specs=whole,
        scratch_shapes=[turned_scratch, seen_scratch],
        compiler_params=params(14),
        name="observe_norm",
    )(obs_count, trade(outgoing), precision, profile_weight, matrix, first_sums, second_sums)

    sums = exchange(sums.reshape(owners, 1, levels)).reshape(owners, levels)

    return pl.pallas_call(
        finish_kernel,
        out_shape=(
            jax.ShapeDtypeStruct((columns, levels), f32),
            jax.ShapeDtypeStruct((columns, levels), f32),
        ),
        in_specs=[whole] * 5,
        out_specs=(whole, whole),
        compiler_params=params(4),
        name="finish",
    )(sums, *(x.reshape(columns, levels) for x in (b, sb, p, sp)))


def solution(mesh):
    def run(*args):
        control, increment = on_device(*args)
        shape = args[0].shape
        return control.reshape(shape), increment.reshape(shape)

    return jax.shard_map(
        run,
        mesh=mesh,
        in_specs=(
            P("gx", "gy", None),
            P(("gx", "gy")),
            P(("gx", "gy")),
            P(("gx", "gy"), None),
            P(None, ("gx", "gy")),
            P(("gx", "gy"), None, None),
            P(None, ("gx", "gy")),
            P(("gx", "gy")),
        ),
        out_specs=(P("gx", "gy", None), P("gx", "gy", None)),
        check_vma=False,
    )
```

time: 259 us -> 200 us (0.77)
  starting transfers between devices: 45.7 us -> 16.4 us
  Pallas kernels: 67.7 us -> 46 us
  local copies, waits for them, and re-layouts: 20.1 us -> 0.99 us
  blocking collectives: 94.8 us -> 109 us
    pallas_call x3 -> x8, Pallas kernels: 50.2 us -> 27.3 us  [the longest x1 9.1 us: on_device(): pl.pallas_call(observe_adjoint_kernel, out_shape=slot_rows, in_specs=[sca...]
    unnamed x27 -> x9, local copies, waits for them, and re-layouts: 19.2 us -> 0.81 us
    ppermute x12, starting transfers between devices: 34.2 us -> 16.4 us  [swap(): return lax.ppermute(cells, axis, pairs + [(j, i) for i, j in pairs])]
    all_to_all x4 -> x5, blocking collectives: 94.8 us -> 109 us  [exchange(): lax.all_to_all(rows, ('gx', 'gy'), split_axis=0, concat_axis=0, tiled=True)]
    all_to_all x1 -> x0, starting transfers between devices: 11.5 us -> none  [exchange(): lax.all_to_all(rows, ('gx', 'gy'), split_axis=0, concat_axis=0, tiled=True)]
  transfers between devices with their start and end apart: 13 -> 12, of which waited for: 7 -> 6; matrix products, arithmetic and copies ran while one was open for 1% -> 0% of each run, Pallas kernels for 1% -> 6%
where the time goes in v2:
time: 200 us; the launch traced here: 199 us
  blocking collectives  109 us (54%)
  Pallas kernels  46 us (23%)
  waiting for transfers between devices  25.9 us (13%)
  starting transfers between devices  16.4 us (8%)
    all_to_all x5, blocking collectives, exchange(): lax.all_to_all(rows, ('gx', 'gy'), split_axis=0, concat_axis=0, tiled=True)  109 us
    ppermute x12, waiting for transfers between devices, swap(): return lax.ppermute(cells, axis, pairs + [(j, i) for i, j in pairs])  25.9 us
    ppermute x12, starting transfers between devices, swap(): return lax.ppermute(cells, axis, pairs + [(j, i) for i, j in pairs])  16.4 us
    pallas_call x2, Pallas kernels, smooth_twice(): pl.pallas_call(smooth_kernel, out_shape=(tile, tile, slot_rows, jax.Shape...  14.9 us
    pallas_call x1, Pallas kernels, on_device(): pl.pallas_call(observe_adjoint_kernel, out_shape=slot_rows, in_specs=[sca...  9.1 us
    pallas_call x1, Pallas kernels, on_device(): pl.pallas_call(matrix_kernel, out_shape=jax.ShapeDtypeStruct((slots, 2 *...  6.28 us
    pallas_call x1, Pallas kernels, on_device(): pl.pallas_call(spread_kernel, out_shape=slot_rows, in_specs=[scalar] + [w...  5.05 us
    pallas_call x1, Pallas kernels, on_device(): pl.pallas_call(observe_norm_kernel, out_shape=jax.ShapeDtypeStruct((owner...  4.19 us
  transfers between devices with their start and end apart: 12, of which 6 were waited for; matrix products, arithmetic and copies ran while one was open for 0% of the time, Pallas kernels for 6%

profile of v2, /device:TPU:1, one launch (start us, length us, event | category | flops | bytes accessed | tf_op | source)
XLA Modules:
  0.0 199.3 jit_solution(693000866539714154)
XLA Ops:
  0.6 0.0 copy-start.1
  0.6 0.0 copy-start.3
  0.7 0.0 copy-start
  0.7 6.9 %collective-permute-start.1 = (f32[8,64,128]{2,1,0:T(8,128)}, f32[8,64,128]{2,1,0:T(8,128)S(1)}, u32[]{:S(2)}, u32[]{:S(2)}) collective-permute-start(f32[8,64,128]{2,1,0:T(8,128)} %cells_ref.3), channel_id=1, source_target_pairs={{8,16},{24,32},{40,48},{56,64},{72,80},{88,96},{104,112},{120,0},{... | collective-permute-start | bytes 786440 | tf_op jit(solution)/shard_map/ppermute | solution.py:299
  7.5 0.0 collective-permute-start
  8.2 0.8 copy.12
  9.0 0.1 reshape.69.send_ref
  9.1 0.1 stack.19.place_ref
  9.2 6.3 %matrix.1.matrix_ref = bf16[2048,4096]{1,0:T(8,128)(2,1)S(1)} custom-call(s32[4,2048]{1,0:T(4,128)} %rows_hbm.1, f32[4,2048]{1,0:T(4,128)} %weights_hbm.1), custom_call_target="tpu_custom_call" | custom-call | flops 1073741824 | bytes 16777216 | tf_op jit(solution)/shard_map/matrix/pallas_call | solution.py:360
  15.5 0.0 collective-permute-done.1.two_ref
  15.5 0.0 collective-permute-done.one_ref
  15.5 0.6 strips.3
  16.1 1.0 collective-permute-start.2
  17.1 1.3 collective-permute-start.3
  18.4 5.1 %spread.1 = f32[2048,128]{1,0:T(8,128)S(1)} custom-call(s32[1]{0:T(128)S(6)} %copy.14.count_ref, f32[1,2048]{1,0:T(1,128)S(1)} %bitcast.51, f32[1,2048]{1,0:T(1,128)S(1)} %bitcast.48, f32[2048,128]{1,0:T(8,128)S(1)} %copy-done, bf16[2048,4096]{1,0:T(8,128)(2,1)S(1)} %matrix.1.matrix_ref), custom_call_target="tpu_custom_call" | custom-call | flops 8589934592 | bytes 16777216 | tf_op jit(solution)/shard_map/spread/pallas_call | solution.py:376
  23.5 0.0 collective-permute-done.2.first_ref
  23.5 0.0 collective-permute-done.3.second_ref
  23.5 0.9 conduct.1
  24.4 25.6 %all_to_all.25 = f32[128,16,128]{2,1,0:T(8,128)S(1)} all-to-all(f32[128,16,128]{2,1,0:T(8,128)S(1)} %bitcast.39), channel_id=1, replica_groups=mesh['gx'=16,'gy'=8] {'gx','gy'}, dimensions={0} | all-to-all | bytes 2097152 | tf_op jit(solution)/shard_map/all_to_all | solution.py:303
  50.1 1.4 place.2
  51.5 1.3 collective-permute-start.5
  52.8 0.0 collective-permute-start.4
  52.8 8.7 %collective-permute-done.5.two_ref = f32[8,64,128]{2,1,0:T(8,128)S(1)} collective-permute-done((f32[8,64,128]{2,1,0:T(8,128)S(1)}, f32[8,64,128]{2,1,0:T(8,128)S(1)}, u32[]{:S(2)}, u32[]{:S(2)}) %collective-permute-start.5) | collective-permute-done | bytes 262176 | tf_op jit(solution)/shard_map/ppermute | solution.py:299
  61.5 0.0 collective-permute-done.4.one_ref
  61.5 0.6 strips.4
  62.0 2.3 %collective-permute-start.6 = (f32[24,8,128]{2,1,0:T(8,128)S(1)}, f32[24,8,128]{2,1,0:T(8,128)S(1)}, u32[]{:S(2)}, u32[]{:S(2)}) collective-permute-start(f32[24,8,128]{2,1,0:T(8,128)S(1)} %get-tuple-element.42), channel_id=1, source_target_pairs={{0,1},{2,3},{4,5},{6,7},{1,0},{3,2},{5,4},{7,6},{8,9},{10,11},{12,... | collective-permute-start | bytes 294920 | tf_op jit(solution)/shard_map/ppermute | solution.py:299
  64.3 0.1 collective-permute-start.7
  64.4 0.9 collective-permute-done.6.first_ref
  65.2 3.4 %collective-permute-done.7.second_ref = f32[24,8,128]{2,1,0:T(8,128)S(1)} collective-permute-done((f32[24,8,128]{2,1,0:T(8,128)S(1)}, f32[24,8,128]{2,1,0:T(8,128)S(1)}, u32[]{:S(2)}, u32[]{:S(2)}) %collective-permute-start.7) | collective-permute-done | bytes 98336 | tf_op jit(solution)/shard_map/ppermute | solution.py:299
  68.6 7.4 %smooth.2 = (f32[8,64,128]{2,1,0:T(8,128)S(1)}, f32[8,64,128]{2,1,0:T(8,128)S(1)}, f32[2048,128]{1,0:T(8,128)S(1)}, f32[1,8,128]{2,1,0:T(8,128)S(1)}) custom-call(s32[6]{0:T(128)S(1)} %stack.19.place_ref, s32[1,2048]{1,0:T(1,128)S(1)} %reshape.69.send_ref, f32[8,64,128]{2,1,0:T(8,128)S(1)} %bitcast.34, f32[8,64,128]{2,1,0:T(8,128)S(1)} %collective-permute-done.4.one_ref, ...), custom_call_target="tpu_custom_call" | custom-call | tf_op jit(solution)/shard_map/smooth/pallas_call | solution.py:412
  76.1 22.8 %all_to_all.26 = f32[128,16,128]{2,1,0:T(8,128)S(1)} all-to-all(f32[128,16,128]{2,1,0:T(8,128)S(1)} %bitcast.41), channel_id=1, replica_groups=mesh['gx'=16,'gy'=8] {'gx','gy'}, dimensions={0} | all-to-all | bytes 2097152 | tf_op jit(solution)/shard_map/all_to_all | solution.py:303
  98.9 9.1 %observe_adjoint.1 = f32[2048,128]{1,0:T(8,128)S(1)} custom-call(s32[1]{0:T(128)S(6)} %copy.14.count_ref, f32[2048,128]{1,0:T(8,128)S(1)} %bitcast.29, f32[1,2048]{1,0:T(1,128)S(1)} %bitcast.49, f32[2048,128]{1,0:T(8,128)S(1)} %copy-done, bf16[2048,4096]{1,0:T(8,128)(2,1)S(1)} %matrix.1.matrix_ref), custom_call_target="tpu_custom_call" | custom-call | tf_op jit(solution)/shard_map/observe_adjoint/pallas_call | solution.py:424
  108.0 23.3 %all_to_all.27 = f32[128,16,128]{2,1,0:T(8,128)S(1)} all-to-all(f32[128,16,128]{2,1,0:T(8,128)S(1)} %bitcast.30), channel_id=1, replica_groups=mesh['gx'=16,'gy'=8] {'gx','gy'}, dimensions={0} | all-to-all | bytes 2097152 | tf_op jit(solution)/shard_map/all_to_all | solution.py:303
  131.3 1.4 place.3
  132.8 1.3 collective-permute-start.9
  134.1 0.0 collective-permute-start.8
  134.1 8.6 %collective-permute-done.9.two_ref = f32[8,64,128]{2,1,0:T(8,128)S(1)} collective-permute-done((f32[8,64,128]{2,1,0:T(8,128)S(1)}, f32[8,64,128]{2,1,0:T(8,128)S(1)}, u32[]{:S(2)}, u32[]{:S(2)}) %collective-permute-start.9) | collective-permute-done | bytes 262176 | tf_op jit(solution)/shard_map/ppermute | solution.py:299
  142.7 0.0 collective-permute-done.8.one_ref
  142.7 0.6 strips.5
  143.3 2.3 %collective-permute-start.10 = (f32[24,8,128]{2,1,0:T(8,128)S(1)}, f32[24,8,128]{2,1,0:T(8,128)S(1)}, u32[]{:S(2)}, u32[]{:S(2)}) collective-permute-start(f32[24,8,128]{2,1,0:T(8,128)S(1)} %get-tuple-element.47), channel_id=1, source_target_pairs={{0,1},{2,3},{4,5},{6,7},{1,0},{3,2},{5,4},{7,6},{8,9},{10,11},{12,... | collective-permute-start | bytes 294920 | tf_op jit(solution)/shard_map/ppermute | solution.py:299
  145.5 0.1 collective-permute-start.11
  145.6 0.9 collective-permute-done.10.first_ref
  146.5 3.4 %collective-permute-done.11.second_ref = f32[24,8,128]{2,1,0:T(8,128)S(1)} collective-permute-done((f32[24,8,128]{2,1,0:T(8,128)S(1)}, f32[24,8,128]{2,1,0:T(8,128)S(1)}, u32[]{:S(2)}, u32[]{:S(2)}) %collective-permute-start.11) | collective-permute-done | bytes 98336 | tf_op jit(solution)/shard_map/ppermute | solution.py:299
  149.9 7.4 %smooth.3 = (f32[8,64,128]{2,1,0:T(8,128)S(1)}, f32[8,64,128]{2,1,0:T(8,128)S(1)}, f32[2048,128]{1,0:T(8,128)S(1)}, f32[2,8,128]{2,1,0:T(8,128)S(1)}) custom-call(s32[6]{0:T(128)S(1)} %stack.19.place_ref, s32[1,2048]{1,0:T(1,128)S(1)} %reshape.69.send_ref, f32[8,64,128]{2,1,0:T(8,128)S(1)} %bitcast.38, f32[8,64,128]{2,1,0:T(8,128)S(1)} %collective-permute-done.8.one_ref, ...), custom_call_target="tpu_custom_call" | custom-call | tf_op jit(solution)/shard_map/smooth/pallas_call | solution.py:412
  157.3 22.8 %all_to_all.28 = f32[128,16,128]{2,1,0:T(8,128)S(1)} all-to-all(f32[128,16,128]{2,1,0:T(8,128)S(1)} %bitcast.40), channel_id=1, replica_groups=mesh['gx'=16,'gy'=8] {'gx','gy'}, dimensions={0} | all-to-all | bytes 2097152 | tf_op jit(solution)/shard_map/all_to_all | solution.py:303
  180.2 4.2 %observe_norm.1 = f32[128,128]{1,0:T(8,128)S(1)} custom-call(s32[1]{0:T(128)S(6)} %copy.14.count_ref, f32[2048,128]{1,0:T(8,128)S(1)} %bitcast.28, f32[1,2048]{1,0:T(1,128)S(1)} %bitcast.50, f32[2048,128]{1,0:T(8,128)S(1)} %copy-done, bf16[2048,4096]{1,0:T(8,128)(2,1)S(1)} %matrix.1.matrix_ref, f32[1,8,128]{2,1,0:T(8,128)S(1)} %get-tuple-element.51.first_ref, ...), custom_call_target="tpu_custom_call" | custom-call | tf_op jit(solution)/shard_map/observe_norm/pallas_call | solution.py:436
  184.4 14.0 %all_to_all.29 = f32[128,1,128]{2,1,0:T(1,128)S(1)} all-to-all(f32[128,1,128]{2,1,0:T(1,128)S(1)} %bitcast.43), channel_id=1, replica_groups=mesh['gx'=16,'gy'=8] {'gx','gy'}, dimensions={0} | all-to-all | bytes 131072 | tf_op jit(solution)/shard_map/all_to_all | solution.py:303
  198.4 1.0 finish.1
  (5 shorter events, 0.0 us)
Async XLA Ops:
  0.6 14.9 %copy-start.1 = (f32[8,64,128]{2,1,0:T(8,128)S(1)}, f32[8,64,128]{2,1,0:T(8,128)}, u32[]{:S(2)}) copy-start(f32[8,64,128]{2,1,0:T(8,128)} %cells_ref.3) | copy-start | bytes 786436
  0.6 17.8 %copy-start.3 = (f32[2048]{0:T(1024)S(1)}, f32[2048]{0:T(1024)}, u32[]{:S(2)}) copy-start(f32[2048]{0:T(1024)} %param.9) | copy-start | bytes 24580
  0.7 17.8 %copy-start = (f32[2048,128]{1,0:T(8,128)S(1)}, f32[2048,128]{1,0:T(8,128)}, u32[]{:S(2)}) copy-start(f32[2048,128]{1,0:T(8,128)} %profile_ref.5) | copy-start | bytes 3145732
  0.7 17.7 %copy-start.2 = (f32[2048]{0:T(1024)S(1)}, f32[2048]{0:T(1024)}, u32[]{:S(2)}) copy-start(f32[2048]{0:T(1024)} %param.10) | copy-start | bytes 24580
  0.7 14.8 %collective-permute-start.1 = (f32[8,64,128]{2,1,0:T(8,128)}, f32[8,64,128]{2,1,0:T(8,128)S(1)}, u32[]{:S(2)}, u32[]{:S(2)}) collective-permute-start(f32[8,64,128]{2,1,0:T(8,128)} %cells_ref.3), channel_id=1, source_target_pairs={{8,16},{24,32},{40,48},{56,64},{72,80},{88,96},{104,112},{120,0},{... | collective-permute-start | bytes 786440 | tf_op jit(solution)/shard_map/ppermute | solution.py:299
  7.5 7.9 %collective-permute-start = (f32[8,64,128]{2,1,0:T(8,128)}, f32[8,64,128]{2,1,0:T(8,128)S(1)}, u32[]{:S(2)}, u32[]{:S(2)}) collective-permute-start(f32[8,64,128]{2,1,0:T(8,128)} %cells_ref.3), channel_id=1, source_target_pairs={{0,8},{16,24},{32,40},{48,56},{64,72},{80,88},{96,104},{112,120},{... | collective-permute-start | bytes 786440 | tf_op jit(solution)/shard_map/ppermute | solution.py:299
  16.1 7.4 %collective-permute-start.2 = (f32[24,8,128]{2,1,0:T(8,128)S(1)}, f32[24,8,128]{2,1,0:T(8,128)S(1)}, u32[]{:S(2)}, u32[]{:S(2)}) collective-permute-start(f32[24,8,128]{2,1,0:T(8,128)S(1)} %get-tuple-element.33), channel_id=1, source_target_pairs={{0,1},{2,3},{4,5},{6,7},{1,0},{3,2},{5,4},{7,6},{8,9},{10,11},{12,... | collective-permute-start | bytes 294920 | tf_op jit(solution)/shard_map/ppermute | solution.py:299
  17.1 6.4 %collective-permute-start.3 = (f32[24,8,128]{2,1,0:T(8,128)S(1)}, f32[24,8,128]{2,1,0:T(8,128)S(1)}, u32[]{:S(2)}, u32[]{:S(2)}) collective-permute-start(f32[24,8,128]{2,1,0:T(8,128)S(1)} %get-tuple-element.34), channel_id=1, source_target_pairs={{1,2},{3,4},{5,6},{7,0},{2,1},{4,3},{6,5},{0,7},{9,10},{11,12},{13... | collective-permute-start | bytes 294920 | tf_op jit(solution)/shard_map/ppermute | solution.py:299
  51.5 9.9 %collective-permute-start.5 = (f32[8,64,128]{2,1,0:T(8,128)S(1)}, f32[8,64,128]{2,1,0:T(8,128)S(1)}, u32[]{:S(2)}, u32[]{:S(2)}) collective-permute-start(f32[8,64,128]{2,1,0:T(8,128)S(1)} %bitcast.31), channel_id=1, source_target_pairs={{8,16},{24,32},{40,48},{56,64},{72,80},{88,96},{104,112},{120,0},{... | collective-permute-start | bytes 786440 | tf_op jit(solution)/shard_map/ppermute | solution.py:299
  52.8 8.7 %collective-permute-start.4 = (f32[8,64,128]{2,1,0:T(8,128)S(1)}, f32[8,64,128]{2,1,0:T(8,128)S(1)}, u32[]{:S(2)}, u32[]{:S(2)}) collective-permute-start(f32[8,64,128]{2,1,0:T(8,128)S(1)} %bitcast.32), channel_id=1, source_target_pairs={{0,8},{16,24},{32,40},{48,56},{64,72},{80,88},{96,104},{112,120},{... | collective-permute-start | bytes 786440 | tf_op jit(solution)/shard_map/ppermute | solution.py:299
  62.0 3.2 %collective-permute-start.6 = (f32[24,8,128]{2,1,0:T(8,128)S(1)}, f32[24,8,128]{2,1,0:T(8,128)S(1)}, u32[]{:S(2)}, u32[]{:S(2)}) collective-permute-start(f32[24,8,128]{2,1,0:T(8,128)S(1)} %get-tuple-element.42), channel_id=1, source_target_pairs={{0,1},{2,3},{4,5},{6,7},{1,0},{3,2},{5,4},{7,6},{8,9},{10,11},{12,... | collective-permute-start | bytes 294920 | tf_op jit(solution)/shard_map/ppermute | solution.py:299
  64.3 4.3 %collective-permute-start.7 = (f32[24,8,128]{2,1,0:T(8,128)S(1)}, f32[24,8,128]{2,1,0:T(8,128)S(1)}, u32[]{:S(2)}, u32[]{:S(2)}) collective-permute-start(f32[24,8,128]{2,1,0:T(8,128)S(1)} %get-tuple-element.43), channel_id=1, source_target_pairs={{1,2},{3,4},{5,6},{7,0},{2,1},{4,3},{6,5},{0,7},{9,10},{11,12},{13... | collective-permute-start | bytes 294920 | tf_op jit(solution)/shard_map/ppermute | solution.py:299
  132.8 9.9 %collective-permute-start.9 = (f32[8,64,128]{2,1,0:T(8,128)S(1)}, f32[8,64,128]{2,1,0:T(8,128)S(1)}, u32[]{:S(2)}, u32[]{:S(2)}) collective-permute-start(f32[8,64,128]{2,1,0:T(8,128)S(1)} %bitcast.35), channel_id=1, source_target_pairs={{8,16},{24,32},{40,48},{56,64},{72,80},{88,96},{104,112},{120,0},{... | collective-permute-start | bytes 786440 | tf_op jit(solution)/shard_map/ppermute | solution.py:299
  134.1 8.7 %collective-permute-start.8 = (f32[8,64,128]{2,1,0:T(8,128)S(1)}, f32[8,64,128]{2,1,0:T(8,128)S(1)}, u32[]{:S(2)}, u32[]{:S(2)}) collective-permute-start(f32[8,64,128]{2,1,0:T(8,128)S(1)} %bitcast.36), channel_id=1, source_target_pairs={{0,8},{16,24},{32,40},{48,56},{64,72},{80,88},{96,104},{112,120},{... | collective-permute-start | bytes 786440 | tf_op jit(solution)/shard_map/ppermute | solution.py:299
  143.3 3.2 %collective-permute-start.10 = (f32[24,8,128]{2,1,0:T(8,128)S(1)}, f32[24,8,128]{2,1,0:T(8,128)S(1)}, u32[]{:S(2)}, u32[]{:S(2)}) collective-permute-start(f32[24,8,128]{2,1,0:T(8,128)S(1)} %get-tuple-element.47), channel_id=1, source_target_pairs={{0,1},{2,3},{4,5},{6,7},{1,0},{3,2},{5,4},{7,6},{8,9},{10,11},{12,... | collective-permute-start | bytes 294920 | tf_op jit(solution)/shard_map/ppermute | solution.py:299
  145.5 4.3 %collective-permute-start.11 = (f32[24,8,128]{2,1,0:T(8,128)S(1)}, f32[24,8,128]{2,1,0:T(8,128)S(1)}, u32[]{:S(2)}, u32[]{:S(2)}) collective-permute-start(f32[24,8,128]{2,1,0:T(8,128)S(1)} %get-tuple-element.48), channel_id=1, source_target_pairs={{1,2},{3,4},{5,6},{7,0},{2,1},{4,3},{6,5},{0,7},{9,10},{11,12},{13... | collective-permute-start | bytes 294920 | tf_op jit(solution)/shard_map/ppermute | solution.py:299

commit v3 on v2

--- a/solution.py
+++ b/solution.py
@@ -143,28 +143,41 @@
     out_ref[...] = row
 
 
-def place_kernel(send_ref, arrived_ref, out_ref, pair_ref):
+def split_pair(arrived_ref, pair_ref):
     slots, levels = arrived_ref.shape
 
-    def split(index, carry):
+    def one(index, carry):
         base = pl.multiple_of(index * CHUNK, CHUNK)
         high, low = halves(arrived_ref[pl.ds(base, CHUNK), :])
         pair_ref[pl.ds(base, CHUNK), :levels] = high
         pair_ref[pl.ds(base, CHUNK), levels:] = low
         return carry
 
-    lax.fori_loop(0, slots // CHUNK, split, 0)
+    lax.fori_loop(0, slots // CHUNK, one, 0)
+
+
+def place_first_kernel(send_ref, arrived_ref, out_ref, matrix_ref, pair_ref):
+    slots, levels = arrived_ref.shape
+    split_pair(arrived_ref, pair_ref)
     size = 128
 
     def one(index, carry):
         base = pl.multiple_of(index * size, size)
         column = base + lax.broadcasted_iota(jnp.int32, (size, slots), 0)
         matrix = jnp.where(column == send_ref[...], 1.0, 0.0).astype(bf16)
+        matrix_ref[pl.ds(base, size), :] = matrix
         both = mm(matrix, pair_ref[...])
         out_ref[pl.ds(base, size), :] = both[:, :levels] + both[:, levels:]
         return carry
 
     lax.fori_loop(0, out_ref.shape[0] // size, one, 0)
+
+
+def place_kernel(matrix_ref, arrived_ref, out_ref, pair_ref):
+    levels = arrived_ref.shape[1]
+    split_pair(arrived_ref, pair_ref)
+    both = mm(matrix_ref[...], pair_ref[...])
+    out_ref[...] = both[:, :levels] + both[:, levels:]
 
 
 def strip_kernel(place_ref, cells_ref, one_ref, two_ref, first_ref, second_ref):
@@ -224,24 +237,39 @@
     lax.fori_loop(0, wide, one, 0)
 
 
-def smooth_kernel(place_ref, send_ref, cells_ref, one_ref, two_ref, first_ref, second_ref, east, north, *rest):
+def select_kernel(send_ref, out_ref):
+    slots, columns = out_ref.shape
+    size = 128
+    lane = lax.broadcasted_iota(jnp.int32, (size, size), 1).astype(f32)
+
+    def one(index, carry):
+        base = pl.multiple_of(index * size, size)
+        wanted = jnp.broadcast_to(send_ref[:, pl.ds(base, size)].astype(f32), (size, size)).T
+        for at in range(0, columns, size):
+            hit = jnp.where(wanted == lane + at, 1.0, 0.0)
+            out_ref[pl.ds(base, size), at : at + size] = hit.astype(bf16)
+        return carry
+
+    lax.fori_loop(0, slots // size, one, 0)
+
+
+def smooth_kernel(place_ref, select_ref, cells_ref, one_ref, two_ref, first_ref, second_ref, east, north, *rest):
     *given, half_ref, full_ref, out_ref, sums_ref, field = rest
     across, along, levels = cells_ref.shape
-    wide = across + 2 * HALO
+    wide, tall = across + 2 * HALO, along + 2 * HALO
     fill(place_ref, field, cells_ref, one_ref, two_ref, first_ref, second_ref)
 
     def sweep(k):
         def row(i, carry):
             here, inward = carry
-            after = field[i + 1, 1:-1]
-            outward = east[i, 1:-1] * (after - here)
-            above = north[i, 1:-1] * (field[i, 2:] - here)
-            below = north[i, :-2] * (here - field[i, :-2])
-            field[i, 1:-1] = here + ((outward - inward) + (above - below))
+            after = field[i + 1]
+            outward = east[i] * (after - here)
+            above = north[i] * (pltpu.roll(here, tall - 1, 0) - here)
+            field[i] = here + ((outward - inward) + (above - pltpu.roll(above, 1, 0)))
             return after, outward
 
-        here = field[k, 1:-1]
-        lax.fori_loop(k, wide - k, row, (here, east[k - 1, 1:-1] * (here - field[k - 1, 1:-1])))
+        here = field[k]
+        lax.fori_loop(k, wide - k, row, (here, east[k - 1] * (here - field[k - 1])), unroll=2)
 
     def middle():
         return field[HALO : HALO + across, HALO : HALO + along]
@@ -262,19 +290,15 @@
     columns = across * along
     pair = jnp.concatenate(halves(full.reshape(columns, levels)), axis=1)
 
+    size = 4 * CHUNK
+
     def gather(index, carry):
-        base = pl.multiple_of(index * levels, levels)
-        wanted = jnp.broadcast_to(send_ref[:, pl.ds(base, levels)].astype(f32), (levels, levels)).T
-        lane = lax.broadcasted_iota(jnp.int32, (levels, levels), 1).astype(f32)
-        matrix = jnp.concatenate(
-            [jnp.where(wanted == lane + q, 1.0, 0.0).astype(bf16) for q in range(0, columns, levels)],
-            axis=1,
-        )
-        both = mm(matrix, pair)
-        out_ref[pl.ds(base, levels), :] = both[:, :levels] + both[:, levels:]
-        return carry
-
-    lax.fori_loop(0, out_ref.shape[0] // levels, gather, 0)
+        base = pl.multiple_of(index * size, size)
+        both = mm(select_ref[pl.ds(base, size), :], pair)
+        out_ref[pl.ds(base, size), :] = both[:, :levels] + both[:, levels:]
+        return carry
+
+    lax.fori_loop(0, out_ref.shape[0] // size, gather, 0)
 
 
 def finish_kernel(sums_ref, b_ref, sb_ref, p_ref, sp_ref, control_ref, increment_ref):
@@ -357,6 +381,7 @@
         return swap(first, "gy", 0), swap(second, "gy", 1)
 
     scale_x = over_x(length_scale)
+    stencil_rows, send, place = lax.optimization_barrier((stencil_rows, send, place))
     matrix = pl.pallas_call(
         matrix_kernel,
         out_shape=jax.ShapeDtypeStruct((slots, 2 * obs), bf16),
@@ -372,7 +397,6 @@
         name="matrix",
     )(*(pltpu.with_memory_space_constraint(x, pltpu.HBM) for x in (stencil_rows, stencil_weight)))
     innovation, *scale_x = lax.optimization_barrier((innovation, *scale_x))
-    scale_y = over_y(*strips(length_scale, *scale_x))
     spread = pl.pallas_call(
         spread_kernel,
         out_shape=slot_rows,
@@ -383,7 +407,28 @@
         cost_estimate=cost(8 << 30, 1 << 24),
         name="spread",
     )(obs_count, innovation, precision, profile_weight, matrix)
-    spread, *scale_y = lax.optimization_barrier((spread, *scale_y))
+    spread, send = lax.optimization_barrier((spread, send))
+    arrived, send, *scale_x = lax.optimization_barrier((trade(spread), send, *scale_x))
+
+    cells, placing = pl.pallas_call(
+        place_first_kernel,
+        out_shape=(jax.ShapeDtypeStruct((columns, levels), f32), jax.ShapeDtypeStruct((columns, slots), bf16)),
+        in_specs=[whole, whole],
+        out_specs=(whole, whole),
+        scratch_shapes=[pltpu.VMEM((slots, 2 * levels), bf16)],
+        compiler_params=params(8),
+        name="place_first",
+    )(send, arrived)
+    selecting = pl.pallas_call(
+        select_kernel,
+        out_shape=jax.ShapeDtypeStruct((slots, columns), bf16),
+        in_specs=[whole],
+        out_specs=whole,
+        compiler_params=params(2),
+        cost_estimate=cost(1 << 28, 1 << 22),
+        name="select",
+    )(send)
+    scale_y = over_y(*strips(length_scale, *scale_x))
     conductances = pl.pallas_call(
         conduct_kernel,
         out_shape=(jax.ShapeDtypeStruct(grown, f32),) * 2,
@@ -391,22 +436,12 @@
         out_specs=(whole, whole),
         scratch_shapes=[pltpu.VMEM(grown, f32)],
         compiler_params=params(4),
+        cost_estimate=cost(1 << 26, 1 << 22),
         name="conduct",
     )(place, length_scale, *scale_x, *scale_y)
-    spread, send, *conductances = lax.optimization_barrier((spread, send, *conductances))
-
-    def to_columns(arrived):
-        return pl.pallas_call(
-            place_kernel,
-            out_shape=jax.ShapeDtypeStruct((columns, levels), f32),
-            in_specs=[whole, whole],
-            out_specs=whole,
-            scratch_shapes=[pltpu.VMEM((slots, 2 * levels), bf16)],
-            compiler_params=params(8),
-            name="place",
-        )(send, arrived).reshape(across, along, levels)
 
     def smooth_twice(cells, given):
+        cells = cells.reshape(across, along, levels)
         aside = over_x(cells)
         count = 1 + len(given)
         return pl.pallas_call(
@@ -415,11 +450,11 @@
             in_specs=[scalar] + [whole] * (8 + len(given)),
             out_specs=(whole,) * 4,
             scratch_shapes=[pltpu.VMEM(grown, f32)],
-            compiler_params=params(8),
+            compiler_params=params(10),
             name="smooth",
-        )(place, send, cells, *aside, *over_y(*strips(cells, *aside)), *conductances, *given)
-
-    b, sb, outgoing, first_sums = smooth_twice(to_columns(trade(spread)), ())
+        )(place, selecting, cells, *aside, *over_y(*strips(cells, *aside)), *conductances, *given)
+
+    b, sb, outgoing, first_sums = smooth_twice(cells, ())
 
     spread = pl.pallas_call(
         observe_adjoint_kernel,
@@ -431,7 +466,16 @@
         name="observe_adjoint",
     )(obs_count, trade(outgoing), precision, profile_weight, matrix)
 
-    p, sp, outgoing, second_sums = smooth_twice(to_columns(trade(spread)), (b,))
+    cells = pl.pallas_call(
+        place_kernel,
+        out_shape=jax.ShapeDtypeStruct((columns, levels), f32),
+        in_specs=[whole, whole],
+        out_specs=whole,
+        scratch_shapes=[pltpu.VMEM((slots, 2 * levels), bf16)],
+        compiler_params=params(8),
+        name="place",
+    )(placing, trade(spread))
+    p, sp, outgoing, second_sums = smooth_twice(cells, (b,))
 
     sums = pl.pallas_call(
         observe_norm_kernel,

time: 200 us -> 190 us (0.950)
  Pallas kernels: 46 us -> 40.4 us
  waiting for transfers between devices: 25.9 us -> 21.2 us
    pallas_call x2, Pallas kernels: 14.9 us -> 8.02 us  [smooth_twice(): pl.pallas_call(smooth_kernel, out_shape=(tile, tile, slot_rows, jax.Shape...]
    ppermute x12, waiting for transfers between devices: 25.9 us -> 21.2 us  [swap(): return lax.ppermute(cells, axis, pairs + [(j, i) for i, j in pairs])]
    pallas_call x2 -> x3, Pallas kernels: 2.88 us -> 4.08 us  [the longest x1 1.69 us: on_device(): pl.pallas_call(select_kernel, out_shape=jax.ShapeDtypeStruct((slots, colu...]
  transfers between devices with their start and end apart: 12 -> 12, of which waited for: 6 -> 5; matrix products, arithmetic and copies ran while one was open for 0% -> 1% of each run, Pallas kernels for 6% -> 5%
where the time goes in v3:
time: 190 us; the launch traced here: 189 us
  blocking collectives  110 us (58%)
  Pallas kernels  40.4 us (21%)
  waiting for transfers between devices  21.2 us (11%)
  starting transfers between devices  15.4 us (8%)
    all_to_all x5, blocking collectives, exchange(): lax.all_to_all(rows, ('gx', 'gy'), split_axis=0, concat_axis=0, tiled=True)  110 us
    ppermute x12, waiting for transfers between devices, swap(): return lax.ppermute(cells, axis, pairs + [(j, i) for i, j in pairs])  21.2 us
    ppermute x12, starting transfers between devices, swap(): return lax.ppermute(cells, axis, pairs + [(j, i) for i, j in pairs])  15.4 us
    pallas_call x1, Pallas kernels, on_device(): pl.pallas_call(observe_adjoint_kernel, out_shape=slot_rows, in_specs=[sca...  9.1 us
    pallas_call x2, Pallas kernels, smooth_twice(): pl.pallas_call(smooth_kernel, out_shape=(tile, tile, slot_rows, jax.Shape...  8.02 us
    pallas_call x1, Pallas kernels, on_device(): pl.pallas_call(matrix_kernel, out_shape=jax.ShapeDtypeStruct((slots, 2 *...  6.37 us
    pallas_call x1, Pallas kernels, on_device(): pl.pallas_call(spread_kernel, out_shape=slot_rows, in_specs=[scalar] + [w...  5.05 us
    pallas_call x1, Pallas kernels, on_device(): pl.pallas_call(observe_norm_kernel, out_shape=jax.ShapeDtypeStruct((owner...  4.19 us
  transfers between devices with their start and end apart: 12, of which 5 were waited for; matrix products, arithmetic and copies ran while one was open for 1% of the time, Pallas kernels for 5%

profile of v3, /device:TPU:1, one launch (start us, length us, event | category | flops | bytes accessed | tf_op | source)
XLA Modules:
  0.0 189.2 jit_solution(12925072020485127126)
XLA Ops:
  0.6 6.9 %collective-permute-start.1 = (f32[8,64,128]{2,1,0:T(8,128)}, f32[8,64,128]{2,1,0:T(8,128)S(1)}, u32[]{:S(2)}, u32[]{:S(2)}) collective-permute-start(f32[8,64,128]{2,1,0:T(8,128)} %cells_ref.3), channel_id=1, source_target_pairs={{8,16},{24,32},{40,48},{56,64},{72,80},{88,96},{104,112},{120,0},{... | collective-permute-start | bytes 786440 | tf_op jit(solution)/shard_map/ppermute | solution.py:323
  7.5 0.0 collective-permute-start
  8.1 0.8 copy.12
  8.9 0.1 reshape.67.send_ref
  9.1 0.1 stack.19.place_ref
  9.1 6.4 %matrix.1.matrix_ref = bf16[2048,4096]{1,0:T(8,128)(2,1)S(1)} custom-call(s32[4,2048]{1,0:T(4,128)} %rows_hbm, f32[4,2048]{1,0:T(4,128)} %weights_hbm.1), custom_call_target="tpu_custom_call" | custom-call | flops 1073741824 | bytes 16777216 | tf_op jit(solution)/shard_map/matrix/pallas_call | solution.py:385
  15.5 0.0 collective-permute-done.1.two_ref
  15.5 0.0 collective-permute-done.one_ref
  15.5 0.0 copy-done
  15.6 5.1 %spread.1 = f32[2048,128]{1,0:T(8,128)S(1)} custom-call(s32[1]{0:T(128)S(6)} %copy.14.count_ref, f32[1,2048]{1,0:T(1,128)S(1)} %bitcast.51, f32[1,2048]{1,0:T(1,128)S(1)} %bitcast.48, f32[2048,128]{1,0:T(8,128)S(1)} %copy-done, bf16[2048,4096]{1,0:T(8,128)(2,1)S(1)} %matrix.1.matrix_ref), custom_call_target="tpu_custom_call" | custom-call | flops 8589934592 | bytes 16777216 | tf_op jit(solution)/shard_map/spread/pallas_call | solution.py:400
  20.6 0.0 copy-start.1
  20.6 26.7 %all_to_all.25 = f32[128,16,128]{2,1,0:T(8,128)S(1)} all-to-all(f32[128,16,128]{2,1,0:T(8,128)S(1)} %bitcast.38), channel_id=1, replica_groups=mesh['gx'=16,'gy'=8] {'gx','gy'}, dimensions={0} | all-to-all | bytes 2097152 | tf_op jit(solution)/shard_map/all_to_all | solution.py:327
  47.3 1.5 place_first.1
  48.8 1.3 collective-permute-start.3
  50.1 0.0 collective-permute-start.2
  50.1 0.6 strips.4
  50.7 1.4 collective-permute-start.6
  52.0 0.0 collective-permute-start.7
  52.0 6.7 %collective-permute-done.3.two_ref = f32[8,64,128]{2,1,0:T(8,128)S(1)} collective-permute-done((f32[8,64,128]{2,1,0:T(8,128)S(1)}, f32[8,64,128]{2,1,0:T(8,128)S(1)}, u32[]{:S(2)}, u32[]{:S(2)}) %collective-permute-start.3) | collective-permute-done | bytes 262176 | tf_op jit(solution)/shard_map/ppermute | solution.py:323
  58.8 0.0 collective-permute-done.2.one_ref
  58.8 0.6 strips.3
  59.3 2.3 %collective-permute-start.4 = (f32[24,8,128]{2,1,0:T(8,128)S(1)}, f32[24,8,128]{2,1,0:T(8,128)S(1)}, u32[]{:S(2)}, u32[]{:S(2)}) collective-permute-start(f32[24,8,128]{2,1,0:T(8,128)S(1)} %get-tuple-element.46), channel_id=1, source_target_pairs={{0,1},{2,3},{4,5},{6,7},{1,0},{3,2},{5,4},{7,6},{8,9},{10,11},{12,... | collective-permute-start | bytes 294920 | tf_op jit(solution)/shard_map/ppermute | solution.py:323
  61.6 0.1 collective-permute-start.5
  61.7 1.7 select.5.select_ref
  63.4 0.0 collective-permute-done.6.first_ref
  63.4 0.0 collective-permute-done.7.second_ref
  63.4 0.9 conduct.1
  64.3 0.0 collective-permute-done.4.first_ref
  64.3 1.6 collective-permute-done.5.second_ref
  65.9 4.0 %smooth.2 = (f32[8,64,128]{2,1,0:T(8,128)S(1)}, f32[8,64,128]{2,1,0:T(8,128)S(1)}, f32[2048,128]{1,0:T(8,128)S(1)}, f32[1,8,128]{2,1,0:T(8,128)S(1)}) custom-call(s32[6]{0:T(128)S(1)} %stack.19.place_ref, bf16[2048,512]{1,0:T(8,128)(2,1)S(1)} %select.5.select_ref, f32[8,64,128]{2,1,0:T(8,128)S(1)} %bitcast.42, ...), custom_call_target="tpu_custom_call" | custom-call | tf_op jit(solution)/shard_map/smooth/pallas_call | solution.py:447
  69.9 22.8 %all_to_all.26 = f32[128,16,128]{2,1,0:T(8,128)S(1)} all-to-all(f32[128,16,128]{2,1,0:T(8,128)S(1)} %bitcast.37), channel_id=1, replica_groups=mesh['gx'=16,'gy'=8] {'gx','gy'}, dimensions={0} | all-to-all | bytes 2097152 | tf_op jit(solution)/shard_map/all_to_all | solution.py:327
  92.8 9.1 %observe_adjoint.1 = f32[2048,128]{1,0:T(8,128)S(1)} custom-call(s32[1]{0:T(128)S(6)} %copy.14.count_ref, f32[2048,128]{1,0:T(8,128)S(1)} %bitcast.29, f32[1,2048]{1,0:T(1,128)S(1)} %bitcast.49, f32[2048,128]{1,0:T(8,128)S(1)} %copy-done, bf16[2048,4096]{1,0:T(8,128)(2,1)S(1)} %matrix.1.matrix_ref), custom_call_target="tpu_custom_call" | custom-call | tf_op jit(solution)/shard_map/observe_adjoint/pallas_call | solution.py:459
  101.9 23.3 %all_to_all.27 = f32[128,16,128]{2,1,0:T(8,128)S(1)} all-to-all(f32[128,16,128]{2,1,0:T(8,128)S(1)} %bitcast.30), channel_id=1, replica_groups=mesh['gx'=16,'gy'=8] {'gx','gy'}, dimensions={0} | all-to-all | bytes 2097152 | tf_op jit(solution)/shard_map/all_to_all | solution.py:327
  125.2 0.9 place.1
  126.1 1.3 collective-permute-start.9
  127.4 0.0 collective-permute-start.8
  127.4 8.7 %collective-permute-done.9.two_ref = f32[8,64,128]{2,1,0:T(8,128)S(1)} collective-permute-done((f32[8,64,128]{2,1,0:T(8,128)S(1)}, f32[8,64,128]{2,1,0:T(8,128)S(1)}, u32[]{:S(2)}, u32[]{:S(2)}) %collective-permute-start.9) | collective-permute-done | bytes 262176 | tf_op jit(solution)/shard_map/ppermute | solution.py:323
  136.0 0.0 collective-permute-done.8.one_ref
  136.1 0.6 strips.5
  136.6 2.3 %collective-permute-start.10 = (f32[24,8,128]{2,1,0:T(8,128)S(1)}, f32[24,8,128]{2,1,0:T(8,128)S(1)}, u32[]{:S(2)}, u32[]{:S(2)}) collective-permute-start(f32[24,8,128]{2,1,0:T(8,128)S(1)} %get-tuple-element.55), channel_id=1, source_target_pairs={{0,1},{2,3},{4,5},{6,7},{1,0},{3,2},{5,4},{7,6},{8,9},{10,11},{12,... | collective-permute-start | bytes 294920 | tf_op jit(solution)/shard_map/ppermute | solution.py:323
  138.9 0.1 collective-permute-start.11
  138.9 0.9 collective-permute-done.10.first_ref
  139.8 3.4 %collective-permute-done.11.second_ref = f32[24,8,128]{2,1,0:T(8,128)S(1)} collective-permute-done((f32[24,8,128]{2,1,0:T(8,128)S(1)}, f32[24,8,128]{2,1,0:T(8,128)S(1)}, u32[]{:S(2)}, u32[]{:S(2)}) %collective-permute-start.11) | collective-permute-done | bytes 98336 | tf_op jit(solution)/shard_map/ppermute | solution.py:323
  143.2 4.0 %smooth.3 = (f32[8,64,128]{2,1,0:T(8,128)S(1)}, f32[8,64,128]{2,1,0:T(8,128)S(1)}, f32[2048,128]{1,0:T(8,128)S(1)}, f32[2,8,128]{2,1,0:T(8,128)S(1)}) custom-call(s32[6]{0:T(128)S(1)} %stack.19.place_ref, bf16[2048,512]{1,0:T(8,128)(2,1)S(1)} %select.5.select_ref, f32[8,64,128]{2,1,0:T(8,128)S(1)} %bitcast.34, ...), custom_call_target="tpu_custom_call" | custom-call | tf_op jit(solution)/shard_map/smooth/pallas_call | solution.py:447
  147.2 22.8 %all_to_all.28 = f32[128,16,128]{2,1,0:T(8,128)S(1)} all-to-all(f32[128,16,128]{2,1,0:T(8,128)S(1)} %bitcast.36), channel_id=1, replica_groups=mesh['gx'=16,'gy'=8] {'gx','gy'}, dimensions={0} | all-to-all | bytes 2097152 | tf_op jit(solution)/shard_map/all_to_all | solution.py:327
  170.1 4.2 %observe_norm.1 = f32[128,128]{1,0:T(8,128)S(1)} custom-call(s32[1]{0:T(128)S(6)} %copy.14.count_ref, f32[2048,128]{1,0:T(8,128)S(1)} %bitcast.28, f32[1,2048]{1,0:T(1,128)S(1)} %bitcast.50, f32[2048,128]{1,0:T(8,128)S(1)} %copy-done, bf16[2048,4096]{1,0:T(8,128)(2,1)S(1)} %matrix.1.matrix_ref, f32[1,8,128]{2,1,0:T(8,128)S(1)} %get-tuple-element.59.first_ref, ...), custom_call_target="tpu_custom_call" | custom-call | tf_op jit(solution)/shard_map/observe_norm/pallas_call | solution.py:480
  174.3 14.0 %all_to_all.29 = f32[128,1,128]{2,1,0:T(1,128)S(1)} all-to-all(f32[128,1,128]{2,1,0:T(1,128)S(1)} %bitcast.43), channel_id=1, replica_groups=mesh['gx'=16,'gy'=8] {'gx','gy'}, dimensions={0} | all-to-all | bytes 131072 | tf_op jit(solution)/shard_map/all_to_all | solution.py:327
  188.3 1.0 finish.1
  (6 shorter events, 0.0 us)
Async XLA Ops:
  0.6 14.9 %collective-permute-start.1 = (f32[8,64,128]{2,1,0:T(8,128)}, f32[8,64,128]{2,1,0:T(8,128)S(1)}, u32[]{:S(2)}, u32[]{:S(2)}) collective-permute-start(f32[8,64,128]{2,1,0:T(8,128)} %cells_ref.3), channel_id=1, source_target_pairs={{8,16},{24,32},{40,48},{56,64},{72,80},{88,96},{104,112},{120,0},{... | collective-permute-start | bytes 786440 | tf_op jit(solution)/shard_map/ppermute | solution.py:323
  7.5 8.0 %collective-permute-start = (f32[8,64,128]{2,1,0:T(8,128)}, f32[8,64,128]{2,1,0:T(8,128)S(1)}, u32[]{:S(2)}, u32[]{:S(2)}) collective-permute-start(f32[8,64,128]{2,1,0:T(8,128)} %cells_ref.3), channel_id=1, source_target_pairs={{0,8},{16,24},{32,40},{48,56},{64,72},{80,88},{96,104},{112,120},{... | collective-permute-start | bytes 786440 | tf_op jit(solution)/shard_map/ppermute | solution.py:323
  9.1 6.4 %copy-start = (f32[2048,128]{1,0:T(8,128)S(1)}, f32[2048,128]{1,0:T(8,128)}, u32[]{:S(2)}) copy-start(f32[2048,128]{1,0:T(8,128)} %profile_ref.5) | copy-start | bytes 3145732
  9.1 6.4 %copy-start.2 = (f32[2048]{0:T(1024)S(1)}, f32[2048]{0:T(1024)}, u32[]{:S(2)}) copy-start(f32[2048]{0:T(1024)} %param.10) | copy-start | bytes 24580
  9.1 6.4 %copy-start.3 = (f32[2048]{0:T(1024)S(1)}, f32[2048]{0:T(1024)}, u32[]{:S(2)}) copy-start(f32[2048]{0:T(1024)} %param.9) | copy-start | bytes 24580
  20.6 29.5 %copy-start.1 = (f32[8,64,128]{2,1,0:T(8,128)S(1)}, f32[8,64,128]{2,1,0:T(8,128)}, u32[]{:S(2)}) copy-start(f32[8,64,128]{2,1,0:T(8,128)} %cells_ref.3) | copy-start | bytes 786436
  48.8 9.9 %collective-permute-start.3 = (f32[8,64,128]{2,1,0:T(8,128)S(1)}, f32[8,64,128]{2,1,0:T(8,128)S(1)}, u32[]{:S(2)}, u32[]{:S(2)}) collective-permute-start(f32[8,64,128]{2,1,0:T(8,128)S(1)} %bitcast.39), channel_id=1, source_target_pairs={{8,16},{24,32},{40,48},{56,64},{72,80},{88,96},{104,112},{120,0},{... | collective-permute-start | bytes 786440 | tf_op jit(solution)/shard_map/ppermute | solution.py:323
  50.1 8.7 %collective-permute-start.2 = (f32[8,64,128]{2,1,0:T(8,128)S(1)}, f32[8,64,128]{2,1,0:T(8,128)S(1)}, u32[]{:S(2)}, u32[]{:S(2)}) collective-permute-start(f32[8,64,128]{2,1,0:T(8,128)S(1)} %bitcast.40), channel_id=1, source_target_pairs={{0,8},{16,24},{32,40},{48,56},{64,72},{80,88},{96,104},{112,120},{... | collective-permute-start | bytes 786440 | tf_op jit(solution)/shard_map/ppermute | solution.py:323
  50.7 12.7 %collective-permute-start.6 = (f32[24,8,128]{2,1,0:T(8,128)S(1)}, f32[24,8,128]{2,1,0:T(8,128)S(1)}, u32[]{:S(2)}, u32[]{:S(2)}) collective-permute-start(f32[24,8,128]{2,1,0:T(8,128)S(1)} %get-tuple-element.50), channel_id=1, source_target_pairs={{0,1},{2,3},{4,5},{6,7},{1,0},{3,2},{5,4},{7,6},{8,9},{10,11},{12,... | collective-permute-start | bytes 294920 | tf_op jit(solution)/shard_map/ppermute | solution.py:323
  52.0 11.3 %collective-permute-start.7 = (f32[24,8,128]{2,1,0:T(8,128)S(1)}, f32[24,8,128]{2,1,0:T(8,128)S(1)}, u32[]{:S(2)}, u32[]{:S(2)}) collective-permute-start(f32[24,8,128]{2,1,0:T(8,128)S(1)} %get-tuple-element.51), channel_id=1, source_target_pairs={{1,2},{3,4},{5,6},{7,0},{2,1},{4,3},{6,5},{0,7},{9,10},{11,12},{13... | collective-permute-start | bytes 294920 | tf_op jit(solution)/shard_map/ppermute | solution.py:323
  59.3 5.0 %collective-permute-start.4 = (f32[24,8,128]{2,1,0:T(8,128)S(1)}, f32[24,8,128]{2,1,0:T(8,128)S(1)}, u32[]{:S(2)}, u32[]{:S(2)}) collective-permute-start(f32[24,8,128]{2,1,0:T(8,128)S(1)} %get-tuple-element.46), channel_id=1, source_target_pairs={{0,1},{2,3},{4,5},{6,7},{1,0},{3,2},{5,4},{7,6},{8,9},{10,11},{12,... | collective-permute-start | bytes 294920 | tf_op jit(solution)/shard_map/ppermute | solution.py:323
  61.6 4.3 %collective-permute-start.5 = (f32[24,8,128]{2,1,0:T(8,128)S(1)}, f32[24,8,128]{2,1,0:T(8,128)S(1)}, u32[]{:S(2)}, u32[]{:S(2)}) collective-permute-start(f32[24,8,128]{2,1,0:T(8,128)S(1)} %get-tuple-element.47), channel_id=1, source_target_pairs={{1,2},{3,4},{5,6},{7,0},{2,1},{4,3},{6,5},{0,7},{9,10},{11,12},{13... | collective-permute-start | bytes 294920 | tf_op jit(solution)/shard_map/ppermute | solution.py:323
  126.1 9.9 %collective-permute-start.9 = (f32[8,64,128]{2,1,0:T(8,128)S(1)}, f32[8,64,128]{2,1,0:T(8,128)S(1)}, u32[]{:S(2)}, u32[]{:S(2)}) collective-permute-start(f32[8,64,128]{2,1,0:T(8,128)S(1)} %bitcast.31), channel_id=1, source_target_pairs={{8,16},{24,32},{40,48},{56,64},{72,80},{88,96},{104,112},{120,0},{... | collective-permute-start | bytes 786440 | tf_op jit(solution)/shard_map/ppermute | solution.py:323
  127.4 8.7 %collective-permute-start.8 = (f32[8,64,128]{2,1,0:T(8,128)S(1)}, f32[8,64,128]{2,1,0:T(8,128)S(1)}, u32[]{:S(2)}, u32[]{:S(2)}) collective-permute-start(f32[8,64,128]{2,1,0:T(8,128)S(1)} %bitcast.32), channel_id=1, source_target_pairs={{0,8},{16,24},{32,40},{48,56},{64,72},{80,88},{96,104},{112,120},{... | collective-permute-start | bytes 786440 | tf_op jit(solution)/shard_map/ppermute | solution.py:323
  136.6 3.2 %collective-permute-start.10 = (f32[24,8,128]{2,1,0:T(8,128)S(1)}, f32[24,8,128]{2,1,0:T(8,128)S(1)}, u32[]{:S(2)}, u32[]{:S(2)}) collective-permute-start(f32[24,8,128]{2,1,0:T(8,128)S(1)} %get-tuple-element.55), channel_id=1, source_target_pairs={{0,1},{2,3},{4,5},{6,7},{1,0},{3,2},{5,4},{7,6},{8,9},{10,11},{12,... | collective-permute-start | bytes 294920 | tf_op jit(solution)/shard_map/ppermute | solution.py:323
  138.9 4.3 %collective-permute-start.11 = (f32[24,8,128]{2,1,0:T(8,128)S(1)}, f32[24,8,128]{2,1,0:T(8,128)S(1)}, u32[]{:S(2)}, u32[]{:S(2)}) collective-permute-start(f32[24,8,128]{2,1,0:T(8,128)S(1)} %get-tuple-element.56), channel_id=1, source_target_pairs={{1,2},{3,4},{5,6},{7,0},{2,1},{4,3},{6,5},{0,7},{9,10},{11,12},{13... | collective-permute-start | bytes 294920 | tf_op jit(solution)/shard_map/ppermute | solution.py:323

commit v4 on v3

--- a/solution.py
+++ b/solution.py
@@ -1,3 +1,5 @@
+import functools
+
 import jax
 import jax.numpy as jnp
 from jax import lax
@@ -29,16 +31,7 @@
     return jnp.where(place < count_ref[0], precision_ref[...], 0.0)
 
 
-def matrix_kernel(rows_hbm, weights_hbm, out_ref, rows_ref, weights_ref, sems):
-    copies = [
-        pltpu.make_async_copy(rows_hbm, rows_ref, sems.at[0]),
-        pltpu.make_async_copy(weights_hbm, weights_ref, sems.at[1]),
-    ]
-    for copy in copies:
-        copy.start()
-    for copy in copies:
-        copy.wait()
-    slots, obs = out_ref.shape[0], rows_ref.shape[1]
+def merge_repeats(rows_ref, weights_ref):
     rows = [rows_ref[k : k + 1, :] for k in range(4)]
     weights = [weights_ref[k : k + 1, :] for k in range(4)]
     for k in range(1, 4):
@@ -46,7 +39,47 @@
             same = rows[k] == rows[j]
             weights[j] = weights[j] + jnp.where(same, weights[k], 0.0)
             weights[k] = jnp.where(same, 0.0, weights[k])
-    parts = [halves(weight) for weight in weights]
+    return rows, [halves(weight) for weight in weights]
+
+
+def flatten_send(send_ref, out_ref):
+    _, slot_count, owners = send_ref.shape
+    lanes = 128
+    group = lanes // slot_count
+    wide = lax.broadcasted_iota(jnp.int32, (slot_count, lanes), 1)
+    tall = lax.broadcasted_iota(jnp.int32, (slot_count, lanes), 0)
+    again = jnp.where(lax.rem(wide, slot_count) == tall, 1.0, 0.0)
+    repeated = jnp.dot(
+        send_ref[0].astype(f32).T, again, precision=lax.Precision.HIGHEST, preferred_element_type=f32
+    )
+    owner = lax.broadcasted_iota(jnp.int32, (owners, lanes), 0)
+    lane = lax.broadcasted_iota(jnp.int32, (owners, lanes), 1)
+    kept = jnp.where(lax.div(lane, slot_count) == lax.rem(owner, group), repeated, 0.0)
+    lines = jnp.sum(kept.reshape(owners // group, group, lanes), axis=1).astype(jnp.int32)
+    for k in range(owners // group):
+        out_ref[:, k * lanes : (k + 1) * lanes] = lines[k : k + 1]
+
+
+def spread_first_kernel(
+    count_ref, rows_hbm, weights_hbm, send_hbm, innovation_hbm, precision_hbm, profile_hbm,
+    matrix_ref, out_ref, flat_ref,
+    rows_ref, weights_ref, send_ref, innovation_ref, precision_ref, profile_ref, pair_ref, sems,
+):
+    moves = (
+        (rows_hbm, rows_ref), (weights_hbm, weights_ref), (send_hbm, send_ref),
+        (innovation_hbm, innovation_ref), (precision_hbm, precision_ref), (profile_hbm, profile_ref),
+    )
+    copies = [pltpu.make_async_copy(*move, sems.at[k]) for k, move in enumerate(moves)]
+    for copy in copies:
+        copy.start()
+    for copy in copies[:5]:
+        copy.wait()
+    flatten_send(send_ref, flat_ref)
+    rows, parts = merge_repeats(rows_ref, weights_ref)
+    forcing = live_precision(count_ref, precision_ref) * innovation_ref[...]
+    copies[5].wait()
+    fill_pair(profile_ref, forcing, pair_ref)
+    slots, obs, levels = matrix_ref.shape[0], rows_ref.shape[1], out_ref.shape[1]
     shape = (CHUNK, CHUNK)
     slot = lax.broadcasted_iota(jnp.int32, shape, 0).astype(f32).astype(bf16)
 
@@ -61,8 +94,10 @@
                 hit = jnp.broadcast_to(near[k][:, cut], shape) == slot
                 high = jnp.where(hit, jnp.broadcast_to(parts[k][0][:, cut], shape), high)
                 low = jnp.where(hit, jnp.broadcast_to(parts[k][1][:, cut], shape), low)
-            out_ref[pl.ds(base, CHUNK), at : at + CHUNK] = high
-            out_ref[pl.ds(base, CHUNK), obs + at : obs + at + CHUNK] = low
+            matrix_ref[pl.ds(base, CHUNK), at : at + CHUNK] = high
+            matrix_ref[pl.ds(base, CHUNK), obs + at : obs + at + CHUNK] = low
+        both = mm(matrix_ref[pl.ds(base, CHUNK), :], pair_ref[...])
+        out_ref[pl.ds(base, CHUNK), :] = both[:, :levels] + both[:, levels:]
         return carry
 
     lax.fori_loop(0, slots // CHUNK, one, 0)
@@ -89,12 +124,6 @@
         for base in (at, obs + at):
             pair_ref[base : base + levels, :levels] = high
             pair_ref[base : base + levels, levels:] = low
-
-
-def spread_kernel(count_ref, innovation_ref, precision_ref, profile_ref, matrix_ref, out_ref, pair_ref):
-    forcing = live_precision(count_ref, precision_ref) * innovation_ref[...]
-    fill_pair(profile_ref, forcing, pair_ref)
-    spread_rows(matrix_ref, pair_ref, out_ref)
 
 
 def observe(received_ref, matrix_ref, profile_ref, turned_ref, seen_ref):
@@ -180,9 +209,13 @@
     out_ref[...] = both[:, :levels] + both[:, levels:]
 
 
-def strip_kernel(place_ref, cells_ref, one_ref, two_ref, first_ref, second_ref):
+def spot(place_ref, sizes):
+    return lax.div(place_ref[0], sizes[1]), lax.rem(place_ref[0], sizes[1])
+
+
+def strip_kernel(sizes, place_ref, cells_ref, one_ref, two_ref, first_ref, second_ref):
     across, along, _ = cells_ref.shape
-    odd = place_ref[1]
+    odd = lax.rem(spot(place_ref, sizes)[1], 2)
     head_or_tail = pl.multiple_of((1 - odd) * (along - HALO), HALO)
     tail_or_head = pl.multiple_of(odd * (along - HALO), HALO)
     for target, at in ((first_ref, head_or_tail), (second_ref, tail_or_head)):
@@ -190,9 +223,9 @@
             target[k * across : (k + 1) * across] = source[:, pl.ds(at, HALO), :]
 
 
-def fill(place_ref, target, cells_ref, one_ref, two_ref, first_ref, second_ref):
+def fill(at_x, at_y, target, cells_ref, one_ref, two_ref, first_ref, second_ref):
     across, along, _ = cells_ref.shape
-    odd_x, odd_y = place_ref[0], place_ref[1]
+    odd_x, odd_y = lax.rem(at_x, 2), lax.rem(at_y, 2)
     above = (1 - odd_x) * (across + HALO)
     below = odd_x * (across + HALO)
     target[HALO : HALO + across, HALO : HALO + along] = cells_ref[...]
@@ -204,11 +237,12 @@
             target[pl.ds(row, HALO), pl.ds(start, HALO), :] = source[k * across : (k + 1) * across]
 
 
-def conduct_kernel(place_ref, cells_ref, one_ref, two_ref, first_ref, second_ref, east_ref, north_ref, field):
+def conduct_kernel(sizes, place_ref, cells_ref, one_ref, two_ref, first_ref, second_ref, east_ref, north_ref, field):
     wide, tall, levels = field.shape
     across, along, _ = cells_ref.shape
-    fill(place_ref, field, cells_ref, one_ref, two_ref, first_ref, second_ref)
-    edges = (place_ref[2] == 0, place_ref[2] == place_ref[4] - 1, place_ref[3] == 0, place_ref[3] == place_ref[5] - 1)
+    at_x, at_y = spot(place_ref, sizes)
+    fill(at_x, at_y, field, cells_ref, one_ref, two_ref, first_ref, second_ref)
+    edges = (at_x == 0, at_x == sizes[0] - 1, at_y == 0, at_y == sizes[1] - 1)
 
     @pl.when(edges[0])
     def _():
@@ -253,11 +287,11 @@
     lax.fori_loop(0, slots // size, one, 0)
 
 
-def smooth_kernel(place_ref, select_ref, cells_ref, one_ref, two_ref, first_ref, second_ref, east, north, *rest):
+def smooth_kernel(sizes, place_ref, select_ref, cells_ref, one_ref, two_ref, first_ref, second_ref, east, north, *rest):
     *given, half_ref, full_ref, out_ref, sums_ref, field = rest
     across, along, levels = cells_ref.shape
     wide, tall = across + 2 * HALO, along + 2 * HALO
-    fill(place_ref, field, cells_ref, one_ref, two_ref, first_ref, second_ref)
+    fill(*spot(place_ref, sizes), field, cells_ref, one_ref, two_ref, first_ref, second_ref)
 
     def sweep(k):
         def row(i, carry):
@@ -343,12 +377,10 @@
     slots = owners * slot_count
     columns = across * along
     obs = innovation.shape[0]
-    send = send_rows.reshape(1, slots)
     innovation = innovation.reshape(1, obs)
     precision = observed_precision.reshape(1, obs)
-    at_x, at_y = lax.axis_index("gx"), lax.axis_index("gy")
-    sizes = [jnp.int32(lax.axis_size(axis)) for axis in ("gx", "gy")]
-    place = jnp.stack([at_x % 2, at_y % 2, at_x, at_y, *sizes]).astype(jnp.int32)
+    sizes = tuple(lax.axis_size(axis) for axis in ("gx", "gy"))
+    place = lax.axis_index(("gx", "gy")).astype(jnp.int32).reshape(1)
 
     whole = pl.BlockSpec(memory_space=pltpu.VMEM)
     scalar = pl.BlockSpec(memory_space=pltpu.SMEM)
@@ -366,7 +398,7 @@
 
     def strips(cells, one, two):
         return pl.pallas_call(
-            strip_kernel,
+            functools.partial(strip_kernel, sizes),
             out_shape=(strip, strip),
             in_specs=[scalar] + [whole] * 3,
             out_specs=(whole, whole),
@@ -381,33 +413,28 @@
         return swap(first, "gy", 0), swap(second, "gy", 1)
 
     scale_x = over_x(length_scale)
-    stencil_rows, send, place = lax.optimization_barrier((stencil_rows, send, place))
-    matrix = pl.pallas_call(
-        matrix_kernel,
-        out_shape=jax.ShapeDtypeStruct((slots, 2 * obs), bf16),
-        in_specs=[afar, afar],
-        out_specs=whole,
+    stencil_rows, place = lax.optimization_barrier((stencil_rows, place))
+    turned = send_rows.transpose(0, 2, 1)
+    given = (stencil_rows, stencil_weight, turned, innovation, precision, profile_weight)
+    matrix, spread, send = pl.pallas_call(
+        spread_first_kernel,
+        out_shape=(
+            jax.ShapeDtypeStruct((slots, 2 * obs), bf16),
+            slot_rows,
+            jax.ShapeDtypeStruct((1, slots), jnp.int32),
+        ),
+        in_specs=[scalar] + [afar] * 6,
+        out_specs=(whole,) * 3,
         scratch_shapes=[
-            pltpu.VMEM((4, obs), jnp.int32),
-            pltpu.VMEM((4, obs), f32),
-            pltpu.SemaphoreType.DMA((2,)),
+            *(pltpu.VMEM(x.shape, x.dtype) for x in given),
+            pair_scratch,
+            pltpu.SemaphoreType.DMA((6,)),
         ],
-        compiler_params=params(4),
-        cost_estimate=cost(1 << 30, 1 << 24),
-        name="matrix",
-    )(*(pltpu.with_memory_space_constraint(x, pltpu.HBM) for x in (stencil_rows, stencil_weight)))
-    innovation, *scale_x = lax.optimization_barrier((innovation, *scale_x))
-    spread = pl.pallas_call(
-        spread_kernel,
-        out_shape=slot_rows,
-        in_specs=[scalar] + [whole] * 4,
-        out_specs=whole,
-        scratch_shapes=[pair_scratch],
         compiler_params=params(14),
         cost_estimate=cost(8 << 30, 1 << 24),
-        name="spread",
-    )(obs_count, innovation, precision, profile_weight, matrix)
-    spread, send = lax.optimization_barrier((spread, send))
+        name="spread_first",
+    )(obs_count, *(pltpu.with_memory_space_constraint(x, pltpu.HBM) for x in given))
+    spread, *scale_x = lax.optimization_barrier((spread, *scale_x))
     arrived, send, *scale_x = lax.optimization_barrier((trade(spread), send, *scale_x))
 
     cells, placing = pl.pallas_call(
@@ -430,7 +457,7 @@
     )(send)
     scale_y = over_y(*strips(length_scale, *scale_x))
     conductances = pl.pallas_call(
-        conduct_kernel,
+        functools.partial(conduct_kernel, sizes),
         out_shape=(jax.ShapeDtypeStruct(grown, f32),) * 2,
         in_specs=[scalar] + [whole] * 5,
         out_specs=(whole, whole),
@@ -445,7 +472,7 @@
         aside = over_x(cells)
         count = 1 + len(given)
         return pl.pallas_call(
-            smooth_kernel,
+            functools.partial(smooth_kernel, sizes),
             out_shape=(tile, tile, slot_rows, jax.ShapeDtypeStruct((count, 8, levels), f32)),
             in_specs=[scalar] + [whole] * (8 + len(given)),
             out_specs=(whole,) * 4,

time: 190 us -> 182 us (0.958)
  Pallas kernels: 40.4 us -> 33.2 us
    pallas_call x8 -> x7, Pallas kernels: 22.1 us -> 14.8 us  [the longest x1 7.64 us: on_device(): pl.pallas_call(spread_first_kernel, out_shape=(jax.ShapeDtypeStruct((slot...]
  transfers between devices with their start and end apart: 12 -> 12, of which waited for: 5 -> 5; matrix products, arithmetic and copies ran while one was open for 1% -> 0% of each run, Pallas kernels for 5% -> 5%
where the time goes in v4:
time: 182 us
  blocking collectives  109 us (60%)
  Pallas kernels  33.2 us (18%)
  waiting for transfers between devices  22.3 us (12%)
  starting transfers between devices  15.6 us (9%)
    all_to_all x5, blocking collectives, exchange(): lax.all_to_all(rows, ('gx', 'gy'), split_axis=0, concat_axis=0, tiled=True)  109 us
    ppermute x12, waiting for transfers between devices, swap(): return lax.ppermute(cells, axis, pairs + [(j, i) for i, j in pairs])  22.3 us
    ppermute x12, starting transfers between devices, swap(): return lax.ppermute(cells, axis, pairs + [(j, i) for i, j in pairs])  15.6 us
    pallas_call x1, Pallas kernels, on_device(): pl.pallas_call(observe_adjoint_kernel, out_shape=slot_rows, in_specs=[sca...  9.12 us
    pallas_call x1, Pallas kernels, on_device(): pl.pallas_call(spread_first_kernel, out_shape=(jax.ShapeDtypeStruct((slot...  7.64 us
    pallas_call x2, Pallas kernels, smooth_twice(): pl.pallas_call(functools.partial(smooth_kernel, sizes), out_shape=(tile,...  6.65 us
    pallas_call x1, Pallas kernels, on_device(): pl.pallas_call(observe_norm_kernel, out_shape=jax.ShapeDtypeStruct((owner...  4.21 us
  transfers between devices with their start and end apart: 12, of which 5 were waited for; matrix products, arithmetic and copies ran while one was open for 0% of the time, Pallas kernels for 5%

profile of v4, /device:TPU:1, one launch (start us, length us, event | category | flops | bytes accessed | tf_op | source)
XLA Modules:
  0.0 182.1 jit_solution(6773733057412962968)
XLA Ops:
  0.6 6.9 %collective-permute-start.1 = (f32[8,64,128]{2,1,0:T(8,128)}, f32[8,64,128]{2,1,0:T(8,128)S(1)}, u32[]{:S(2)}, u32[]{:S(2)}) collective-permute-start(f32[8,64,128]{2,1,0:T(8,128)} %cells_ref.3), channel_id=1, source_target_pairs={{8,16},{24,32},{40,48},{56,64},{72,80},{88,96},{104,112},{120,0},{... | collective-permute-start | bytes 786440 | tf_op jit(solution)/shard_map/ppermute | solution.py:357
  7.5 0.0 collective-permute-start
  8.1 7.6 %spread_first.1 = (bf16[2048,4096]{1,0:T(8,128)(2,1)S(1)}, f32[2048,128]{1,0:T(8,128)S(1)}, s32[1,2048]{1,0:T(1,128)S(1)}) custom-call(s32[1]{0:T(128)S(6)} %copy.11.count_ref, s32[4,2048]{1,0:T(4,128)} %rows_hbm, f32[4,2048]{1,0:T(4,128)} %weights_hbm.1, s32[1,16,128]{2,1,0:T(8,128)} %bitcast.51, f32[1,2048]{1,0:T(1,128)} %bitcast.52, f32[1,2048]{1,0:T(1,128)} %bitcast.46, ...), custom_call_target="tpu_custom_call" | custom-call | flops 8589934592 | bytes 16777216 | tf_op jit(solution)/shard_map/spread_first/pallas_call | solution.py:419
  15.8 0.0 copy-start.1
  15.8 0.0 collective-permute-done.1.two_ref
  15.8 0.0 collective-permute-done.one_ref
  15.8 26.4 %all_to_all.25 = f32[128,16,128]{2,1,0:T(8,128)S(1)} all-to-all(f32[128,16,128]{2,1,0:T(8,128)S(1)} %bitcast.35), channel_id=1, replica_groups=mesh['gx'=16,'gy'=8] {'gx','gy'}, dimensions={0} | all-to-all | bytes 2097152 | tf_op jit(solution)/shard_map/all_to_all | solution.py:361
  42.2 1.5 place_first.1
  43.7 1.3 collective-permute-start.3
  45.0 0.0 collective-permute-start.2
  45.0 0.0 copy-done.1
  45.0 1.4 collective-permute-start.6
  46.4 0.0 collective-permute-start.7
  46.4 7.3 %collective-permute-done.3.two_ref = f32[8,64,128]{2,1,0:T(8,128)S(1)} collective-permute-done((f32[8,64,128]{2,1,0:T(8,128)S(1)}, f32[8,64,128]{2,1,0:T(8,128)S(1)}, u32[]{:S(2)}, u32[]{:S(2)}) %collective-permute-start.3) | collective-permute-done | bytes 262176 | tf_op jit(solution)/shard_map/ppermute | solution.py:357
  53.7 0.0 collective-permute-done.2.one_ref
  53.7 2.3 %collective-permute-start.4 = (f32[24,8,128]{2,1,0:T(8,128)S(1)}, f32[24,8,128]{2,1,0:T(8,128)S(1)}, u32[]{:S(2)}, u32[]{:S(2)}) collective-permute-start(f32[24,8,128]{2,1,0:T(8,128)S(1)} %get-tuple-element.45), channel_id=1, source_target_pairs={{0,1},{2,3},{4,5},{6,7},{1,0},{3,2},{5,4},{7,6},{8,9},{10,11},{12,... | collective-permute-start | bytes 294920 | tf_op jit(solution)/shard_map/ppermute | solution.py:357
  55.9 0.1 collective-permute-start.5
  56.0 1.7 select.1.select_ref
  57.7 0.0 collective-permute-done.6.first_ref
  57.7 0.0 collective-permute-done.7.second_ref
  57.7 0.4 conduct.1
  58.2 0.0 collective-permute-done.4.first_ref
  58.2 2.1 %collective-permute-done.5.second_ref = f32[24,8,128]{2,1,0:T(8,128)S(1)} collective-permute-done((f32[24,8,128]{2,1,0:T(8,128)S(1)}, f32[24,8,128]{2,1,0:T(8,128)S(1)}, u32[]{:S(2)}, u32[]{:S(2)}) %collective-permute-start.5) | collective-permute-done | bytes 98336 | tf_op jit(solution)/shard_map/ppermute | solution.py:357
  60.3 3.3 %smooth.2 = (f32[8,64,128]{2,1,0:T(8,128)S(1)}, f32[8,64,128]{2,1,0:T(8,128)S(1)}, f32[2048,128]{1,0:T(8,128)S(1)}, f32[1,8,128]{2,1,0:T(8,128)S(1)}) custom-call(s32[1]{0:T(128)} %bitcast.place_ref, bf16[2048,512]{1,0:T(8,128)(2,1)S(1)} %select.1.select_ref, f32[8,64,128]{2,1,0:T(8,128)S(1)} %bitcast.40, f32[8,64,128]{2,1,0:T(8,128)S(1)} %collective-permute-done.2.one_ref, ...), custom_call_target="tpu_custom_call" | custom-call | tf_op jit(solution)/shard_map/smooth/pallas_call | solution.py:474
  63.6 0.0 copy-start
  63.6 0.0 copy-start.2
  63.6 23.0 %all_to_all.26 = f32[128,16,128]{2,1,0:T(8,128)S(1)} all-to-all(f32[128,16,128]{2,1,0:T(8,128)S(1)} %bitcast.36), channel_id=1, replica_groups=mesh['gx'=16,'gy'=8] {'gx','gy'}, dimensions={0} | all-to-all | bytes 2097152 | tf_op jit(solution)/shard_map/all_to_all | solution.py:361
  86.6 0.0 copy-done
  86.6 0.0 copy-done.2
  86.6 9.1 %observe_adjoint.1 = f32[2048,128]{1,0:T(8,128)S(1)} custom-call(s32[1]{0:T(128)S(6)} %copy.11.count_ref, f32[2048,128]{1,0:T(8,128)S(1)} %bitcast.27, f32[1,2048]{1,0:T(1,128)S(1)} %bitcast.47, f32[2048,128]{1,0:T(8,128)S(1)} %copy-done, bf16[2048,4096]{1,0:T(8,128)(2,1)S(1)} %get-tuple-element.54.matrix_ref), custom_call_target="tpu_custom_call" | custom-call | tf_op jit(solution)/shard_map/observe_adjoint/pallas_call | solution.py:486
  95.7 23.3 %all_to_all.27 = f32[128,16,128]{2,1,0:T(8,128)S(1)} all-to-all(f32[128,16,128]{2,1,0:T(8,128)S(1)} %bitcast.28), channel_id=1, replica_groups=mesh['gx'=16,'gy'=8] {'gx','gy'}, dimensions={0} | all-to-all | bytes 2097152 | tf_op jit(solution)/shard_map/all_to_all | solution.py:361
  119.0 0.9 place.1
  119.9 1.3 collective-permute-start.9
  121.2 0.0 collective-permute-start.8
  121.2 8.7 %collective-permute-done.9.two_ref = f32[8,64,128]{2,1,0:T(8,128)S(1)} collective-permute-done((f32[8,64,128]{2,1,0:T(8,128)S(1)}, f32[8,64,128]{2,1,0:T(8,128)S(1)}, u32[]{:S(2)}, u32[]{:S(2)}) %collective-permute-start.9) | collective-permute-done | bytes 262176 | tf_op jit(solution)/shard_map/ppermute | solution.py:357
  129.9 0.0 collective-permute-done.8.one_ref
  129.9 2.4 %collective-permute-start.10 = (f32[24,8,128]{2,1,0:T(8,128)S(1)}, f32[24,8,128]{2,1,0:T(8,128)S(1)}, u32[]{:S(2)}, u32[]{:S(2)}) collective-permute-start(f32[24,8,128]{2,1,0:T(8,128)S(1)} %get-tuple-element.55), channel_id=1, source_target_pairs={{0,1},{2,3},{4,5},{6,7},{1,0},{3,2},{5,4},{7,6},{8,9},{10,11},{12,... | collective-permute-start | bytes 294920 | tf_op jit(solution)/shard_map/ppermute | solution.py:357
  132.4 0.1 collective-permute-start.11
  132.4 0.9 collective-permute-done.10.first_ref
  133.3 3.4 %collective-permute-done.11.second_ref = f32[24,8,128]{2,1,0:T(8,128)S(1)} collective-permute-done((f32[24,8,128]{2,1,0:T(8,128)S(1)}, f32[24,8,128]{2,1,0:T(8,128)S(1)}, u32[]{:S(2)}, u32[]{:S(2)}) %collective-permute-start.11) | collective-permute-done | bytes 98336 | tf_op jit(solution)/shard_map/ppermute | solution.py:357
  136.7 3.3 %smooth.3 = (f32[8,64,128]{2,1,0:T(8,128)S(1)}, f32[8,64,128]{2,1,0:T(8,128)S(1)}, f32[2048,128]{1,0:T(8,128)S(1)}, f32[2,8,128]{2,1,0:T(8,128)S(1)}) custom-call(s32[1]{0:T(128)} %bitcast.place_ref, bf16[2048,512]{1,0:T(8,128)(2,1)S(1)} %select.1.select_ref, f32[8,64,128]{2,1,0:T(8,128)S(1)} %bitcast.32, f32[8,64,128]{2,1,0:T(8,128)S(1)} %collective-permute-done.8.one_ref, ...), custom_call_target="tpu_custom_call" | custom-call | tf_op jit(solution)/shard_map/smooth/pallas_call | solution.py:474
  140.0 22.8 %all_to_all.28 = f32[128,16,128]{2,1,0:T(8,128)S(1)} all-to-all(f32[128,16,128]{2,1,0:T(8,128)S(1)} %bitcast.34), channel_id=1, replica_groups=mesh['gx'=16,'gy'=8] {'gx','gy'}, dimensions={0} | all-to-all | bytes 2097152 | tf_op jit(solution)/shard_map/all_to_all | solution.py:361
  162.9 4.2 %observe_norm.1 = f32[128,128]{1,0:T(8,128)S(1)} custom-call(s32[1]{0:T(128)S(6)} %copy.11.count_ref, f32[2048,128]{1,0:T(8,128)S(1)} %bitcast.26, f32[1,2048]{1,0:T(1,128)S(1)} %bitcast.48, f32[2048,128]{1,0:T(8,128)S(1)} %copy-done, bf16[2048,4096]{1,0:T(8,128)(2,1)S(1)} %get-tuple-element.54.matrix_ref, f32[1,8,128]{2,1,0:T(8,128)S(1)} %get-tuple-element.59.first_ref, ...), custom_call_target="tpu_custom_call" | custom-call | tf_op jit(solution)/shard_map/observe_norm/pallas_call | solution.py:507
  167.1 14.0 %all_to_all.29 = f32[128,1,128]{2,1,0:T(1,128)S(1)} all-to-all(f32[128,1,128]{2,1,0:T(1,128)S(1)} %bitcast.41), channel_id=1, replica_groups=mesh['gx'=16,'gy'=8] {'gx','gy'}, dimensions={0} | all-to-all | bytes 131072 | tf_op jit(solution)/shard_map/all_to_all | solution.py:361
  181.1 1.0 finish.1
  (3 shorter events, 0.1 us)
Async XLA Ops:
  0.6 15.2 %collective-permute-start.1 = (f32[8,64,128]{2,1,0:T(8,128)}, f32[8,64,128]{2,1,0:T(8,128)S(1)}, u32[]{:S(2)}, u32[]{:S(2)}) collective-permute-start(f32[8,64,128]{2,1,0:T(8,128)} %cells_ref.3), channel_id=1, source_target_pairs={{8,16},{24,32},{40,48},{56,64},{72,80},{88,96},{104,112},{120,0},{... | collective-permute-start | bytes 786440 | tf_op jit(solution)/shard_map/ppermute | solution.py:357
  7.5 8.3 %collective-permute-start = (f32[8,64,128]{2,1,0:T(8,128)}, f32[8,64,128]{2,1,0:T(8,128)S(1)}, u32[]{:S(2)}, u32[]{:S(2)}) collective-permute-start(f32[8,64,128]{2,1,0:T(8,128)} %cells_ref.3), channel_id=1, source_target_pairs={{0,8},{16,24},{32,40},{48,56},{64,72},{80,88},{96,104},{112,120},{... | collective-permute-start | bytes 786440 | tf_op jit(solution)/shard_map/ppermute | solution.py:357
  15.8 29.2 %copy-start.1 = (f32[8,64,128]{2,1,0:T(8,128)S(1)}, f32[8,64,128]{2,1,0:T(8,128)}, u32[]{:S(2)}) copy-start(f32[8,64,128]{2,1,0:T(8,128)} %cells_ref.3) | copy-start | bytes 786436
  43.7 9.9 %collective-permute-start.3 = (f32[8,64,128]{2,1,0:T(8,128)S(1)}, f32[8,64,128]{2,1,0:T(8,128)S(1)}, u32[]{:S(2)}, u32[]{:S(2)}) collective-permute-start(f32[8,64,128]{2,1,0:T(8,128)S(1)} %bitcast.37), channel_id=1, source_target_pairs={{8,16},{24,32},{40,48},{56,64},{72,80},{88,96},{104,112},{120,0},{... | collective-permute-start | bytes 786440 | tf_op jit(solution)/shard_map/ppermute | solution.py:357
  45.0 8.7 %collective-permute-start.2 = (f32[8,64,128]{2,1,0:T(8,128)S(1)}, f32[8,64,128]{2,1,0:T(8,128)S(1)}, u32[]{:S(2)}, u32[]{:S(2)}) collective-permute-start(f32[8,64,128]{2,1,0:T(8,128)S(1)} %bitcast.38), channel_id=1, source_target_pairs={{0,8},{16,24},{32,40},{48,56},{64,72},{80,88},{96,104},{112,120},{... | collective-permute-start | bytes 786440 | tf_op jit(solution)/shard_map/ppermute | solution.py:357
  45.0 12.7 %collective-permute-start.6 = (f32[24,8,128]{2,1,0:T(8,128)S(1)}, f32[24,8,128]{2,1,0:T(8,128)S(1)}, u32[]{:S(2)}, u32[]{:S(2)}) collective-permute-start(f32[24,8,128]{2,1,0:T(8,128)S(1)} %get-tuple-element.49), channel_id=1, source_target_pairs={{0,1},{2,3},{4,5},{6,7},{1,0},{3,2},{5,4},{7,6},{8,9},{10,11},{12,... | collective-permute-start | bytes 294920 | tf_op jit(solution)/shard_map/ppermute | solution.py:357
  46.4 11.3 %collective-permute-start.7 = (f32[24,8,128]{2,1,0:T(8,128)S(1)}, f32[24,8,128]{2,1,0:T(8,128)S(1)}, u32[]{:S(2)}, u32[]{:S(2)}) collective-permute-start(f32[24,8,128]{2,1,0:T(8,128)S(1)} %get-tuple-element.50), channel_id=1, source_target_pairs={{1,2},{3,4},{5,6},{7,0},{2,1},{4,3},{6,5},{0,7},{9,10},{11,12},{13... | collective-permute-start | bytes 294920 | tf_op jit(solution)/shard_map/ppermute | solution.py:357
  53.7 4.5 %collective-permute-start.4 = (f32[24,8,128]{2,1,0:T(8,128)S(1)}, f32[24,8,128]{2,1,0:T(8,128)S(1)}, u32[]{:S(2)}, u32[]{:S(2)}) collective-permute-start(f32[24,8,128]{2,1,0:T(8,128)S(1)} %get-tuple-element.45), channel_id=1, source_target_pairs={{0,1},{2,3},{4,5},{6,7},{1,0},{3,2},{5,4},{7,6},{8,9},{10,11},{12,... | collective-permute-start | bytes 294920 | tf_op jit(solution)/shard_map/ppermute | solution.py:357
  55.9 4.3 %collective-permute-start.5 = (f32[24,8,128]{2,1,0:T(8,128)S(1)}, f32[24,8,128]{2,1,0:T(8,128)S(1)}, u32[]{:S(2)}, u32[]{:S(2)}) collective-permute-start(f32[24,8,128]{2,1,0:T(8,128)S(1)} %get-tuple-element.46), channel_id=1, source_target_pairs={{1,2},{3,4},{5,6},{7,0},{2,1},{4,3},{6,5},{0,7},{9,10},{11,12},{13... | collective-permute-start | bytes 294920 | tf_op jit(solution)/shard_map/ppermute | solution.py:357
  63.6 23.0 %copy-start = (f32[2048,128]{1,0:T(8,128)S(1)}, f32[2048,128]{1,0:T(8,128)}, u32[]{:S(2)}) copy-start(f32[2048,128]{1,0:T(8,128)} %profile_ref.3) | copy-start | bytes 3145732
  63.6 23.0 %copy-start.2 = (f32[2048]{0:T(1024)S(1)}, f32[2048]{0:T(1024)}, u32[]{:S(2)}) copy-start(f32[2048]{0:T(1024)} %param.10) | copy-start | bytes 24580
  119.9 9.9 %collective-permute-start.9 = (f32[8,64,128]{2,1,0:T(8,128)S(1)}, f32[8,64,128]{2,1,0:T(8,128)S(1)}, u32[]{:S(2)}, u32[]{:S(2)}) collective-permute-start(f32[8,64,128]{2,1,0:T(8,128)S(1)} %bitcast.29), channel_id=1, source_target_pairs={{8,16},{24,32},{40,48},{56,64},{72,80},{88,96},{104,112},{120,0},{... | collective-permute-start | bytes 786440 | tf_op jit(solution)/shard_map/ppermute | solution.py:357
  121.2 8.7 %collective-permute-start.8 = (f32[8,64,128]{2,1,0:T(8,128)S(1)}, f32[8,64,128]{2,1,0:T(8,128)S(1)}, u32[]{:S(2)}, u32[]{:S(2)}) collective-permute-start(f32[8,64,128]{2,1,0:T(8,128)S(1)} %bitcast.30), channel_id=1, source_target_pairs={{0,8},{16,24},{32,40},{48,56},{64,72},{80,88},{96,104},{112,120},{... | collective-permute-start | bytes 786440 | tf_op jit(solution)/shard_map/ppermute | solution.py:357
  129.9 3.4 %collective-permute-start.10 = (f32[24,8,128]{2,1,0:T(8,128)S(1)}, f32[24,8,128]{2,1,0:T(8,128)S(1)}, u32[]{:S(2)}, u32[]{:S(2)}) collective-permute-start(f32[24,8,128]{2,1,0:T(8,128)S(1)} %get-tuple-element.55), channel_id=1, source_target_pairs={{0,1},{2,3},{4,5},{6,7},{1,0},{3,2},{5,4},{7,6},{8,9},{10,11},{12,... | collective-permute-start | bytes 294920 | tf_op jit(solution)/shard_map/ppermute | solution.py:357
  132.4 4.3 %collective-permute-start.11 = (f32[24,8,128]{2,1,0:T(8,128)S(1)}, f32[24,8,128]{2,1,0:T(8,128)S(1)}, u32[]{:S(2)}, u32[]{:S(2)}) collective-permute-start(f32[24,8,128]{2,1,0:T(8,128)S(1)} %get-tuple-element.56), channel_id=1, source_target_pairs={{1,2},{3,4},{5,6},{7,0},{2,1},{4,3},{6,5},{0,7},{9,10},{11,12},{13... | collective-permute-start | bytes 294920 | tf_op jit(solution)/shard_map/ppermute | solution.py:357

commit v5 on v4

--- a/solution.py
+++ b/solution.py
@@ -104,16 +104,11 @@
 
 
 def spread_rows(matrix_ref, pair_ref, out_ref):
-    levels = out_ref.shape[1]
-    size = 4 * CHUNK
-
-    def one(index, carry):
-        base = pl.multiple_of(index * size, size)
-        both = mm(matrix_ref[pl.ds(base, size), :], pair_ref[...])
-        out_ref[pl.ds(base, size), :] = both[:, :levels] + both[:, levels:]
-        return carry
-
-    lax.fori_loop(0, out_ref.shape[0] // size, one, 0)
+    slots, levels = out_ref.shape
+    size = slots // 2
+    for base in range(0, slots, size):
+        both = mm(matrix_ref[base : base + size, :], pair_ref[...])
+        out_ref[base : base + size, :] = both[:, :levels] + both[:, levels:]
 
 
 def fill_pair(profile_ref, forcing, pair_ref):
@@ -133,21 +128,14 @@
         high, low = halves(received_ref[at : at + levels, :].T)
         turned_ref[:levels, at : at + levels] = high
         turned_ref[levels:, at : at + levels] = low
-    size = 4 * CHUNK
-
-    def one(index, carry):
-        base = pl.multiple_of(index * size, size)
-        both = mm(turned_ref[...], matrix_ref[:, pl.ds(base, size)])
+    size = obs // 2
+    for base in range(0, obs, size):
+        both = mm(turned_ref[...], matrix_ref[:, base : base + size])
         gathered = both[:levels] + both[levels:]
-        gathered = gathered + mm(
-            turned_ref[:levels], matrix_ref[:, pl.ds(pl.multiple_of(obs + index * size, size), size)]
+        gathered = gathered + mm(turned_ref[:levels], matrix_ref[:, obs + base : obs + base + size])
+        seen_ref[:, base : base + size] = jnp.sum(
+            profile_ref[base : base + size, :].T * gathered, axis=0, keepdims=True
         )
-        seen_ref[:, pl.ds(base, size)] = jnp.sum(
-            profile_ref[pl.ds(base, size), :].T * gathered, axis=0, keepdims=True
-        )
-        return carry
-
-    lax.fori_loop(0, obs // size, one, 0)
 
 
 def observe_adjoint_kernel(
@@ -174,32 +162,26 @@
 
 def split_pair(arrived_ref, pair_ref):
     slots, levels = arrived_ref.shape
-
-    def one(index, carry):
-        base = pl.multiple_of(index * CHUNK, CHUNK)
-        high, low = halves(arrived_ref[pl.ds(base, CHUNK), :])
-        pair_ref[pl.ds(base, CHUNK), :levels] = high
-        pair_ref[pl.ds(base, CHUNK), levels:] = low
-        return carry
-
-    lax.fori_loop(0, slots // CHUNK, one, 0)
+    for base in range(0, slots, CHUNK):
+        high, low = halves(arrived_ref[base : base + CHUNK, :])
+        pair_ref[base : base + CHUNK, :levels] = high
+        pair_ref[base : base + CHUNK, levels:] = low
 
 
 def place_first_kernel(send_ref, arrived_ref, out_ref, matrix_ref, pair_ref):
     slots, levels = arrived_ref.shape
     split_pair(arrived_ref, pair_ref)
     size = 128
-
-    def one(index, carry):
-        base = pl.multiple_of(index * size, size)
-        column = base + lax.broadcasted_iota(jnp.int32, (size, slots), 0)
-        matrix = jnp.where(column == send_ref[...], 1.0, 0.0).astype(bf16)
-        matrix_ref[pl.ds(base, size), :] = matrix
-        both = mm(matrix, pair_ref[...])
-        out_ref[pl.ds(base, size), :] = both[:, :levels] + both[:, levels:]
-        return carry
-
-    lax.fori_loop(0, out_ref.shape[0] // size, one, 0)
+    shape = (size, CHUNK)
+    column = lax.broadcasted_iota(jnp.int32, shape, 0).astype(f32).astype(bf16)
+    one, zero = jnp.ones(shape, bf16), jnp.zeros(shape, bf16)
+    for base in range(0, out_ref.shape[0], size):
+        near = (send_ref[...] - base).astype(f32).astype(bf16)
+        for at in range(0, slots, CHUNK):
+            hit = jnp.broadcast_to(near[:, at : at + CHUNK], shape) == column
+            matrix_ref[base : base + size, at : at + CHUNK] = jnp.where(hit, one, zero)
+    both = mm(matrix_ref[...], pair_ref[...])
+    out_ref[...] = both[:, :levels] + both[:, levels:]
 
 
 def place_kernel(matrix_ref, arrived_ref, out_ref, pair_ref):
@@ -303,7 +285,7 @@
             return after, outward
 
         here = field[k]
-        lax.fori_loop(k, wide - k, row, (here, east[k - 1] * (here - field[k - 1])), unroll=2)
+        lax.fori_loop(k, wide - k, row, (here, east[k - 1] * (here - field[k - 1])), unroll=4)
 
     def middle():
         return field[HALO : HALO + across, HALO : HALO + along]
@@ -324,28 +306,59 @@
     columns = across * along
     pair = jnp.concatenate(halves(full.reshape(columns, levels)), axis=1)
 
-    size = 4 * CHUNK
-
-    def gather(index, carry):
-        base = pl.multiple_of(index * size, size)
-        both = mm(select_ref[pl.ds(base, size), :], pair)
-        out_ref[pl.ds(base, size), :] = both[:, :levels] + both[:, levels:]
-        return carry
-
-    lax.fori_loop(0, out_ref.shape[0] // size, gather, 0)
+    size = out_ref.shape[0] // 2
+    for base in range(0, out_ref.shape[0], size):
+        both = mm(select_ref[base : base + size, :], pair)
+        out_ref[base : base + size, :] = both[:, :levels] + both[:, levels:]
+
+
+def exact_sum(x, y):
+    total = x + y
+    part = total - x
+    return total, (x - (total - part)) + (y - part)
+
+
+def exact_product(x, y):
+    def cut(value):
+        scaled = 4097.0 * value
+        high = scaled - (scaled - value)
+        return high, value - high
+
+    product = x * y
+    (xh, xl), (yh, yl) = cut(x), cut(y)
+    return product, ((xh * yh - product) + xh * yl + xl * yh) + xl * yl
+
+
+def fraction(top, bottom):
+    high = top[0] / bottom[0]
+    product, rest = exact_product(high, bottom[0])
+    return high, (((top[0] - product) - rest) + (top[1] - high * bottom[1])) / bottom[0]
+
+
+def minus_product(x, y, z):
+    product, rest = exact_product(y[0], z[0])
+    return (x[0] - product) + ((x[1] - rest) - (y[0] * z[1] + y[1] * z[0]))
 
 
 def finish_kernel(sums_ref, b_ref, sb_ref, p_ref, sp_ref, control_ref, increment_ref):
-    total = jnp.sum(sums_ref[...], axis=0, keepdims=True)
+    total = sums_ref[...]
+    error = jnp.zeros_like(total)
+    while total.shape[0] > 1:
+        half = total.shape[0] // 2
+        total, more = exact_sum(total[:half], total[half:])
+        error = (error[:half] + error[half:]) + more
     lane = lax.broadcasted_iota(jnp.int32, total.shape, 1)
-    a, c, e, f = [jnp.sum(jnp.where(lane == k, total, 0.0), axis=1, keepdims=True) for k in range(4)]
-    slope = c / a
-    first = 1.0 / (1.0 + slope)
-    rest = e / a - slope * slope
-    ratio = first * first * rest
-    curved = rest + (f / a - 2.0 * slope * (e / a) + slope * slope * slope)
-    second = ratio / (first * first * curved - ratio * ratio * (1.0 + slope))
-    of_b = first + second * (ratio + first * slope)
+
+    def pick(values, k):
+        return jnp.sum(jnp.where(lane == k, values, 0.0), axis=1, keepdims=True)
+
+    a, c, e, f = [(pick(total, k), pick(error, k)) for k in range(4)]
+    slope, square, cube = fraction(c, a), fraction(e, a), fraction(f, a)
+    first = 1.0 / (1.0 + slope[0])
+    rest = minus_product(square, slope, slope)
+    curved = rest + (minus_product(cube, slope, square) - slope[0] * rest)
+    second = jnp.clip(rest / (curved - first * rest * rest), 0.0, 1.0)
+    of_b = first + second * (first * first * rest + first * slope[0])
     of_p = -second * first
     control_ref[...] = of_b * b_ref[...] + of_p * p_ref[...]
     increment_ref[...] = of_b * sb_ref[...] + of_p * sp_ref[...]

time: 182 us -> 179 us (0.984)
  Pallas kernels: 33.2 us -> 30.4 us
where the time goes in v5:
time: 179 us
  blocking collectives  109 us (61%)
  Pallas kernels  30.4 us (17%)
  waiting for transfers between devices  22.3 us (12%)
  starting transfers between devices  15.4 us (9%)
    all_to_all x5, blocking collectives, exchange(): lax.all_to_all(rows, ('gx', 'gy'), split_axis=0, concat_axis=0, tiled=True)  109 us
    ppermute x12, waiting for transfers between devices, swap(): return lax.ppermute(cells, axis, pairs + [(j, i) for i, j in pairs])  22.3 us
    ppermute x12, starting transfers between devices, swap(): return lax.ppermute(cells, axis, pairs + [(j, i) for i, j in pairs])  15.4 us
    pallas_call x1, Pallas kernels, on_device(): pl.pallas_call(observe_adjoint_kernel, out_shape=slot_rows, in_specs=[sca...  8.05 us
    pallas_call x1, Pallas kernels, on_device(): pl.pallas_call(spread_first_kernel, out_shape=(jax.ShapeDtypeStruct((slot...  7.64 us
    pallas_call x2, Pallas kernels, smooth_twice(): pl.pallas_call(functools.partial(smooth_kernel, sizes), out_shape=(tile,...  6.08 us
    pallas_call x1, Pallas kernels, on_device(): pl.pallas_call(observe_norm_kernel, out_shape=jax.ShapeDtypeStruct((owner...  3.8 us
  transfers between devices with their start and end apart: 12, of which 5 were waited for; matrix products, arithmetic and copies ran while one was open for 0% of the time, Pallas kernels for 5%

profile of v5, /device:TPU:1, one launch (start us, length us, event | category | flops | bytes accessed | tf_op | source)
XLA Modules:
  0.0 179.1 jit_solution(16021654886089447196)
XLA Ops:
  0.6 6.9 %collective-permute-start.1 = (f32[8,64,128]{2,1,0:T(8,128)}, f32[8,64,128]{2,1,0:T(8,128)S(1)}, u32[]{:S(2)}, u32[]{:S(2)}) collective-permute-start(f32[8,64,128]{2,1,0:T(8,128)} %cells_ref.3), channel_id=1, source_target_pairs={{8,16},{24,32},{40,48},{56,64},{72,80},{88,96},{104,112},{120,0},{... | collective-permute-start | bytes 786440 | tf_op jit(solution)/shard_map/ppermute | solution.py:370
  7.5 0.0 collective-permute-start
  8.1 7.6 %spread_first.1 = (bf16[2048,4096]{1,0:T(8,128)(2,1)S(1)}, f32[2048,128]{1,0:T(8,128)S(1)}, s32[1,2048]{1,0:T(1,128)S(1)}) custom-call(s32[1]{0:T(128)S(6)} %copy.11.count_ref, s32[4,2048]{1,0:T(4,128)} %rows_hbm, f32[4,2048]{1,0:T(4,128)} %weights_hbm.1, s32[1,16,128]{2,1,0:T(8,128)} %bitcast.51, f32[1,2048]{1,0:T(1,128)} %bitcast.52, f32[1,2048]{1,0:T(1,128)} %bitcast.46, ...), custom_call_target="tpu_custom_call" | custom-call | flops 8589934592 | bytes 16777216 | tf_op jit(solution)/shard_map/spread_first/pallas_call | solution.py:432
  15.8 0.0 copy-start.1
  15.8 0.0 collective-permute-done.1.two_ref
  15.8 0.0 collective-permute-done.one_ref
  15.8 26.4 %all_to_all.25 = f32[128,16,128]{2,1,0:T(8,128)S(1)} all-to-all(f32[128,16,128]{2,1,0:T(8,128)S(1)} %bitcast.35), channel_id=1, replica_groups=mesh['gx'=16,'gy'=8] {'gx','gy'}, dimensions={0} | all-to-all | bytes 2097152 | tf_op jit(solution)/shard_map/all_to_all | solution.py:374
  42.2 0.8 place_first.1
  43.1 1.3 collective-permute-start.3
  44.4 0.0 collective-permute-start.2
  44.4 0.0 copy-done.1
  44.4 1.4 collective-permute-start.6
  45.8 0.0 collective-permute-start.7
  45.8 7.3 %collective-permute-done.3.two_ref = f32[8,64,128]{2,1,0:T(8,128)S(1)} collective-permute-done((f32[8,64,128]{2,1,0:T(8,128)S(1)}, f32[8,64,128]{2,1,0:T(8,128)S(1)}, u32[]{:S(2)}, u32[]{:S(2)}) %collective-permute-start.3) | collective-permute-done | bytes 262176 | tf_op jit(solution)/shard_map/ppermute | solution.py:370
  53.0 0.0 collective-permute-done.2.one_ref
  53.1 2.3 %collective-permute-start.4 = (f32[24,8,128]{2,1,0:T(8,128)S(1)}, f32[24,8,128]{2,1,0:T(8,128)S(1)}, u32[]{:S(2)}, u32[]{:S(2)}) collective-permute-start(f32[24,8,128]{2,1,0:T(8,128)S(1)} %get-tuple-element.45), channel_id=1, source_target_pairs={{0,1},{2,3},{4,5},{6,7},{1,0},{3,2},{5,4},{7,6},{8,9},{10,11},{12,... | collective-permute-start | bytes 294920 | tf_op jit(solution)/shard_map/ppermute | solution.py:370
  55.3 0.1 collective-permute-start.5
  55.4 1.7 select.1.select_ref
  57.1 0.0 collective-permute-done.6.first_ref
  57.1 0.0 collective-permute-done.7.second_ref
  57.1 0.4 conduct.1
  57.5 0.0 collective-permute-done.4.first_ref
  57.5 2.1 %collective-permute-done.5.second_ref = f32[24,8,128]{2,1,0:T(8,128)S(1)} collective-permute-done((f32[24,8,128]{2,1,0:T(8,128)S(1)}, f32[24,8,128]{2,1,0:T(8,128)S(1)}, u32[]{:S(2)}, u32[]{:S(2)}) %collective-permute-start.5) | collective-permute-done | bytes 98336 | tf_op jit(solution)/shard_map/ppermute | solution.py:370
  59.7 3.0 %smooth.2 = (f32[8,64,128]{2,1,0:T(8,128)S(1)}, f32[8,64,128]{2,1,0:T(8,128)S(1)}, f32[2048,128]{1,0:T(8,128)S(1)}, f32[1,8,128]{2,1,0:T(8,128)S(1)}) custom-call(s32[1]{0:T(128)} %bitcast.place_ref, bf16[2048,512]{1,0:T(8,128)(2,1)S(1)} %select.1.select_ref, f32[8,64,128]{2,1,0:T(8,128)S(1)} %bitcast.40, f32[8,64,128]{2,1,0:T(8,128)S(1)} %collective-permute-done.2.one_ref, ...), custom_call_target="tpu_custom_call" | custom-call | tf_op jit(solution)/shard_map/smooth/pallas_call | solution.py:487
  62.7 0.0 copy-start
  62.7 0.0 copy-start.2
  62.7 23.0 %all_to_all.26 = f32[128,16,128]{2,1,0:T(8,128)S(1)} all-to-all(f32[128,16,128]{2,1,0:T(8,128)S(1)} %bitcast.36), channel_id=1, replica_groups=mesh['gx'=16,'gy'=8] {'gx','gy'}, dimensions={0} | all-to-all | bytes 2097152 | tf_op jit(solution)/shard_map/all_to_all | solution.py:374
  85.7 0.0 copy-done
  85.7 0.0 copy-done.2
  85.7 8.1 %observe_adjoint.1 = f32[2048,128]{1,0:T(8,128)S(1)} custom-call(s32[1]{0:T(128)S(6)} %copy.11.count_ref, f32[2048,128]{1,0:T(8,128)S(1)} %bitcast.27, f32[1,2048]{1,0:T(1,128)S(1)} %bitcast.47, f32[2048,128]{1,0:T(8,128)S(1)} %copy-done, bf16[2048,4096]{1,0:T(8,128)(2,1)S(1)} %get-tuple-element.54.matrix_ref), custom_call_target="tpu_custom_call" | custom-call | tf_op jit(solution)/shard_map/observe_adjoint/pallas_call | solution.py:499
  93.8 23.3 %all_to_all.27 = f32[128,16,128]{2,1,0:T(8,128)S(1)} all-to-all(f32[128,16,128]{2,1,0:T(8,128)S(1)} %bitcast.28), channel_id=1, replica_groups=mesh['gx'=16,'gy'=8] {'gx','gy'}, dimensions={0} | all-to-all | bytes 2097152 | tf_op jit(solution)/shard_map/all_to_all | solution.py:374
  117.1 0.8 place.1
  117.9 1.3 collective-permute-start.9
  119.2 0.0 collective-permute-start.8
  119.2 8.7 %collective-permute-done.9.two_ref = f32[8,64,128]{2,1,0:T(8,128)S(1)} collective-permute-done((f32[8,64,128]{2,1,0:T(8,128)S(1)}, f32[8,64,128]{2,1,0:T(8,128)S(1)}, u32[]{:S(2)}, u32[]{:S(2)}) %collective-permute-start.9) | collective-permute-done | bytes 262176 | tf_op jit(solution)/shard_map/ppermute | solution.py:370
  127.8 0.0 collective-permute-done.8.one_ref
  127.9 2.3 %collective-permute-start.10 = (f32[24,8,128]{2,1,0:T(8,128)S(1)}, f32[24,8,128]{2,1,0:T(8,128)S(1)}, u32[]{:S(2)}, u32[]{:S(2)}) collective-permute-start(f32[24,8,128]{2,1,0:T(8,128)S(1)} %get-tuple-element.55), channel_id=1, source_target_pairs={{0,1},{2,3},{4,5},{6,7},{1,0},{3,2},{5,4},{7,6},{8,9},{10,11},{12,... | collective-permute-start | bytes 294920 | tf_op jit(solution)/shard_map/ppermute | solution.py:370
  130.1 0.1 collective-permute-start.11
  130.2 0.9 collective-permute-done.10.first_ref
  131.1 3.4 %collective-permute-done.11.second_ref = f32[24,8,128]{2,1,0:T(8,128)S(1)} collective-permute-done((f32[24,8,128]{2,1,0:T(8,128)S(1)}, f32[24,8,128]{2,1,0:T(8,128)S(1)}, u32[]{:S(2)}, u32[]{:S(2)}) %collective-permute-start.11) | collective-permute-done | bytes 98336 | tf_op jit(solution)/shard_map/ppermute | solution.py:370
  134.5 3.0 %smooth.3 = (f32[8,64,128]{2,1,0:T(8,128)S(1)}, f32[8,64,128]{2,1,0:T(8,128)S(1)}, f32[2048,128]{1,0:T(8,128)S(1)}, f32[2,8,128]{2,1,0:T(8,128)S(1)}) custom-call(s32[1]{0:T(128)} %bitcast.place_ref, bf16[2048,512]{1,0:T(8,128)(2,1)S(1)} %select.1.select_ref, f32[8,64,128]{2,1,0:T(8,128)S(1)} %bitcast.32, f32[8,64,128]{2,1,0:T(8,128)S(1)} %collective-permute-done.8.one_ref, ...), custom_call_target="tpu_custom_call" | custom-call | tf_op jit(solution)/shard_map/smooth/pallas_call | solution.py:487
  137.5 22.8 %all_to_all.28 = f32[128,16,128]{2,1,0:T(8,128)S(1)} all-to-all(f32[128,16,128]{2,1,0:T(8,128)S(1)} %bitcast.34), channel_id=1, replica_groups=mesh['gx'=16,'gy'=8] {'gx','gy'}, dimensions={0} | all-to-all | bytes 2097152 | tf_op jit(solution)/shard_map/all_to_all | solution.py:374
  160.3 3.8 %observe_norm.1 = f32[128,128]{1,0:T(8,128)S(1)} custom-call(s32[1]{0:T(128)S(6)} %copy.11.count_ref, f32[2048,128]{1,0:T(8,128)S(1)} %bitcast.26, f32[1,2048]{1,0:T(1,128)S(1)} %bitcast.48, f32[2048,128]{1,0:T(8,128)S(1)} %copy-done, bf16[2048,4096]{1,0:T(8,128)(2,1)S(1)} %get-tuple-element.54.matrix_ref, f32[1,8,128]{2,1,0:T(8,128)S(1)} %get-tuple-element.59.first_ref, ...), custom_call_target="tpu_custom_call" | custom-call | tf_op jit(solution)/shard_map/observe_norm/pallas_call | solution.py:520
  164.1 14.0 %all_to_all.29 = f32[128,1,128]{2,1,0:T(1,128)S(1)} all-to-all(f32[128,1,128]{2,1,0:T(1,128)S(1)} %bitcast.41), channel_id=1, replica_groups=mesh['gx'=16,'gy'=8] {'gx','gy'}, dimensions={0} | all-to-all | bytes 131072 | tf_op jit(solution)/shard_map/all_to_all | solution.py:374
  178.1 1.0 finish.1
  (3 shorter events, 0.1 us)
Async XLA Ops:
  0.6 15.2 %collective-permute-start.1 = (f32[8,64,128]{2,1,0:T(8,128)}, f32[8,64,128]{2,1,0:T(8,128)S(1)}, u32[]{:S(2)}, u32[]{:S(2)}) collective-permute-start(f32[8,64,128]{2,1,0:T(8,128)} %cells_ref.3), channel_id=1, source_target_pairs={{8,16},{24,32},{40,48},{56,64},{72,80},{88,96},{104,112},{120,0},{... | collective-permute-start | bytes 786440 | tf_op jit(solution)/shard_map/ppermute | solution.py:370
  7.5 8.3 %collective-permute-start = (f32[8,64,128]{2,1,0:T(8,128)}, f32[8,64,128]{2,1,0:T(8,128)S(1)}, u32[]{:S(2)}, u32[]{:S(2)}) collective-permute-start(f32[8,64,128]{2,1,0:T(8,128)} %cells_ref.3), channel_id=1, source_target_pairs={{0,8},{16,24},{32,40},{48,56},{64,72},{80,88},{96,104},{112,120},{... | collective-permute-start | bytes 786440 | tf_op jit(solution)/shard_map/ppermute | solution.py:370
  15.8 28.6 %copy-start.1 = (f32[8,64,128]{2,1,0:T(8,128)S(1)}, f32[8,64,128]{2,1,0:T(8,128)}, u32[]{:S(2)}) copy-start(f32[8,64,128]{2,1,0:T(8,128)} %cells_ref.3) | copy-start | bytes 786436
  43.1 9.9 %collective-permute-start.3 = (f32[8,64,128]{2,1,0:T(8,128)S(1)}, f32[8,64,128]{2,1,0:T(8,128)S(1)}, u32[]{:S(2)}, u32[]{:S(2)}) collective-permute-start(f32[8,64,128]{2,1,0:T(8,128)S(1)} %bitcast.37), channel_id=1, source_target_pairs={{8,16},{24,32},{40,48},{56,64},{72,80},{88,96},{104,112},{120,0},{... | collective-permute-start | bytes 786440 | tf_op jit(solution)/shard_map/ppermute | solution.py:370
  44.4 8.7 %collective-permute-start.2 = (f32[8,64,128]{2,1,0:T(8,128)S(1)}, f32[8,64,128]{2,1,0:T(8,128)S(1)}, u32[]{:S(2)}, u32[]{:S(2)}) collective-permute-start(f32[8,64,128]{2,1,0:T(8,128)S(1)} %bitcast.38), channel_id=1, source_target_pairs={{0,8},{16,24},{32,40},{48,56},{64,72},{80,88},{96,104},{112,120},{... | collective-permute-start | bytes 786440 | tf_op jit(solution)/shard_map/ppermute | solution.py:370
  44.4 12.7 %collective-permute-start.6 = (f32[24,8,128]{2,1,0:T(8,128)S(1)}, f32[24,8,128]{2,1,0:T(8,128)S(1)}, u32[]{:S(2)}, u32[]{:S(2)}) collective-permute-start(f32[24,8,128]{2,1,0:T(8,128)S(1)} %get-tuple-element.49), channel_id=1, source_target_pairs={{0,1},{2,3},{4,5},{6,7},{1,0},{3,2},{5,4},{7,6},{8,9},{10,11},{12,... | collective-permute-start | bytes 294920 | tf_op jit(solution)/shard_map/ppermute | solution.py:370
  45.8 11.3 %collective-permute-start.7 = (f32[24,8,128]{2,1,0:T(8,128)S(1)}, f32[24,8,128]{2,1,0:T(8,128)S(1)}, u32[]{:S(2)}, u32[]{:S(2)}) collective-permute-start(f32[24,8,128]{2,1,0:T(8,128)S(1)} %get-tuple-element.50), channel_id=1, source_target_pairs={{1,2},{3,4},{5,6},{7,0},{2,1},{4,3},{6,5},{0,7},{9,10},{11,12},{13... | collective-permute-start | bytes 294920 | tf_op jit(solution)/shard_map/ppermute | solution.py:370
  53.1 4.5 %collective-permute-start.4 = (f32[24,8,128]{2,1,0:T(8,128)S(1)}, f32[24,8,128]{2,1,0:T(8,128)S(1)}, u32[]{:S(2)}, u32[]{:S(2)}) collective-permute-start(f32[24,8,128]{2,1,0:T(8,128)S(1)} %get-tuple-element.45), channel_id=1, source_target_pairs={{0,1},{2,3},{4,5},{6,7},{1,0},{3,2},{5,4},{7,6},{8,9},{10,11},{12,... | collective-permute-start | bytes 294920 | tf_op jit(solution)/shard_map/ppermute | solution.py:370
  55.3 4.3 %collective-permute-start.5 = (f32[24,8,128]{2,1,0:T(8,128)S(1)}, f32[24,8,128]{2,1,0:T(8,128)S(1)}, u32[]{:S(2)}, u32[]{:S(2)}) collective-permute-start(f32[24,8,128]{2,1,0:T(8,128)S(1)} %get-tuple-element.46), channel_id=1, source_target_pairs={{1,2},{3,4},{5,6},{7,0},{2,1},{4,3},{6,5},{0,7},{9,10},{11,12},{13... | collective-permute-start | bytes 294920 | tf_op jit(solution)/shard_map/ppermute | solution.py:370
  62.7 23.0 %copy-start = (f32[2048,128]{1,0:T(8,128)S(1)}, f32[2048,128]{1,0:T(8,128)}, u32[]{:S(2)}) copy-start(f32[2048,128]{1,0:T(8,128)} %profile_ref.3) | copy-start | bytes 3145732
  62.7 23.0 %copy-start.2 = (f32[2048]{0:T(1024)S(1)}, f32[2048]{0:T(1024)}, u32[]{:S(2)}) copy-start(f32[2048]{0:T(1024)} %param.10) | copy-start | bytes 24580
  117.9 9.9 %collective-permute-start.9 = (f32[8,64,128]{2,1,0:T(8,128)S(1)}, f32[8,64,128]{2,1,0:T(8,128)S(1)}, u32[]{:S(2)}, u32[]{:S(2)}) collective-permute-start(f32[8,64,128]{2,1,0:T(8,128)S(1)} %bitcast.29), channel_id=1, source_target_pairs={{8,16},{24,32},{40,48},{56,64},{72,80},{88,96},{104,112},{120,0},{... | collective-permute-start | bytes 786440 | tf_op jit(solution)/shard_map/ppermute | solution.py:370
  119.2 8.7 %collective-permute-start.8 = (f32[8,64,128]{2,1,0:T(8,128)S(1)}, f32[8,64,128]{2,1,0:T(8,128)S(1)}, u32[]{:S(2)}, u32[]{:S(2)}) collective-permute-start(f32[8,64,128]{2,1,0:T(8,128)S(1)} %bitcast.30), channel_id=1, source_target_pairs={{0,8},{16,24},{32,40},{48,56},{64,72},{80,88},{96,104},{112,120},{... | collective-permute-start | bytes 786440 | tf_op jit(solution)/shard_map/ppermute | solution.py:370
  127.9 3.2 %collective-permute-start.10 = (f32[24,8,128]{2,1,0:T(8,128)S(1)}, f32[24,8,128]{2,1,0:T(8,128)S(1)}, u32[]{:S(2)}, u32[]{:S(2)}) collective-permute-start(f32[24,8,128]{2,1,0:T(8,128)S(1)} %get-tuple-element.55), channel_id=1, source_target_pairs={{0,1},{2,3},{4,5},{6,7},{1,0},{3,2},{5,4},{7,6},{8,9},{10,11},{12,... | collective-permute-start | bytes 294920 | tf_op jit(solution)/shard_map/ppermute | solution.py:370
  130.1 4.3 %collective-permute-start.11 = (f32[24,8,128]{2,1,0:T(8,128)S(1)}, f32[24,8,128]{2,1,0:T(8,128)S(1)}, u32[]{:S(2)}, u32[]{:S(2)}) collective-permute-start(f32[24,8,128]{2,1,0:T(8,128)S(1)} %get-tuple-element.56), channel_id=1, source_target_pairs={{1,2},{3,4},{5,6},{7,0},{2,1},{4,3},{6,5},{0,7},{9,10},{11,12},{13... | collective-permute-start | bytes 294920 | tf_op jit(solution)/shard_map/ppermute | solution.py:370

commit v6 on v5

--- a/solution.py
+++ b/solution.py
@@ -150,7 +150,18 @@
     count_ref, received_ref, precision_ref, profile_ref, matrix_ref, first_ref, second_ref,
     out_ref, turned_ref, seen_ref,
 ):
-    observe(received_ref, matrix_ref, profile_ref, turned_ref, seen_ref)
+    slots, levels = received_ref.shape
+    obs = profile_ref.shape[0]
+    for at in range(0, slots, levels):
+        turned_ref[:, at : at + levels] = received_ref[at : at + levels, :].T.astype(bf16)
+    size = obs // 2
+    for base in range(0, obs, size):
+        gathered = mm(turned_ref[...], matrix_ref[:, base : base + size]) + mm(
+            turned_ref[...], matrix_ref[:, obs + base : obs + base + size]
+        )
+        seen_ref[:, base : base + size] = jnp.sum(
+            profile_ref[base : base + size, :].T * gathered, axis=0, keepdims=True
+        )
     seen = seen_ref[...]
     lane = lax.broadcasted_iota(jnp.int32, out_ref.shape, 1)
     parts = (first_ref[0], second_ref[0], second_ref[1], live_precision(count_ref, precision_ref) * seen * seen)
@@ -522,7 +533,7 @@
         out_shape=jax.ShapeDtypeStruct((owners, levels), f32),
         in_specs=[scalar] + [whole] * 6,
         out_specs=whole,
-        scratch_shapes=[turned_scratch, seen_scratch],
+        scratch_shapes=[pltpu.VMEM((levels, slots), bf16), seen_scratch],
         compiler_params=params(14),
         name="observe_norm",
     )(obs_count, trade(outgoing), precision, profile_weight, matrix, first_sums, second_sums)

time: 179 us -> 178 us (level)
  transfers between devices with their start and end apart: 12 -> 12, of which waited for: 5 -> 5; matrix products, arithmetic and copies ran while one was open for 0% -> 0% of each run, Pallas kernels for 5% -> 6%
where the time goes in v6:
time: 178 us
  blocking collectives  109 us (61%)
  Pallas kernels  29.3 us (16%)
  waiting for transfers between devices  22.3 us (13%)
  starting transfers between devices  15.4 us (9%)
    all_to_all x5, blocking collectives, exchange(): lax.all_to_all(rows, ('gx', 'gy'), split_axis=0, concat_axis=0, tiled=True)  109 us
    ppermute x12, waiting for transfers between devices, swap(): return lax.ppermute(cells, axis, pairs + [(j, i) for i, j in pairs])  22.3 us
    ppermute x12, starting transfers between devices, swap(): return lax.ppermute(cells, axis, pairs + [(j, i) for i, j in pairs])  15.4 us
    pallas_call x1, Pallas kernels, on_device(): pl.pallas_call(observe_adjoint_kernel, out_shape=slot_rows, in_specs=[sca...  8.05 us
    pallas_call x1, Pallas kernels, on_device(): pl.pallas_call(spread_first_kernel, out_shape=(jax.ShapeDtypeStruct((slot...  7.64 us
    pallas_call x2, Pallas kernels, smooth_twice(): pl.pallas_call(functools.partial(smooth_kernel, sizes), out_shape=(tile,...  6.08 us
  transfers between devices with their start and end apart: 12, of which 5 were waited for; matrix products, arithmetic and copies ran while one was open for 0% of the time, Pallas kernels for 6%

profile of v6, /device:TPU:1, one launch (start us, length us, event | category | flops | bytes accessed | tf_op | source)
XLA Modules:
  0.0 178.0 jit_solution(17725090729658389120)
XLA Ops:
  0.6 6.9 %collective-permute-start.1 = (f32[8,64,128]{2,1,0:T(8,128)}, f32[8,64,128]{2,1,0:T(8,128)S(1)}, u32[]{:S(2)}, u32[]{:S(2)}) collective-permute-start(f32[8,64,128]{2,1,0:T(8,128)} %cells_ref.3), channel_id=1, source_target_pairs={{8,16},{24,32},{40,48},{56,64},{72,80},{88,96},{104,112},{120,0},{... | collective-permute-start | bytes 786440 | tf_op jit(solution)/shard_map/ppermute | solution.py:381
  7.5 0.0 collective-permute-start
  8.1 7.6 %spread_first.1 = (bf16[2048,4096]{1,0:T(8,128)(2,1)S(1)}, f32[2048,128]{1,0:T(8,128)S(1)}, s32[1,2048]{1,0:T(1,128)S(1)}) custom-call(s32[1]{0:T(128)S(6)} %copy.11.count_ref, s32[4,2048]{1,0:T(4,128)} %rows_hbm, f32[4,2048]{1,0:T(4,128)} %weights_hbm.1, s32[1,16,128]{2,1,0:T(8,128)} %bitcast.51, f32[1,2048]{1,0:T(1,128)} %bitcast.52, f32[1,2048]{1,0:T(1,128)} %bitcast.46, ...), custom_call_target="tpu_custom_call" | custom-call | flops 8589934592 | bytes 16777216 | tf_op jit(solution)/shard_map/spread_first/pallas_call | solution.py:443
  15.8 0.0 copy-start.1
  15.8 0.0 collective-permute-done.1.two_ref
  15.8 0.0 collective-permute-done.one_ref
  15.8 26.4 %all_to_all.25 = f32[128,16,128]{2,1,0:T(8,128)S(1)} all-to-all(f32[128,16,128]{2,1,0:T(8,128)S(1)} %bitcast.35), channel_id=1, replica_groups=mesh['gx'=16,'gy'=8] {'gx','gy'}, dimensions={0} | all-to-all | bytes 2097152 | tf_op jit(solution)/shard_map/all_to_all | solution.py:385
  42.2 0.8 place_first.1
  43.1 1.3 collective-permute-start.3
  44.4 0.0 collective-permute-start.2
  44.4 0.0 copy-done.1
  44.4 1.4 collective-permute-start.6
  45.8 0.0 collective-permute-start.7
  45.8 7.3 %collective-permute-done.3.two_ref = f32[8,64,128]{2,1,0:T(8,128)S(1)} collective-permute-done((f32[8,64,128]{2,1,0:T(8,128)S(1)}, f32[8,64,128]{2,1,0:T(8,128)S(1)}, u32[]{:S(2)}, u32[]{:S(2)}) %collective-permute-start.3) | collective-permute-done | bytes 262176 | tf_op jit(solution)/shard_map/ppermute | solution.py:381
  53.0 0.0 collective-permute-done.2.one_ref
  53.1 2.3 %collective-permute-start.4 = (f32[24,8,128]{2,1,0:T(8,128)S(1)}, f32[24,8,128]{2,1,0:T(8,128)S(1)}, u32[]{:S(2)}, u32[]{:S(2)}) collective-permute-start(f32[24,8,128]{2,1,0:T(8,128)S(1)} %get-tuple-element.45), channel_id=1, source_target_pairs={{0,1},{2,3},{4,5},{6,7},{1,0},{3,2},{5,4},{7,6},{8,9},{10,11},{12,... | collective-permute-start | bytes 294920 | tf_op jit(solution)/shard_map/ppermute | solution.py:381
  55.3 0.1 collective-permute-start.5
  55.4 1.7 select.1.select_ref
  57.1 0.0 collective-permute-done.6.first_ref
  57.1 0.0 collective-permute-done.7.second_ref
  57.1 0.4 conduct.1
  57.5 0.0 collective-permute-done.4.first_ref
  57.5 2.1 %collective-permute-done.5.second_ref = f32[24,8,128]{2,1,0:T(8,128)S(1)} collective-permute-done((f32[24,8,128]{2,1,0:T(8,128)S(1)}, f32[24,8,128]{2,1,0:T(8,128)S(1)}, u32[]{:S(2)}, u32[]{:S(2)}) %collective-permute-start.5) | collective-permute-done | bytes 98336 | tf_op jit(solution)/shard_map/ppermute | solution.py:381
  59.7 3.0 %smooth.2 = (f32[8,64,128]{2,1,0:T(8,128)S(1)}, f32[8,64,128]{2,1,0:T(8,128)S(1)}, f32[2048,128]{1,0:T(8,128)S(1)}, f32[1,8,128]{2,1,0:T(8,128)S(1)}) custom-call(s32[1]{0:T(128)} %bitcast.place_ref, bf16[2048,512]{1,0:T(8,128)(2,1)S(1)} %select.1.select_ref, f32[8,64,128]{2,1,0:T(8,128)S(1)} %bitcast.40, f32[8,64,128]{2,1,0:T(8,128)S(1)} %collective-permute-done.2.one_ref, ...), custom_call_target="tpu_custom_call" | custom-call | tf_op jit(solution)/shard_map/smooth/pallas_call | solution.py:498
  62.7 0.0 copy-start
  62.7 0.0 copy-start.2
  62.7 23.0 %all_to_all.26 = f32[128,16,128]{2,1,0:T(8,128)S(1)} all-to-all(f32[128,16,128]{2,1,0:T(8,128)S(1)} %bitcast.36), channel_id=1, replica_groups=mesh['gx'=16,'gy'=8] {'gx','gy'}, dimensions={0} | all-to-all | bytes 2097152 | tf_op jit(solution)/shard_map/all_to_all | solution.py:385
  85.7 0.0 copy-done
  85.7 0.0 copy-done.2
  85.7 8.1 %observe_adjoint.1 = f32[2048,128]{1,0:T(8,128)S(1)} custom-call(s32[1]{0:T(128)S(6)} %copy.11.count_ref, f32[2048,128]{1,0:T(8,128)S(1)} %bitcast.27, f32[1,2048]{1,0:T(1,128)S(1)} %bitcast.47, f32[2048,128]{1,0:T(8,128)S(1)} %copy-done, bf16[2048,4096]{1,0:T(8,128)(2,1)S(1)} %get-tuple-element.54.matrix_ref), custom_call_target="tpu_custom_call" | custom-call | tf_op jit(solution)/shard_map/observe_adjoint/pallas_call | solution.py:510
  93.8 23.3 %all_to_all.27 = f32[128,16,128]{2,1,0:T(8,128)S(1)} all-to-all(f32[128,16,128]{2,1,0:T(8,128)S(1)} %bitcast.28), channel_id=1, replica_groups=mesh['gx'=16,'gy'=8] {'gx','gy'}, dimensions={0} | all-to-all | bytes 2097152 | tf_op jit(solution)/shard_map/all_to_all | solution.py:385
  117.1 0.8 place.1
  117.9 1.3 collective-permute-start.9
  119.2 0.0 collective-permute-start.8
  119.2 8.7 %collective-permute-done.9.two_ref = f32[8,64,128]{2,1,0:T(8,128)S(1)} collective-permute-done((f32[8,64,128]{2,1,0:T(8,128)S(1)}, f32[8,64,128]{2,1,0:T(8,128)S(1)}, u32[]{:S(2)}, u32[]{:S(2)}) %collective-permute-start.9) | collective-permute-done | bytes 262176 | tf_op jit(solution)/shard_map/ppermute | solution.py:381
  127.8 0.0 collective-permute-done.8.one_ref
  127.9 2.3 %collective-permute-start.10 = (f32[24,8,128]{2,1,0:T(8,128)S(1)}, f32[24,8,128]{2,1,0:T(8,128)S(1)}, u32[]{:S(2)}, u32[]{:S(2)}) collective-permute-start(f32[24,8,128]{2,1,0:T(8,128)S(1)} %get-tuple-element.55), channel_id=1, source_target_pairs={{0,1},{2,3},{4,5},{6,7},{1,0},{3,2},{5,4},{7,6},{8,9},{10,11},{12,... | collective-permute-start | bytes 294920 | tf_op jit(solution)/shard_map/ppermute | solution.py:381
  130.1 0.1 collective-permute-start.11
  130.2 0.9 collective-permute-done.10.first_ref
  131.1 3.4 %collective-permute-done.11.second_ref = f32[24,8,128]{2,1,0:T(8,128)S(1)} collective-permute-done((f32[24,8,128]{2,1,0:T(8,128)S(1)}, f32[24,8,128]{2,1,0:T(8,128)S(1)}, u32[]{:S(2)}, u32[]{:S(2)}) %collective-permute-start.11) | collective-permute-done | bytes 98336 | tf_op jit(solution)/shard_map/ppermute | solution.py:381
  134.5 3.0 %smooth.3 = (f32[8,64,128]{2,1,0:T(8,128)S(1)}, f32[8,64,128]{2,1,0:T(8,128)S(1)}, f32[2048,128]{1,0:T(8,128)S(1)}, f32[2,8,128]{2,1,0:T(8,128)S(1)}) custom-call(s32[1]{0:T(128)} %bitcast.place_ref, bf16[2048,512]{1,0:T(8,128)(2,1)S(1)} %select.1.select_ref, f32[8,64,128]{2,1,0:T(8,128)S(1)} %bitcast.32, f32[8,64,128]{2,1,0:T(8,128)S(1)} %collective-permute-done.8.one_ref, ...), custom_call_target="tpu_custom_call" | custom-call | tf_op jit(solution)/shard_map/smooth/pallas_call | solution.py:498
  137.5 22.8 %all_to_all.28 = f32[128,16,128]{2,1,0:T(8,128)S(1)} all-to-all(f32[128,16,128]{2,1,0:T(8,128)S(1)} %bitcast.34), channel_id=1, replica_groups=mesh['gx'=16,'gy'=8] {'gx','gy'}, dimensions={0} | all-to-all | bytes 2097152 | tf_op jit(solution)/shard_map/all_to_all | solution.py:385
  160.3 2.7 %observe_norm.1 = f32[128,128]{1,0:T(8,128)S(1)} custom-call(s32[1]{0:T(128)S(6)} %copy.11.count_ref, f32[2048,128]{1,0:T(8,128)S(1)} %bitcast.26, f32[1,2048]{1,0:T(1,128)S(1)} %bitcast.48, f32[2048,128]{1,0:T(8,128)S(1)} %copy-done, bf16[2048,4096]{1,0:T(8,128)(2,1)S(1)} %get-tuple-element.54.matrix_ref, f32[1,8,128]{2,1,0:T(8,128)S(1)} %get-tuple-element.59.first_ref, ...), custom_call_target="tpu_custom_call" | custom-call | tf_op jit(solution)/shard_map/observe_norm/pallas_call | solution.py:531
  163.0 14.0 %all_to_all.29 = f32[128,1,128]{2,1,0:T(1,128)S(1)} all-to-all(f32[128,1,128]{2,1,0:T(1,128)S(1)} %bitcast.41), channel_id=1, replica_groups=mesh['gx'=16,'gy'=8] {'gx','gy'}, dimensions={0} | all-to-all | bytes 131072 | tf_op jit(solution)/shard_map/all_to_all | solution.py:385
  177.0 1.0 finish.1
  (3 shorter events, 0.1 us)
Async XLA Ops:
  0.6 15.2 %collective-permute-start.1 = (f32[8,64,128]{2,1,0:T(8,128)}, f32[8,64,128]{2,1,0:T(8,128)S(1)}, u32[]{:S(2)}, u32[]{:S(2)}) collective-permute-start(f32[8,64,128]{2,1,0:T(8,128)} %cells_ref.3), channel_id=1, source_target_pairs={{8,16},{24,32},{40,48},{56,64},{72,80},{88,96},{104,112},{120,0},{... | collective-permute-start | bytes 786440 | tf_op jit(solution)/shard_map/ppermute | solution.py:381
  7.5 8.3 %collective-permute-start = (f32[8,64,128]{2,1,0:T(8,128)}, f32[8,64,128]{2,1,0:T(8,128)S(1)}, u32[]{:S(2)}, u32[]{:S(2)}) collective-permute-start(f32[8,64,128]{2,1,0:T(8,128)} %cells_ref.3), channel_id=1, source_target_pairs={{0,8},{16,24},{32,40},{48,56},{64,72},{80,88},{96,104},{112,120},{... | collective-permute-start | bytes 786440 | tf_op jit(solution)/shard_map/ppermute | solution.py:381
  15.8 28.6 %copy-start.1 = (f32[8,64,128]{2,1,0:T(8,128)S(1)}, f32[8,64,128]{2,1,0:T(8,128)}, u32[]{:S(2)}) copy-start(f32[8,64,128]{2,1,0:T(8,128)} %cells_ref.3) | copy-start | bytes 786436
  43.1 9.9 %collective-permute-start.3 = (f32[8,64,128]{2,1,0:T(8,128)S(1)}, f32[8,64,128]{2,1,0:T(8,128)S(1)}, u32[]{:S(2)}, u32[]{:S(2)}) collective-permute-start(f32[8,64,128]{2,1,0:T(8,128)S(1)} %bitcast.37), channel_id=1, source_target_pairs={{8,16},{24,32},{40,48},{56,64},{72,80},{88,96},{104,112},{120,0},{... | collective-permute-start | bytes 786440 | tf_op jit(solution)/shard_map/ppermute | solution.py:381
  44.4 8.7 %collective-permute-start.2 = (f32[8,64,128]{2,1,0:T(8,128)S(1)}, f32[8,64,128]{2,1,0:T(8,128)S(1)}, u32[]{:S(2)}, u32[]{:S(2)}) collective-permute-start(f32[8,64,128]{2,1,0:T(8,128)S(1)} %bitcast.38), channel_id=1, source_target_pairs={{0,8},{16,24},{32,40},{48,56},{64,72},{80,88},{96,104},{112,120},{... | collective-permute-start | bytes 786440 | tf_op jit(solution)/shard_map/ppermute | solution.py:381
  44.4 12.7 %collective-permute-start.6 = (f32[24,8,128]{2,1,0:T(8,128)S(1)}, f32[24,8,128]{2,1,0:T(8,128)S(1)}, u32[]{:S(2)}, u32[]{:S(2)}) collective-permute-start(f32[24,8,128]{2,1,0:T(8,128)S(1)} %get-tuple-element.49), channel_id=1, source_target_pairs={{0,1},{2,3},{4,5},{6,7},{1,0},{3,2},{5,4},{7,6},{8,9},{10,11},{12,... | collective-permute-start | bytes 294920 | tf_op jit(solution)/shard_map/ppermute | solution.py:381
  45.8 11.3 %collective-permute-start.7 = (f32[24,8,128]{2,1,0:T(8,128)S(1)}, f32[24,8,128]{2,1,0:T(8,128)S(1)}, u32[]{:S(2)}, u32[]{:S(2)}) collective-permute-start(f32[24,8,128]{2,1,0:T(8,128)S(1)} %get-tuple-element.50), channel_id=1, source_target_pairs={{1,2},{3,4},{5,6},{7,0},{2,1},{4,3},{6,5},{0,7},{9,10},{11,12},{13... | collective-permute-start | bytes 294920 | tf_op jit(solution)/shard_map/ppermute | solution.py:381
  53.1 4.5 %collective-permute-start.4 = (f32[24,8,128]{2,1,0:T(8,128)S(1)}, f32[24,8,128]{2,1,0:T(8,128)S(1)}, u32[]{:S(2)}, u32[]{:S(2)}) collective-permute-start(f32[24,8,128]{2,1,0:T(8,128)S(1)} %get-tuple-element.45), channel_id=1, source_target_pairs={{0,1},{2,3},{4,5},{6,7},{1,0},{3,2},{5,4},{7,6},{8,9},{10,11},{12,... | collective-permute-start | bytes 294920 | tf_op jit(solution)/shard_map/ppermute | solution.py:381
  55.3 4.3 %collective-permute-start.5 = (f32[24,8,128]{2,1,0:T(8,128)S(1)}, f32[24,8,128]{2,1,0:T(8,128)S(1)}, u32[]{:S(2)}, u32[]{:S(2)}) collective-permute-start(f32[24,8,128]{2,1,0:T(8,128)S(1)} %get-tuple-element.46), channel_id=1, source_target_pairs={{1,2},{3,4},{5,6},{7,0},{2,1},{4,3},{6,5},{0,7},{9,10},{11,12},{13... | collective-permute-start | bytes 294920 | tf_op jit(solution)/shard_map/ppermute | solution.py:381
  62.7 23.0 %copy-start = (f32[2048,128]{1,0:T(8,128)S(1)}, f32[2048,128]{1,0:T(8,128)}, u32[]{:S(2)}) copy-start(f32[2048,128]{1,0:T(8,128)} %profile_ref.3) | copy-start | bytes 3145732
  62.7 23.0 %copy-start.2 = (f32[2048]{0:T(1024)S(1)}, f32[2048]{0:T(1024)}, u32[]{:S(2)}) copy-start(f32[2048]{0:T(1024)} %param.10) | copy-start | bytes 24580
  117.9 9.9 %collective-permute-start.9 = (f32[8,64,128]{2,1,0:T(8,128)S(1)}, f32[8,64,128]{2,1,0:T(8,128)S(1)}, u32[]{:S(2)}, u32[]{:S(2)}) collective-permute-start(f32[8,64,128]{2,1,0:T(8,128)S(1)} %bitcast.29), channel_id=1, source_target_pairs={{8,16},{24,32},{40,48},{56,64},{72,80},{88,96},{104,112},{120,0},{... | collective-permute-start | bytes 786440 | tf_op jit(solution)/shard_map/ppermute | solution.py:381
  119.2 8.7 %collective-permute-start.8 = (f32[8,64,128]{2,1,0:T(8,128)S(1)}, f32[8,64,128]{2,1,0:T(8,128)S(1)}, u32[]{:S(2)}, u32[]{:S(2)}) collective-permute-start(f32[8,64,128]{2,1,0:T(8,128)S(1)} %bitcast.30), channel_id=1, source_target_pairs={{0,8},{16,24},{32,40},{48,56},{64,72},{80,88},{96,104},{112,120},{... | collective-permute-start | bytes 786440 | tf_op jit(solution)/shard_map/ppermute | solution.py:381
  127.9 3.2 %collective-permute-start.10 = (f32[24,8,128]{2,1,0:T(8,128)S(1)}, f32[24,8,128]{2,1,0:T(8,128)S(1)}, u32[]{:S(2)}, u32[]{:S(2)}) collective-permute-start(f32[24,8,128]{2,1,0:T(8,128)S(1)} %get-tuple-element.55), channel_id=1, source_target_pairs={{0,1},{2,3},{4,5},{6,7},{1,0},{3,2},{5,4},{7,6},{8,9},{10,11},{12,... | collective-permute-start | bytes 294920 | tf_op jit(solution)/shard_map/ppermute | solution.py:381
  130.1 4.3 %collective-permute-start.11 = (f32[24,8,128]{2,1,0:T(8,128)S(1)}, f32[24,8,128]{2,1,0:T(8,128)S(1)}, u32[]{:S(2)}, u32[]{:S(2)}) collective-permute-start(f32[24,8,128]{2,1,0:T(8,128)S(1)} %get-tuple-element.56), channel_id=1, source_target_pairs={{1,2},{3,4},{5,6},{7,0},{2,1},{4,3},{6,5},{0,7},{9,10},{11,12},{13... | collective-permute-start | bytes 294920 | tf_op jit(solution)/shard_map/ppermute | solution.py:381

commit v7 on v6

--- a/solution.py
+++ b/solution.py
@@ -121,7 +121,7 @@
             pair_ref[base : base + levels, levels:] = low
 
 
-def observe(received_ref, matrix_ref, profile_ref, turned_ref, seen_ref):
+def observe(received_ref, matrix_ref, profile_ref, upright_ref, turned_ref, seen_ref):
     slots, levels = received_ref.shape
     obs = profile_ref.shape[0]
     for at in range(0, slots, levels):
@@ -133,25 +133,25 @@
         both = mm(turned_ref[...], matrix_ref[:, base : base + size])
         gathered = both[:levels] + both[levels:]
         gathered = gathered + mm(turned_ref[:levels], matrix_ref[:, obs + base : obs + base + size])
-        seen_ref[:, base : base + size] = jnp.sum(
-            profile_ref[base : base + size, :].T * gathered, axis=0, keepdims=True
-        )
+        upright = profile_ref[base : base + size, :].T
+        upright_ref[:, base : base + size] = upright
+        seen_ref[:, base : base + size] = jnp.sum(upright * gathered, axis=0, keepdims=True)
 
 
 def observe_adjoint_kernel(
-    count_ref, received_ref, precision_ref, profile_ref, matrix_ref, out_ref, turned_ref, seen_ref, pair_ref,
+    count_ref, received_ref, precision_ref, profile_ref, matrix_ref, out_ref, upright_ref, turned_ref, seen_ref, pair_ref,
 ):
-    observe(received_ref, matrix_ref, profile_ref, turned_ref, seen_ref)
+    observe(received_ref, matrix_ref, profile_ref, upright_ref, turned_ref, seen_ref)
     fill_pair(profile_ref, live_precision(count_ref, precision_ref) * seen_ref[...], pair_ref)
     spread_rows(matrix_ref, pair_ref, out_ref)
 
 
 def observe_norm_kernel(
-    count_ref, received_ref, precision_ref, profile_ref, matrix_ref, first_ref, second_ref,
+    count_ref, received_ref, precision_ref, upright_ref, matrix_ref, first_ref, second_ref,
     out_ref, turned_ref, seen_ref,
 ):
     slots, levels = received_ref.shape
-    obs = profile_ref.shape[0]
+    obs = upright_ref.shape[1]
     for at in range(0, slots, levels):
         turned_ref[:, at : at + levels] = received_ref[at : at + levels, :].T.astype(bf16)
     size = obs // 2
@@ -160,7 +160,7 @@
             turned_ref[...], matrix_ref[:, obs + base : obs + base + size]
         )
         seen_ref[:, base : base + size] = jnp.sum(
-            profile_ref[base : base + size, :].T * gathered, axis=0, keepdims=True
+            upright_ref[:, base : base + size] * gathered, axis=0, keepdims=True
         )
     seen = seen_ref[...]
     lane = lax.broadcasted_iota(jnp.int32, out_ref.shape, 1)
@@ -296,7 +296,9 @@
             return after, outward
 
         here = field[k]
-        lax.fori_loop(k, wide - k, row, (here, east[k - 1] * (here - field[k - 1])), unroll=4)
+        carry = (here, east[k - 1] * (here - field[k - 1]))
+        for i in range(k, wide - k):
+            carry = row(i, carry)
 
     def middle():
         return field[HALO : HALO + across, HALO : HALO + along]
@@ -507,11 +509,11 @@
 
     b, sb, outgoing, first_sums = smooth_twice(cells, ())
 
-    spread = pl.pallas_call(
+    spread, upright = pl.pallas_call(
         observe_adjoint_kernel,
-        out_shape=slot_rows,
+        out_shape=(slot_rows, jax.ShapeDtypeStruct((levels, obs), f32)),
         in_specs=[scalar] + [whole] * 4,
-        out_specs=whole,
+        out_specs=(whole, whole),
         scratch_shapes=[turned_scratch, seen_scratch, pair_scratch],
         compiler_params=params(16),
         name="observe_adjoint",
@@ -536,7 +538,7 @@
         scratch_shapes=[pltpu.VMEM((levels, slots), bf16), seen_scratch],
         compiler_params=params(14),
         name="observe_norm",
-    )(obs_count, trade(outgoing), precision, profile_weight, matrix, first_sums, second_sums)
+    )(obs_count, trade(outgoing), precision, upright, matrix, first_sums, second_sums)
 
     sums = exchange(sums.reshape(owners, 1, levels)).reshape(owners, levels)
 

time: 178 us -> 178 us (level)
  no operation moved by 1% of the time
where the time goes in v7:
time: 178 us
  blocking collectives  109 us (61%)
  Pallas kernels  29.1 us (16%)
  waiting for transfers between devices  22.3 us (13%)
  starting transfers between devices  15.4 us (9%)
    all_to_all x5, blocking collectives, exchange(): lax.all_to_all(rows, ('gx', 'gy'), split_axis=0, concat_axis=0, tiled=True)  109 us
    ppermute x12, waiting for transfers between devices, swap(): return lax.ppermute(cells, axis, pairs + [(j, i) for i, j in pairs])  22.3 us
    ppermute x12, starting transfers between devices, swap(): return lax.ppermute(cells, axis, pairs + [(j, i) for i, j in pairs])  15.4 us
    pallas_call x1, Pallas kernels, on_device(): pl.pallas_call(observe_adjoint_kernel, out_shape=(slot_rows, jax.ShapeDty...  8.01 us
    pallas_call x1, Pallas kernels, on_device(): pl.pallas_call(spread_first_kernel, out_shape=(jax.ShapeDtypeStruct((slot...  7.64 us
    pallas_call x2, Pallas kernels, smooth_twice(): pl.pallas_call(functools.partial(smooth_kernel, sizes), out_shape=(tile,...  5.94 us
  transfers between devices with their start and end apart: 12, of which 5 were waited for; matrix products, arithmetic and copies ran while one was open for 0% of the time, Pallas kernels for 6%

profile of v7, /device:TPU:1, one launch (start us, length us, event | category | flops | bytes accessed | tf_op | source)
XLA Modules:
  0.0 177.8 jit_solution(5061667625837165080)
XLA Ops:
  0.6 6.9 %collective-permute-start.1 = (f32[8,64,128]{2,1,0:T(8,128)}, f32[8,64,128]{2,1,0:T(8,128)S(1)}, u32[]{:S(2)}, u32[]{:S(2)}) collective-permute-start(f32[8,64,128]{2,1,0:T(8,128)} %cells_ref.3), channel_id=1, source_target_pairs={{8,16},{24,32},{40,48},{56,64},{72,80},{88,96},{104,112},{120,0},{... | collective-permute-start | bytes 786440 | tf_op jit(solution)/shard_map/ppermute | solution.py:383
  7.5 0.0 collective-permute-start
  8.1 7.6 %spread_first.1 = (bf16[2048,4096]{1,0:T(8,128)(2,1)S(1)}, f32[2048,128]{1,0:T(8,128)S(1)}, s32[1,2048]{1,0:T(1,128)S(1)}) custom-call(s32[1]{0:T(128)S(6)} %copy.11.count_ref, s32[4,2048]{1,0:T(4,128)} %rows_hbm, f32[4,2048]{1,0:T(4,128)} %weights_hbm.1, s32[1,16,128]{2,1,0:T(8,128)} %bitcast.51, f32[1,2048]{1,0:T(1,128)} %bitcast.52, f32[1,2048]{1,0:T(1,128)} %bitcast.46, ...), custom_call_target="tpu_custom_call" | custom-call | flops 8589934592 | bytes 16777216 | tf_op jit(solution)/shard_map/spread_first/pallas_call | solution.py:445
  15.8 0.0 copy-start.1
  15.8 0.0 collective-permute-done.1.two_ref
  15.8 0.0 collective-permute-done.one_ref
  15.8 26.4 %all_to_all.25 = f32[128,16,128]{2,1,0:T(8,128)S(1)} all-to-all(f32[128,16,128]{2,1,0:T(8,128)S(1)} %bitcast.34), channel_id=1, replica_groups=mesh['gx'=16,'gy'=8] {'gx','gy'}, dimensions={0} | all-to-all | bytes 2097152 | tf_op jit(solution)/shard_map/all_to_all | solution.py:387
  42.2 0.8 place_first.1
  43.1 1.3 collective-permute-start.3
  44.4 0.0 collective-permute-start.2
  44.4 0.0 copy-done.1
  44.4 1.4 collective-permute-start.6
  45.8 0.0 collective-permute-start.7
  45.8 7.3 %collective-permute-done.3.two_ref = f32[8,64,128]{2,1,0:T(8,128)S(1)} collective-permute-done((f32[8,64,128]{2,1,0:T(8,128)S(1)}, f32[8,64,128]{2,1,0:T(8,128)S(1)}, u32[]{:S(2)}, u32[]{:S(2)}) %collective-permute-start.3) | collective-permute-done | bytes 262176 | tf_op jit(solution)/shard_map/ppermute | solution.py:383
  53.0 0.0 collective-permute-done.2.one_ref
  53.1 2.3 %collective-permute-start.4 = (f32[24,8,128]{2,1,0:T(8,128)S(1)}, f32[24,8,128]{2,1,0:T(8,128)S(1)}, u32[]{:S(2)}, u32[]{:S(2)}) collective-permute-start(f32[24,8,128]{2,1,0:T(8,128)S(1)} %get-tuple-element.47), channel_id=1, source_target_pairs={{0,1},{2,3},{4,5},{6,7},{1,0},{3,2},{5,4},{7,6},{8,9},{10,11},{12,... | collective-permute-start | bytes 294920 | tf_op jit(solution)/shard_map/ppermute | solution.py:383
  55.3 0.1 collective-permute-start.5
  55.4 1.7 select.1.select_ref
  57.1 0.0 collective-permute-done.6.first_ref
  57.1 0.0 collective-permute-done.7.second_ref
  57.1 0.4 conduct.1
  57.5 0.0 collective-permute-done.4.first_ref
  57.5 2.1 %collective-permute-done.5.second_ref = f32[24,8,128]{2,1,0:T(8,128)S(1)} collective-permute-done((f32[24,8,128]{2,1,0:T(8,128)S(1)}, f32[24,8,128]{2,1,0:T(8,128)S(1)}, u32[]{:S(2)}, u32[]{:S(2)}) %collective-permute-start.5) | collective-permute-done | bytes 98336 | tf_op jit(solution)/shard_map/ppermute | solution.py:383
  59.7 2.9 %smooth.2 = (f32[8,64,128]{2,1,0:T(8,128)S(1)}, f32[8,64,128]{2,1,0:T(8,128)S(1)}, f32[2048,128]{1,0:T(8,128)S(1)}, f32[1,8,128]{2,1,0:T(8,128)S(1)}) custom-call(s32[1]{0:T(128)} %bitcast.place_ref, bf16[2048,512]{1,0:T(8,128)(2,1)S(1)} %select.1.select_ref, f32[8,64,128]{2,1,0:T(8,128)S(1)} %bitcast.40, f32[8,64,128]{2,1,0:T(8,128)S(1)} %collective-permute-done.2.one_ref, ...), custom_call_target="tpu_custom_call" | custom-call | tf_op jit(solution)/shard_map/smooth/pallas_call | solution.py:500
  62.6 0.0 copy-start
  62.6 0.0 copy-start.2
  62.6 23.0 %all_to_all.26 = f32[128,16,128]{2,1,0:T(8,128)S(1)} all-to-all(f32[128,16,128]{2,1,0:T(8,128)S(1)} %bitcast.35), channel_id=1, replica_groups=mesh['gx'=16,'gy'=8] {'gx','gy'}, dimensions={0} | all-to-all | bytes 2097152 | tf_op jit(solution)/shard_map/all_to_all | solution.py:387
  85.6 0.0 copy-done
  85.6 0.0 copy-done.2
  85.6 8.0 %observe_adjoint.1 = (f32[2048,128]{1,0:T(8,128)S(1)}, f32[128,2048]{1,0:T(8,128)S(1)}) custom-call(s32[1]{0:T(128)S(6)} %copy.11.count_ref, f32[2048,128]{1,0:T(8,128)S(1)} %bitcast.24, f32[1,2048]{1,0:T(1,128)S(1)} %bitcast.47, f32[2048,128]{1,0:T(8,128)S(1)} %copy-done, bf16[2048,4096]{1,0:T(8,128)(2,1)S(1)} %get-tuple-element.56.matrix_ref), custom_call_target="tpu_custom_call" | custom-call | tf_op jit(solution)/shard_map/observe_adjoint/pallas_call | solution.py:512
  93.6 23.3 %all_to_all.27 = f32[128,16,128]{2,1,0:T(8,128)S(1)} all-to-all(f32[128,16,128]{2,1,0:T(8,128)S(1)} %bitcast.36), channel_id=1, replica_groups=mesh['gx'=16,'gy'=8] {'gx','gy'}, dimensions={0} | all-to-all | bytes 2097152 | tf_op jit(solution)/shard_map/all_to_all | solution.py:387
  116.9 0.8 place.1
  117.7 1.3 collective-permute-start.9
  119.0 0.0 collective-permute-start.8
  119.0 8.7 %collective-permute-done.9.two_ref = f32[8,64,128]{2,1,0:T(8,128)S(1)} collective-permute-done((f32[8,64,128]{2,1,0:T(8,128)S(1)}, f32[8,64,128]{2,1,0:T(8,128)S(1)}, u32[]{:S(2)}, u32[]{:S(2)}) %collective-permute-start.9) | collective-permute-done | bytes 262176 | tf_op jit(solution)/shard_map/ppermute | solution.py:383
  127.7 0.0 collective-permute-done.8.one_ref
  127.7 2.3 %collective-permute-start.10 = (f32[24,8,128]{2,1,0:T(8,128)S(1)}, f32[24,8,128]{2,1,0:T(8,128)S(1)}, u32[]{:S(2)}, u32[]{:S(2)}) collective-permute-start(f32[24,8,128]{2,1,0:T(8,128)S(1)} %get-tuple-element.58), channel_id=1, source_target_pairs={{0,1},{2,3},{4,5},{6,7},{1,0},{3,2},{5,4},{7,6},{8,9},{10,11},{12,... | collective-permute-start | bytes 294920 | tf_op jit(solution)/shard_map/ppermute | solution.py:383
  130.0 0.1 collective-permute-start.11
  130.0 0.9 collective-permute-done.10.first_ref
  130.9 3.4 %collective-permute-done.11.second_ref = f32[24,8,128]{2,1,0:T(8,128)S(1)} collective-permute-done((f32[24,8,128]{2,1,0:T(8,128)S(1)}, f32[24,8,128]{2,1,0:T(8,128)S(1)}, u32[]{:S(2)}, u32[]{:S(2)}) %collective-permute-start.11) | collective-permute-done | bytes 98336 | tf_op jit(solution)/shard_map/ppermute | solution.py:383
  134.3 3.0 %smooth.3 = (f32[8,64,128]{2,1,0:T(8,128)S(1)}, f32[8,64,128]{2,1,0:T(8,128)S(1)}, f32[2048,128]{1,0:T(8,128)S(1)}, f32[2,8,128]{2,1,0:T(8,128)S(1)}) custom-call(s32[1]{0:T(128)} %bitcast.place_ref, bf16[2048,512]{1,0:T(8,128)(2,1)S(1)} %select.1.select_ref, f32[8,64,128]{2,1,0:T(8,128)S(1)} %bitcast.31, f32[8,64,128]{2,1,0:T(8,128)S(1)} %collective-permute-done.8.one_ref, ...), custom_call_target="tpu_custom_call" | custom-call | tf_op jit(solution)/shard_map/smooth/pallas_call | solution.py:500
  137.3 22.8 %all_to_all.28 = f32[128,16,128]{2,1,0:T(8,128)S(1)} all-to-all(f32[128,16,128]{2,1,0:T(8,128)S(1)} %bitcast.33), channel_id=1, replica_groups=mesh['gx'=16,'gy'=8] {'gx','gy'}, dimensions={0} | all-to-all | bytes 2097152 | tf_op jit(solution)/shard_map/all_to_all | solution.py:387
  160.2 2.7 %observe_norm.1 = f32[128,128]{1,0:T(8,128)S(1)} custom-call(s32[1]{0:T(128)S(6)} %copy.11.count_ref, f32[2048,128]{1,0:T(8,128)S(1)} %bitcast.27, f32[1,2048]{1,0:T(1,128)S(1)} %bitcast.48, f32[128,2048]{1,0:T(8,128)S(1)} %get-tuple-element.62.upright_ref, bf16[2048,4096]{1,0:T(8,128)(2,1)S(1)} %get-tuple-element.56.matrix_ref, ...), custom_call_target="tpu_custom_call" | custom-call | tf_op jit(solution)/shard_map/observe_norm/pallas_call | solution.py:533
  162.8 14.0 %all_to_all.29 = f32[128,1,128]{2,1,0:T(1,128)S(1)} all-to-all(f32[128,1,128]{2,1,0:T(1,128)S(1)} %bitcast.41), channel_id=1, replica_groups=mesh['gx'=16,'gy'=8] {'gx','gy'}, dimensions={0} | all-to-all | bytes 131072 | tf_op jit(solution)/shard_map/all_to_all | solution.py:387
  176.8 1.0 finish.1
  (3 shorter events, 0.1 us)
Async XLA Ops:
  0.6 15.2 %collective-permute-start.1 = (f32[8,64,128]{2,1,0:T(8,128)}, f32[8,64,128]{2,1,0:T(8,128)S(1)}, u32[]{:S(2)}, u32[]{:S(2)}) collective-permute-start(f32[8,64,128]{2,1,0:T(8,128)} %cells_ref.3), channel_id=1, source_target_pairs={{8,16},{24,32},{40,48},{56,64},{72,80},{88,96},{104,112},{120,0},{... | collective-permute-start | bytes 786440 | tf_op jit(solution)/shard_map/ppermute | solution.py:383
  7.5 8.3 %collective-permute-start = (f32[8,64,128]{2,1,0:T(8,128)}, f32[8,64,128]{2,1,0:T(8,128)S(1)}, u32[]{:S(2)}, u32[]{:S(2)}) collective-permute-start(f32[8,64,128]{2,1,0:T(8,128)} %cells_ref.3), channel_id=1, source_target_pairs={{0,8},{16,24},{32,40},{48,56},{64,72},{80,88},{96,104},{112,120},{... | collective-permute-start | bytes 786440 | tf_op jit(solution)/shard_map/ppermute | solution.py:383
  15.8 28.6 %copy-start.1 = (f32[8,64,128]{2,1,0:T(8,128)S(1)}, f32[8,64,128]{2,1,0:T(8,128)}, u32[]{:S(2)}) copy-start(f32[8,64,128]{2,1,0:T(8,128)} %cells_ref.3) | copy-start | bytes 786436
  43.1 9.9 %collective-permute-start.3 = (f32[8,64,128]{2,1,0:T(8,128)S(1)}, f32[8,64,128]{2,1,0:T(8,128)S(1)}, u32[]{:S(2)}, u32[]{:S(2)}) collective-permute-start(f32[8,64,128]{2,1,0:T(8,128)S(1)} %bitcast.37), channel_id=1, source_target_pairs={{8,16},{24,32},{40,48},{56,64},{72,80},{88,96},{104,112},{120,0},{... | collective-permute-start | bytes 786440 | tf_op jit(solution)/shard_map/ppermute | solution.py:383
  44.4 8.7 %collective-permute-start.2 = (f32[8,64,128]{2,1,0:T(8,128)S(1)}, f32[8,64,128]{2,1,0:T(8,128)S(1)}, u32[]{:S(2)}, u32[]{:S(2)}) collective-permute-start(f32[8,64,128]{2,1,0:T(8,128)S(1)} %bitcast.38), channel_id=1, source_target_pairs={{0,8},{16,24},{32,40},{48,56},{64,72},{80,88},{96,104},{112,120},{... | collective-permute-start | bytes 786440 | tf_op jit(solution)/shard_map/ppermute | solution.py:383
  44.4 12.7 %collective-permute-start.6 = (f32[24,8,128]{2,1,0:T(8,128)S(1)}, f32[24,8,128]{2,1,0:T(8,128)S(1)}, u32[]{:S(2)}, u32[]{:S(2)}) collective-permute-start(f32[24,8,128]{2,1,0:T(8,128)S(1)} %get-tuple-element.51), channel_id=1, source_target_pairs={{0,1},{2,3},{4,5},{6,7},{1,0},{3,2},{5,4},{7,6},{8,9},{10,11},{12,... | collective-permute-start | bytes 294920 | tf_op jit(solution)/shard_map/ppermute | solution.py:383
  45.8 11.3 %collective-permute-start.7 = (f32[24,8,128]{2,1,0:T(8,128)S(1)}, f32[24,8,128]{2,1,0:T(8,128)S(1)}, u32[]{:S(2)}, u32[]{:S(2)}) collective-permute-start(f32[24,8,128]{2,1,0:T(8,128)S(1)} %get-tuple-element.52), channel_id=1, source_target_pairs={{1,2},{3,4},{5,6},{7,0},{2,1},{4,3},{6,5},{0,7},{9,10},{11,12},{13... | collective-permute-start | bytes 294920 | tf_op jit(solution)/shard_map/ppermute | solution.py:383
  53.1 4.5 %collective-permute-start.4 = (f32[24,8,128]{2,1,0:T(8,128)S(1)}, f32[24,8,128]{2,1,0:T(8,128)S(1)}, u32[]{:S(2)}, u32[]{:S(2)}) collective-permute-start(f32[24,8,128]{2,1,0:T(8,128)S(1)} %get-tuple-element.47), channel_id=1, source_target_pairs={{0,1},{2,3},{4,5},{6,7},{1,0},{3,2},{5,4},{7,6},{8,9},{10,11},{12,... | collective-permute-start | bytes 294920 | tf_op jit(solution)/shard_map/ppermute | solution.py:383
  55.3 4.3 %collective-permute-start.5 = (f32[24,8,128]{2,1,0:T(8,128)S(1)}, f32[24,8,128]{2,1,0:T(8,128)S(1)}, u32[]{:S(2)}, u32[]{:S(2)}) collective-permute-start(f32[24,8,128]{2,1,0:T(8,128)S(1)} %get-tuple-element.48), channel_id=1, source_target_pairs={{1,2},{3,4},{5,6},{7,0},{2,1},{4,3},{6,5},{0,7},{9,10},{11,12},{13... | collective-permute-start | bytes 294920 | tf_op jit(solution)/shard_map/ppermute | solution.py:383
  62.6 23.0 %copy-start = (f32[2048,128]{1,0:T(8,128)S(1)}, f32[2048,128]{1,0:T(8,128)}, u32[]{:S(2)}) copy-start(f32[2048,128]{1,0:T(8,128)} %profile_ref.1) | copy-start | bytes 3145732
  62.6 23.0 %copy-start.2 = (f32[2048]{0:T(1024)S(1)}, f32[2048]{0:T(1024)}, u32[]{:S(2)}) copy-start(f32[2048]{0:T(1024)} %param.10) | copy-start | bytes 24580
  117.7 9.9 %collective-permute-start.9 = (f32[8,64,128]{2,1,0:T(8,128)S(1)}, f32[8,64,128]{2,1,0:T(8,128)S(1)}, u32[]{:S(2)}, u32[]{:S(2)}) collective-permute-start(f32[8,64,128]{2,1,0:T(8,128)S(1)} %bitcast.28), channel_id=1, source_target_pairs={{8,16},{24,32},{40,48},{56,64},{72,80},{88,96},{104,112},{120,0},{... | collective-permute-start | bytes 786440 | tf_op jit(solution)/shard_map/ppermute | solution.py:383
  119.0 8.7 %collective-permute-start.8 = (f32[8,64,128]{2,1,0:T(8,128)S(1)}, f32[8,64,128]{2,1,0:T(8,128)S(1)}, u32[]{:S(2)}, u32[]{:S(2)}) collective-permute-start(f32[8,64,128]{2,1,0:T(8,128)S(1)} %bitcast.29), channel_id=1, source_target_pairs={{0,8},{16,24},{32,40},{48,56},{64,72},{80,88},{96,104},{112,120},{... | collective-permute-start | bytes 786440 | tf_op jit(solution)/shard_map/ppermute | solution.py:383
  127.7 3.2 %collective-permute-start.10 = (f32[24,8,128]{2,1,0:T(8,128)S(1)}, f32[24,8,128]{2,1,0:T(8,128)S(1)}, u32[]{:S(2)}, u32[]{:S(2)}) collective-permute-start(f32[24,8,128]{2,1,0:T(8,128)S(1)} %get-tuple-element.58), channel_id=1, source_target_pairs={{0,1},{2,3},{4,5},{6,7},{1,0},{3,2},{5,4},{7,6},{8,9},{10,11},{12,... | collective-permute-start | bytes 294920 | tf_op jit(solution)/shard_map/ppermute | solution.py:383
  130.0 4.3 %collective-permute-start.11 = (f32[24,8,128]{2,1,0:T(8,128)S(1)}, f32[24,8,128]{2,1,0:T(8,128)S(1)}, u32[]{:S(2)}, u32[]{:S(2)}) collective-permute-start(f32[24,8,128]{2,1,0:T(8,128)S(1)} %get-tuple-element.59), channel_id=1, source_target_pairs={{1,2},{3,4},{5,6},{7,0},{2,1},{4,3},{6,5},{0,7},{9,10},{11,12},{13... | collective-permute-start | bytes 294920 | tf_op jit(solution)/shard_map/ppermute | solution.py:383

commit v8 on v7

--- a/solution.py
+++ b/solution.py
@@ -317,12 +317,12 @@
     full = middle()
     full_ref[...] = full
     columns = across * along
-    pair = jnp.concatenate(halves(full.reshape(columns, levels)), axis=1)
-
     size = out_ref.shape[0] // 2
+    high, low = halves(full.reshape(columns, levels))
+    pair = high if given else jnp.concatenate((high, low), axis=1)
     for base in range(0, out_ref.shape[0], size):
         both = mm(select_ref[base : base + size, :], pair)
-        out_ref[base : base + size, :] = both[:, :levels] + both[:, levels:]
+        out_ref[base : base + size, :] = both if given else both[:, :levels] + both[:, levels:]
 
 
 def exact_sum(x, y):

time: 178 us -> 178 us (level)
  no operation moved by 1% of the time
where the time goes in v8:
time: 178 us
  blocking collectives  109 us (61%)
  Pallas kernels  29.1 us (16%)
  waiting for transfers between devices  22.3 us (13%)
  starting transfers between devices  15.4 us (9%)
    all_to_all x5, blocking collectives, exchange(): lax.all_to_all(rows, ('gx', 'gy'), split_axis=0, concat_axis=0, tiled=True)  109 us
    ppermute x12, waiting for transfers between devices, swap(): return lax.ppermute(cells, axis, pairs + [(j, i) for i, j in pairs])  22.3 us
    ppermute x12, starting transfers between devices, swap(): return lax.ppermute(cells, axis, pairs + [(j, i) for i, j in pairs])  15.4 us
    pallas_call x1, Pallas kernels, on_device(): pl.pallas_call(observe_adjoint_kernel, out_shape=(slot_rows, jax.ShapeDty...  8.01 us
    pallas_call x1, Pallas kernels, on_device(): pl.pallas_call(spread_first_kernel, out_shape=(jax.ShapeDtypeStruct((slot...  7.64 us
    pallas_call x2, Pallas kernels, smooth_twice(): pl.pallas_call(functools.partial(smooth_kernel, sizes), out_shape=(tile,...  5.93 us
  transfers between devices with their start and end apart: 12, of which 5 were waited for; matrix products, arithmetic and copies ran while one was open for 0% of the time, Pallas kernels for 6%

profile of v8, /device:TPU:1, one launch (start us, length us, event | category | flops | bytes accessed | tf_op | source)
XLA Modules:
  0.0 177.8 jit_solution(9979557076356754653)
XLA Ops:
  0.6 6.9 %collective-permute-start.1 = (f32[8,64,128]{2,1,0:T(8,128)}, f32[8,64,128]{2,1,0:T(8,128)S(1)}, u32[]{:S(2)}, u32[]{:S(2)}) collective-permute-start(f32[8,64,128]{2,1,0:T(8,128)} %cells_ref.3), channel_id=1, source_target_pairs={{8,16},{24,32},{40,48},{56,64},{72,80},{88,96},{104,112},{120,0},{... | collective-permute-start | bytes 786440 | tf_op jit(solution)/shard_map/ppermute | solution.py:383
  7.5 0.0 collective-permute-start
  8.1 7.6 %spread_first.1 = (bf16[2048,4096]{1,0:T(8,128)(2,1)S(1)}, f32[2048,128]{1,0:T(8,128)S(1)}, s32[1,2048]{1,0:T(1,128)S(1)}) custom-call(s32[1]{0:T(128)S(6)} %copy.11.count_ref, s32[4,2048]{1,0:T(4,128)} %rows_hbm, f32[4,2048]{1,0:T(4,128)} %weights_hbm.1, s32[1,16,128]{2,1,0:T(8,128)} %bitcast.51, f32[1,2048]{1,0:T(1,128)} %bitcast.52, f32[1,2048]{1,0:T(1,128)} %bitcast.46, ...), custom_call_target="tpu_custom_call" | custom-call | flops 8589934592 | bytes 16777216 | tf_op jit(solution)/shard_map/spread_first/pallas_call | solution.py:445
  15.8 0.0 copy-start.1
  15.8 0.0 collective-permute-done.1.two_ref
  15.8 0.0 collective-permute-done.one_ref
  15.8 26.4 %all_to_all.25 = f32[128,16,128]{2,1,0:T(8,128)S(1)} all-to-all(f32[128,16,128]{2,1,0:T(8,128)S(1)} %bitcast.34), channel_id=1, replica_groups=mesh['gx'=16,'gy'=8] {'gx','gy'}, dimensions={0} | all-to-all | bytes 2097152 | tf_op jit(solution)/shard_map/all_to_all | solution.py:387
  42.2 0.8 place_first.1
  43.1 1.3 collective-permute-start.3
  44.4 0.0 collective-permute-start.2
  44.4 0.0 copy-done.1
  44.4 1.4 collective-permute-start.6
  45.8 0.0 collective-permute-start.7
  45.8 7.3 %collective-permute-done.3.two_ref = f32[8,64,128]{2,1,0:T(8,128)S(1)} collective-permute-done((f32[8,64,128]{2,1,0:T(8,128)S(1)}, f32[8,64,128]{2,1,0:T(8,128)S(1)}, u32[]{:S(2)}, u32[]{:S(2)}) %collective-permute-start.3) | collective-permute-done | bytes 262176 | tf_op jit(solution)/shard_map/ppermute | solution.py:383
  53.0 0.0 collective-permute-done.2.one_ref
  53.1 2.3 %collective-permute-start.4 = (f32[24,8,128]{2,1,0:T(8,128)S(1)}, f32[24,8,128]{2,1,0:T(8,128)S(1)}, u32[]{:S(2)}, u32[]{:S(2)}) collective-permute-start(f32[24,8,128]{2,1,0:T(8,128)S(1)} %get-tuple-element.47), channel_id=1, source_target_pairs={{0,1},{2,3},{4,5},{6,7},{1,0},{3,2},{5,4},{7,6},{8,9},{10,11},{12,... | collective-permute-start | bytes 294920 | tf_op jit(solution)/shard_map/ppermute | solution.py:383
  55.3 0.1 collective-permute-start.5
  55.4 1.7 select.1.select_ref
  57.1 0.0 collective-permute-done.6.first_ref
  57.1 0.0 collective-permute-done.7.second_ref
  57.1 0.4 conduct.1
  57.5 0.0 collective-permute-done.4.first_ref
  57.5 2.1 %collective-permute-done.5.second_ref = f32[24,8,128]{2,1,0:T(8,128)S(1)} collective-permute-done((f32[24,8,128]{2,1,0:T(8,128)S(1)}, f32[24,8,128]{2,1,0:T(8,128)S(1)}, u32[]{:S(2)}, u32[]{:S(2)}) %collective-permute-start.5) | collective-permute-done | bytes 98336 | tf_op jit(solution)/shard_map/ppermute | solution.py:383
  59.7 2.9 %smooth.2 = (f32[8,64,128]{2,1,0:T(8,128)S(1)}, f32[8,64,128]{2,1,0:T(8,128)S(1)}, f32[2048,128]{1,0:T(8,128)S(1)}, f32[1,8,128]{2,1,0:T(8,128)S(1)}) custom-call(s32[1]{0:T(128)} %bitcast.place_ref, bf16[2048,512]{1,0:T(8,128)(2,1)S(1)} %select.1.select_ref, f32[8,64,128]{2,1,0:T(8,128)S(1)} %bitcast.40, f32[8,64,128]{2,1,0:T(8,128)S(1)} %collective-permute-done.2.one_ref, ...), custom_call_target="tpu_custom_call" | custom-call | tf_op jit(solution)/shard_map/smooth/pallas_call | solution.py:500
  62.6 0.0 copy-start
  62.6 0.0 copy-start.2
  62.6 23.0 %all_to_all.26 = f32[128,16,128]{2,1,0:T(8,128)S(1)} all-to-all(f32[128,16,128]{2,1,0:T(8,128)S(1)} %bitcast.35), channel_id=1, replica_groups=mesh['gx'=16,'gy'=8] {'gx','gy'}, dimensions={0} | all-to-all | bytes 2097152 | tf_op jit(solution)/shard_map/all_to_all | solution.py:387
  85.6 0.0 copy-done
  85.6 0.0 copy-done.2
  85.6 8.0 %observe_adjoint.1 = (f32[2048,128]{1,0:T(8,128)S(1)}, f32[128,2048]{1,0:T(8,128)S(1)}) custom-call(s32[1]{0:T(128)S(6)} %copy.11.count_ref, f32[2048,128]{1,0:T(8,128)S(1)} %bitcast.24, f32[1,2048]{1,0:T(1,128)S(1)} %bitcast.47, f32[2048,128]{1,0:T(8,128)S(1)} %copy-done, bf16[2048,4096]{1,0:T(8,128)(2,1)S(1)} %get-tuple-element.56.matrix_ref), custom_call_target="tpu_custom_call" | custom-call | tf_op jit(solution)/shard_map/observe_adjoint/pallas_call | solution.py:512
  93.6 23.3 %all_to_all.27 = f32[128,16,128]{2,1,0:T(8,128)S(1)} all-to-all(f32[128,16,128]{2,1,0:T(8,128)S(1)} %bitcast.36), channel_id=1, replica_groups=mesh['gx'=16,'gy'=8] {'gx','gy'}, dimensions={0} | all-to-all | bytes 2097152 | tf_op jit(solution)/shard_map/all_to_all | solution.py:387
  116.9 0.8 place.1
  117.7 1.3 collective-permute-start.9
  119.0 0.0 collective-permute-start.8
  119.0 8.7 %collective-permute-done.9.two_ref = f32[8,64,128]{2,1,0:T(8,128)S(1)} collective-permute-done((f32[8,64,128]{2,1,0:T(8,128)S(1)}, f32[8,64,128]{2,1,0:T(8,128)S(1)}, u32[]{:S(2)}, u32[]{:S(2)}) %collective-permute-start.9) | collective-permute-done | bytes 262176 | tf_op jit(solution)/shard_map/ppermute | solution.py:383
  127.7 0.0 collective-permute-done.8.one_ref
  127.7 2.3 %collective-permute-start.10 = (f32[24,8,128]{2,1,0:T(8,128)S(1)}, f32[24,8,128]{2,1,0:T(8,128)S(1)}, u32[]{:S(2)}, u32[]{:S(2)}) collective-permute-start(f32[24,8,128]{2,1,0:T(8,128)S(1)} %get-tuple-element.58), channel_id=1, source_target_pairs={{0,1},{2,3},{4,5},{6,7},{1,0},{3,2},{5,4},{7,6},{8,9},{10,11},{12,... | collective-permute-start | bytes 294920 | tf_op jit(solution)/shard_map/ppermute | solution.py:383
  130.0 0.1 collective-permute-start.11
  130.0 0.9 collective-permute-done.10.first_ref
  130.9 3.4 %collective-permute-done.11.second_ref = f32[24,8,128]{2,1,0:T(8,128)S(1)} collective-permute-done((f32[24,8,128]{2,1,0:T(8,128)S(1)}, f32[24,8,128]{2,1,0:T(8,128)S(1)}, u32[]{:S(2)}, u32[]{:S(2)}) %collective-permute-start.11) | collective-permute-done | bytes 98336 | tf_op jit(solution)/shard_map/ppermute | solution.py:383
  134.3 3.0 %smooth.3 = (f32[8,64,128]{2,1,0:T(8,128)S(1)}, f32[8,64,128]{2,1,0:T(8,128)S(1)}, f32[2048,128]{1,0:T(8,128)S(1)}, f32[2,8,128]{2,1,0:T(8,128)S(1)}) custom-call(s32[1]{0:T(128)} %bitcast.place_ref, bf16[2048,512]{1,0:T(8,128)(2,1)S(1)} %select.1.select_ref, f32[8,64,128]{2,1,0:T(8,128)S(1)} %bitcast.31, f32[8,64,128]{2,1,0:T(8,128)S(1)} %collective-permute-done.8.one_ref, ...), custom_call_target="tpu_custom_call" | custom-call | tf_op jit(solution)/shard_map/smooth/pallas_call | solution.py:500
  137.3 22.8 %all_to_all.28 = f32[128,16,128]{2,1,0:T(8,128)S(1)} all-to-all(f32[128,16,128]{2,1,0:T(8,128)S(1)} %bitcast.33), channel_id=1, replica_groups=mesh['gx'=16,'gy'=8] {'gx','gy'}, dimensions={0} | all-to-all | bytes 2097152 | tf_op jit(solution)/shard_map/all_to_all | solution.py:387
  160.1 2.6 %observe_norm.1 = f32[128,128]{1,0:T(8,128)S(1)} custom-call(s32[1]{0:T(128)S(6)} %copy.11.count_ref, f32[2048,128]{1,0:T(8,128)S(1)} %bitcast.27, f32[1,2048]{1,0:T(1,128)S(1)} %bitcast.48, f32[128,2048]{1,0:T(8,128)S(1)} %get-tuple-element.62.upright_ref, bf16[2048,4096]{1,0:T(8,128)(2,1)S(1)} %get-tuple-element.56.matrix_ref, ...), custom_call_target="tpu_custom_call" | custom-call | tf_op jit(solution)/shard_map/observe_norm/pallas_call | solution.py:533
  162.8 14.0 %all_to_all.29 = f32[128,1,128]{2,1,0:T(1,128)S(1)} all-to-all(f32[128,1,128]{2,1,0:T(1,128)S(1)} %bitcast.41), channel_id=1, replica_groups=mesh['gx'=16,'gy'=8] {'gx','gy'}, dimensions={0} | all-to-all | bytes 131072 | tf_op jit(solution)/shard_map/all_to_all | solution.py:387
  176.8 1.0 finish.1
  (3 shorter events, 0.1 us)
Async XLA Ops:
  0.6 15.2 %collective-permute-start.1 = (f32[8,64,128]{2,1,0:T(8,128)}, f32[8,64,128]{2,1,0:T(8,128)S(1)}, u32[]{:S(2)}, u32[]{:S(2)}) collective-permute-start(f32[8,64,128]{2,1,0:T(8,128)} %cells_ref.3), channel_id=1, source_target_pairs={{8,16},{24,32},{40,48},{56,64},{72,80},{88,96},{104,112},{120,0},{... | collective-permute-start | bytes 786440 | tf_op jit(solution)/shard_map/ppermute | solution.py:383
  7.5 8.3 %collective-permute-start = (f32[8,64,128]{2,1,0:T(8,128)}, f32[8,64,128]{2,1,0:T(8,128)S(1)}, u32[]{:S(2)}, u32[]{:S(2)}) collective-permute-start(f32[8,64,128]{2,1,0:T(8,128)} %cells_ref.3), channel_id=1, source_target_pairs={{0,8},{16,24},{32,40},{48,56},{64,72},{80,88},{96,104},{112,120},{... | collective-permute-start | bytes 786440 | tf_op jit(solution)/shard_map/ppermute | solution.py:383
  15.8 28.6 %copy-start.1 = (f32[8,64,128]{2,1,0:T(8,128)S(1)}, f32[8,64,128]{2,1,0:T(8,128)}, u32[]{:S(2)}) copy-start(f32[8,64,128]{2,1,0:T(8,128)} %cells_ref.3) | copy-start | bytes 786436
  43.1 9.9 %collective-permute-start.3 = (f32[8,64,128]{2,1,0:T(8,128)S(1)}, f32[8,64,128]{2,1,0:T(8,128)S(1)}, u32[]{:S(2)}, u32[]{:S(2)}) collective-permute-start(f32[8,64,128]{2,1,0:T(8,128)S(1)} %bitcast.37), channel_id=1, source_target_pairs={{8,16},{24,32},{40,48},{56,64},{72,80},{88,96},{104,112},{120,0},{... | collective-permute-start | bytes 786440 | tf_op jit(solution)/shard_map/ppermute | solution.py:383
  44.4 8.7 %collective-permute-start.2 = (f32[8,64,128]{2,1,0:T(8,128)S(1)}, f32[8,64,128]{2,1,0:T(8,128)S(1)}, u32[]{:S(2)}, u32[]{:S(2)}) collective-permute-start(f32[8,64,128]{2,1,0:T(8,128)S(1)} %bitcast.38), channel_id=1, source_target_pairs={{0,8},{16,24},{32,40},{48,56},{64,72},{80,88},{96,104},{112,120},{... | collective-permute-start | bytes 786440 | tf_op jit(solution)/shard_map/ppermute | solution.py:383
  44.4 12.7 %collective-permute-start.6 = (f32[24,8,128]{2,1,0:T(8,128)S(1)}, f32[24,8,128]{2,1,0:T(8,128)S(1)}, u32[]{:S(2)}, u32[]{:S(2)}) collective-permute-start(f32[24,8,128]{2,1,0:T(8,128)S(1)} %get-tuple-element.51), channel_id=1, source_target_pairs={{0,1},{2,3},{4,5},{6,7},{1,0},{3,2},{5,4},{7,6},{8,9},{10,11},{12,... | collective-permute-start | bytes 294920 | tf_op jit(solution)/shard_map/ppermute | solution.py:383
  45.8 11.3 %collective-permute-start.7 = (f32[24,8,128]{2,1,0:T(8,128)S(1)}, f32[24,8,128]{2,1,0:T(8,128)S(1)}, u32[]{:S(2)}, u32[]{:S(2)}) collective-permute-start(f32[24,8,128]{2,1,0:T(8,128)S(1)} %get-tuple-element.52), channel_id=1, source_target_pairs={{1,2},{3,4},{5,6},{7,0},{2,1},{4,3},{6,5},{0,7},{9,10},{11,12},{13... | collective-permute-start | bytes 294920 | tf_op jit(solution)/shard_map/ppermute | solution.py:383
  53.1 4.5 %collective-permute-start.4 = (f32[24,8,128]{2,1,0:T(8,128)S(1)}, f32[24,8,128]{2,1,0:T(8,128)S(1)}, u32[]{:S(2)}, u32[]{:S(2)}) collective-permute-start(f32[24,8,128]{2,1,0:T(8,128)S(1)} %get-tuple-element.47), channel_id=1, source_target_pairs={{0,1},{2,3},{4,5},{6,7},{1,0},{3,2},{5,4},{7,6},{8,9},{10,11},{12,... | collective-permute-start | bytes 294920 | tf_op jit(solution)/shard_map/ppermute | solution.py:383
  55.3 4.3 %collective-permute-start.5 = (f32[24,8,128]{2,1,0:T(8,128)S(1)}, f32[24,8,128]{2,1,0:T(8,128)S(1)}, u32[]{:S(2)}, u32[]{:S(2)}) collective-permute-start(f32[24,8,128]{2,1,0:T(8,128)S(1)} %get-tuple-element.48), channel_id=1, source_target_pairs={{1,2},{3,4},{5,6},{7,0},{2,1},{4,3},{6,5},{0,7},{9,10},{11,12},{13... | collective-permute-start | bytes 294920 | tf_op jit(solution)/shard_map/ppermute | solution.py:383
  62.6 23.0 %copy-start = (f32[2048,128]{1,0:T(8,128)S(1)}, f32[2048,128]{1,0:T(8,128)}, u32[]{:S(2)}) copy-start(f32[2048,128]{1,0:T(8,128)} %profile_ref.1) | copy-start | bytes 3145732
  62.6 23.0 %copy-start.2 = (f32[2048]{0:T(1024)S(1)}, f32[2048]{0:T(1024)}, u32[]{:S(2)}) copy-start(f32[2048]{0:T(1024)} %param.10) | copy-start | bytes 24580
  117.7 9.9 %collective-permute-start.9 = (f32[8,64,128]{2,1,0:T(8,128)S(1)}, f32[8,64,128]{2,1,0:T(8,128)S(1)}, u32[]{:S(2)}, u32[]{:S(2)}) collective-permute-start(f32[8,64,128]{2,1,0:T(8,128)S(1)} %bitcast.28), channel_id=1, source_target_pairs={{8,16},{24,32},{40,48},{56,64},{72,80},{88,96},{104,112},{120,0},{... | collective-permute-start | bytes 786440 | tf_op jit(solution)/shard_map/ppermute | solution.py:383
  119.0 8.7 %collective-permute-start.8 = (f32[8,64,128]{2,1,0:T(8,128)S(1)}, f32[8,64,128]{2,1,0:T(8,128)S(1)}, u32[]{:S(2)}, u32[]{:S(2)}) collective-permute-start(f32[8,64,128]{2,1,0:T(8,128)S(1)} %bitcast.29), channel_id=1, source_target_pairs={{0,8},{16,24},{32,40},{48,56},{64,72},{80,88},{96,104},{112,120},{... | collective-permute-start | bytes 786440 | tf_op jit(solution)/shard_map/ppermute | solution.py:383
  127.7 3.2 %collective-permute-start.10 = (f32[24,8,128]{2,1,0:T(8,128)S(1)}, f32[24,8,128]{2,1,0:T(8,128)S(1)}, u32[]{:S(2)}, u32[]{:S(2)}) collective-permute-start(f32[24,8,128]{2,1,0:T(8,128)S(1)} %get-tuple-element.58), channel_id=1, source_target_pairs={{0,1},{2,3},{4,5},{6,7},{1,0},{3,2},{5,4},{7,6},{8,9},{10,11},{12,... | collective-permute-start | bytes 294920 | tf_op jit(solution)/shard_map/ppermute | solution.py:383
  130.0 4.3 %collective-permute-start.11 = (f32[24,8,128]{2,1,0:T(8,128)S(1)}, f32[24,8,128]{2,1,0:T(8,128)S(1)}, u32[]{:S(2)}, u32[]{:S(2)}) collective-permute-start(f32[24,8,128]{2,1,0:T(8,128)S(1)} %get-tuple-element.59), channel_id=1, source_target_pairs={{1,2},{3,4},{5,6},{7,0},{2,1},{4,3},{6,5},{0,7},{9,10},{11,12},{13... | collective-permute-start | bytes 294920 | tf_op jit(solution)/shard_map/ppermute | solution.py:383
